TPU v7x, 768 devices: a whole 4x8x12 slice. The times are simulated.
768 devices in a mesh: lon: 96 (over x, y_hi, z), lat: 8 (over y_lo, core).
Axes of the slice: x: 4, y: 8 (y_hi: 2, y_lo: 4; y = y_hi * 4 + y_lo), z: 12, core: 2. Of those that a mesh axis runs over, the one named last changes fastest.
Arguments:
- fields: bfloat16 [256, 4608, 128], P('lat', 'lon'), may hold values from -6 to 6
- ocean: int32 [256, 4608], P('lat', 'lon'), may hold values 0 or 1
- cotangent: bfloat16 [256, 4608, 128], P('lat', 'lon'), may hold values from -6 to 6
- kernel: float32 [7, 7, 128], replicated, may hold values from -0.875 to 0.875
- ln_gain: float32 [128], replicated, may hold values from 0.1 to 1.9
- w_in: bfloat16 [128, 256], replicated, may hold values from -0.5 to 0.5
- b_in: float32 [256], replicated, may hold values from -3 to 3
- w_out: bfloat16 [256, 128], replicated, may hold values from -0.375 to 0.375
Outputs:
- advanced: bfloat16 [256, 4608, 128], P('lat', 'lon')
- field_grad: bfloat16 [256, 4608, 128], P('lat', 'lon')
- kernel_grad: float32 [7, 7, 128], replicated
- w_in_grad: float32 [128, 256], replicated
- w_out_grad: float32 [256, 128], replicated
Inputs may be any that keep to these rules, and one draw needn't show every extreme that they name: 1 marks an ocean cell, 0 a land cell.
All inputs are finite; a program needn't handle non-finite values. No bound on the sum of `ocean` on one device may be relied on, other than what follows from the above.
Results may differ from a plain program's by a relative error of at most 0.0056.
Values may be sent and summed in bfloat16 or wider, within the bound.
No kernel may reach another device: no remote copies, remote signals or barrier semaphores. Data moves between devices by JAX's collectives and lax.ppermute only.
A program may use at most 32 MiB of HBM per device.

v0:
```python
import jax
import jax.numpy as jnp
from jax import lax
from jax.sharding import PartitionSpec as P


def with_halo(cells, sides, width):
    for axis, dim in sides:
        count = lax.axis_size(axis)
        head = lax.slice_in_dim(cells, 0, width, axis=dim)
        tail = lax.slice_in_dim(cells, cells.shape[dim] - width, cells.shape[dim], axis=dim)
        cells = jnp.concatenate(
            [
                lax.ppermute(tail, axis, [(i, (i + 1) % count) for i in range(count)]),
                cells,
                lax.ppermute(head, axis, [((i + 1) % count, i) for i in range(count)]),
            ],
            axis=dim,
        )
    return cells


def depthwise(padded, kernel, row_count, col_count):
    running = jnp.zeros((row_count, col_count, padded.shape[2]), jnp.float32)
    for row_off in range(7):
        for col_off in range(7):
            running = (
                running
                + padded[row_off : row_off + row_count, col_off : col_off + col_count].astype(
                    jnp.float32
                )
                * kernel[row_off, col_off]
            )
    return running


def depthwise_back(padded, kernel, row_count, col_count):
    running = jnp.zeros((row_count, col_count, padded.shape[2]), jnp.float32)
    for row_off in range(7):
        for col_off in range(7):
            running = (
                running
                + padded[
                    6 - row_off : 6 - row_off + row_count, 6 - col_off : 6 - col_off + col_count
                ].astype(jnp.float32)
                * kernel[row_off, col_off]
            )
    return running


def kernel_terms(padded, dz_cells, row_count, col_count):
    grads = dz_cells.astype(jnp.float32)
    rows_out = []
    for row_off in range(7):
        line = []
        for col_off in range(7):
            line.append(
                jnp.sum(
                    padded[row_off : row_off + row_count, col_off : col_off + col_count].astype(
                        jnp.float32
                    )
                    * grads,
                    axis=(0, 1),
                )
            )
        rows_out.append(jnp.stack(line))
    return jnp.stack(rows_out)


def pointwise(z_cells, gmask, ln_gain, w_in, b_in, w_out):
    grid_shape = z_cells.shape
    flat_cells = z_cells.reshape(-1, grid_shape[-1])
    flat_grad = gmask.reshape(-1, grid_shape[-1])
    average = jnp.mean(flat_cells, axis=-1, keepdims=True)
    centre = flat_cells - average
    inverse = lax.rsqrt(jnp.mean(centre * centre, axis=-1, keepdims=True) + 1e-06)
    unit_cells = centre * inverse
    normed = (unit_cells * ln_gain).astype(jnp.bfloat16)
    preact = jnp.dot(normed, w_in, preferred_element_type=jnp.float32) + b_in
    normal_cdf = 0.5 * (1.0 + lax.erf(preact * 0.7071067811865476))
    hidden = (preact * normal_cdf).astype(jnp.bfloat16)
    out_term = jnp.dot(hidden, w_out, preferred_element_type=jnp.float32)
    d_hidden = lax.dot_general(
        flat_grad, w_out, (((1,), (1,)), ((), ())), preferred_element_type=jnp.float32
    )
    slopes = normal_cdf + preact * jnp.exp(-0.5 * preact * preact) * 0.3989422804014327
    d_pre = (d_hidden * slopes).astype(jnp.bfloat16)
    w_out_term = lax.dot_general(
        hidden, flat_grad, (((0,), (0,)), ((), ())), preferred_element_type=jnp.float32
    )
    w_in_term = lax.dot_general(
        normed, d_pre, (((0,), (0,)), ((), ())), preferred_element_type=jnp.float32
    )
    d_norm = lax.dot_general(
        d_pre, w_in, (((1,), (1,)), ((), ())), preferred_element_type=jnp.float32
    )
    scaled = d_norm * ln_gain
    dz_flat = inverse * (
        scaled
        - jnp.mean(scaled, axis=-1, keepdims=True)
        - unit_cells * jnp.mean(scaled * unit_cells, axis=-1, keepdims=True)
    )
    return (
        out_term.reshape(grid_shape),
        dz_flat.astype(jnp.bfloat16).reshape(grid_shape),
        w_in_term,
        w_out_term,
    )


def zero_poles(padded, width):
    position = lax.axis_index("lat")
    count = lax.axis_size("lat")
    row_ids = lax.broadcasted_iota(jnp.int32, (padded.shape[0], 1, 1), 0)
    north = jnp.logical_and(position == 0, row_ids < width)
    south = jnp.logical_and(position == count - 1, row_ids >= padded.shape[0] - width)
    return jnp.where(jnp.logical_or(north, south), jnp.zeros_like(padded), padded)


def shards(fields, ocean, cotangent, kernel, ln_gain, w_in, b_in, w_out):
    row_count = fields.shape[0]
    col_count = fields.shape[1]
    ocean_b = ocean.astype(jnp.bfloat16)[..., None]
    ocean_f = ocean.astype(jnp.float32)[..., None]
    masked = fields * ocean_b
    gmask = cotangent * ocean_b
    padded = zero_poles(with_halo(masked, (("lon", 1), ("lat", 0)), 3), 3)
    z_cells = depthwise(padded, kernel, row_count, col_count)
    out_term, dz_cells, w_in_term, w_out_term = pointwise(
        z_cells, gmask, ln_gain, w_in, b_in, w_out
    )
    kernel_term = kernel_terms(padded, dz_cells, row_count, col_count)
    dz_padded = zero_poles(with_halo(dz_cells, (("lon", 1), ("lat", 0)), 3), 3)
    advanced = (ocean_f * (fields.astype(jnp.float32) + out_term)).astype(jnp.bfloat16)
    back = depthwise_back(dz_padded, kernel, row_count, col_count)
    field_grad = (ocean_f * (cotangent.astype(jnp.float32) + back)).astype(jnp.bfloat16)
    kernel_sum, w_in_sum, w_out_sum = lax.psum((kernel_term, w_in_term, w_out_term), ("lon", "lat"))
    factor = 1.0 / jnp.sqrt(
        jnp.float32(row_count * col_count * lax.axis_size("lat") * lax.axis_size("lon"))
    )
    return (advanced, field_grad, kernel_sum * factor, w_in_sum * factor, w_out_sum * factor)


def solution(mesh):
    in_specs = (
        P("lat", "lon", None),
        P("lat", "lon"),
        P("lat", "lon", None),
        P(),
        P(),
        P(),
        P(),
        P(),
    )
    out_specs = (P("lat", "lon", None), P("lat", "lon", None), P(), P(), P())
    return jax.shard_map(shards, mesh=mesh, in_specs=in_specs, out_specs=out_specs, check_vma=False)
```

profile of v0, /device:TPU:1, one launch (start us, length us, event | category | flops | bytes accessed | tf_op | source)
XLA Modules:
  0.0 665.6 jit_solution(13252657742974998973)
XLA Ops:
  7.2 0.8 fusion.108
  8.0 1.4 broadcast_multiply_fusion
  9.5 4.8 collective-permute-start
  14.3 19.7 %collective-permute-start.1 = (bf16[32,3,128]{2,1,0:T(4,128)(2,1)S(1)}, bf16[32,3,128]{2,1,0:T(4,128)(2,1)S(1)}, u32[]{:S(2)}, u32[]{:S(2)}) collective-permute-start(bf16[32,3,128]{2,1,0:T(4,128)(2,1)S(1)} %get-tuple-element.67), channel_id=1, source_target_pairs={{8,0},{16,8},{24,16},{32,24},{40,32},{48,40},{56,48},{64,56},{72,6... | collective-permute-start | bytes 73736 | tf_op jit(solution)/shard_map/ppermute | solution.py:16
  34.2 0.8 collective-permute-done.1
  35.0 3.7 collective-permute-start.2
  38.8 1.9 collective-permute-start.3
  40.7 3.4 collective-permute-done.3
  44.3 6.0 fusion.104
  50.5 0.5 multiply_reduce_fusion.1
  51.2 0.5 multiply_convert_fusion.4
  51.7 0.5 multiply_convert_fusion
  52.2 1.1 fusion.111
  53.6 0.8 fusion
  54.3 1.0 fusion.110
  55.3 2.6 fusion.103
  57.9 1.2 multiply_convert_fusion.2
  59.1 1.1 fusion.99
  60.2 2.0 fusion.100
  62.3 2.0 fusion.101
  64.4 1.9 collective-permute-start.4
  66.3 12.2 %collective-permute-start.5 = (bf16[32,3,128]{2,1,0:T(4,128)(2,1)S(1)}, bf16[32,3,128]{2,1,0:T(4,128)(2,1)S(1)}, u32[]{:S(2)}, u32[]{:S(2)}) collective-permute-start(bf16[32,3,128]{2,1,0:T(4,128)(2,1)S(1)} %get-tuple-element.65), channel_id=1, source_target_pairs={{8,0},{16,8},{24,16},{32,24},{40,32},{48,40},{56,48},{64,56},{72,6... | collective-permute-start | bytes 73736 | tf_op jit(solution)/shard_map/ppermute | solution.py:16
  78.6 1.0 multiply_convert_fusion.3
  79.9 105.2 %psum.21 = f32[7,7,128]{2,1,0:T(8,128)S(1)} all-reduce(f32[7,7,128]{2,1,0:T(8,128)S(1)} %constant_dynamic-update-slice_fusion), channel_id=1, replica_groups=mesh['lon'=96,'lat'=8] {'lon','lat'}, use_global_device_ids=true, to_apply=%region_53.54 | all-reduce | flops 6272 | bytes 50176 | tf_op jit(solution)/shard_map/psum | solution.py:137
  185.1 1.9 collective-permute-start.6
  187.0 2.6 collective-permute-start.7
  189.6 0.6 broadcast_multiply_fusion.4
  190.3 2.5 collective-permute-done.7
  193.1 6.7 multiply_convert_fusion.1
  199.8 455.8 %all-reduce.3.cloned.1.call-done = (f32[128,256]{1,0:T(8,128)}, f32[256,128]{1,0:T(8,128)}) async-done(((f32[128,256]{1,0:T(8,128)}, f32[256,128]{1,0:T(8,128)}), (f32[128,256]{1,0:T(8,128)}, f32[256,128]{1,0:T(8,128)})) %all-reduce.3.cloned.1.call-update) | async-done | bytes 262160 | tf_op jit(solution)/shard_map/psum | solution.py:137
  655.6 1.6 broadcast_multiply_fusion.3
  657.1 1.6 broadcast_multiply_fusion.2
  (95 shorter events, 1.6 us)
Async XLA Ops:
  7.2 44.5 %copy-start = (bf16[128,256]{1,0:T(8,128)(2,1)S(1)}, bf16[128,256]{1,0:T(8,128)(2,1)}, u32[]{:S(2)}) copy-start(bf16[128,256]{1,0:T(8,128)(2,1)} %param.13) | copy-start | bytes 196612
  7.2 26.8 %copy-start.4 = (f32[7,7,128]{2,1,0:T(8,128)S(1)}, f32[7,7,128]{2,1,0:T(8,128)}, u32[]{:S(2)}) copy-start(f32[7,7,128]{2,1,0:T(8,128)} %param.11) | copy-start | bytes 75268
  7.2 648.4 %all-reduce.3.cloned.1.call-start = ((), (), s32[]{:S(2)}) async-start(), calls=%async_computation | async-start | bytes 524288 | tf_op jit(solution)/shard_map/psum | solution.py:137
  9.5 24.7 %collective-permute-start = (bf16[32,3,128]{2,1,0:T(4,128)(2,1)S(1)}, bf16[32,3,128]{2,1,0:T(4,128)(2,1)S(1)}, u32[]{:S(2)}, u32[]{:S(2)}) collective-permute-start(bf16[32,3,128]{2,1,0:T(4,128)(2,1)S(1)} %get-tuple-element.66), channel_id=1, source_target_pairs={{0,8},{8,16},{16,24},{24,32},{32,40},{40,48},{48,56},{56,64},{64,7... | collective-permute-start | bytes 73736 | tf_op jit(solution)/shard_map/ppermute | solution.py:14
  14.3 20.7 %collective-permute-start.1 = (bf16[32,3,128]{2,1,0:T(4,128)(2,1)S(1)}, bf16[32,3,128]{2,1,0:T(4,128)(2,1)S(1)}, u32[]{:S(2)}, u32[]{:S(2)}) collective-permute-start(bf16[32,3,128]{2,1,0:T(4,128)(2,1)S(1)} %get-tuple-element.67), channel_id=1, source_target_pairs={{8,0},{16,8},{24,16},{32,24},{40,32},{48,40},{56,48},{64,56},{72,6... | collective-permute-start | bytes 73736 | tf_op jit(solution)/shard_map/ppermute | solution.py:16
  34.1 16.3 %copy-start.5 = (f32[128]{0:T(128)}, f32[128]{0:T(128)S(1)}, u32[]{:S(2)}) copy-start(f32[128]{0:T(128)S(1)} %get-tuple-element.107) | copy-start | bytes 1540
  34.1 16.3 %copy-start.7 = (f32[128]{0:T(128)}, f32[128]{0:T(128)S(1)}, u32[]{:S(2)}) copy-start(f32[128]{0:T(128)S(1)} %get-tuple-element.108) | copy-start | bytes 1540
  34.1 16.3 %copy-start.9 = (f32[128]{0:T(128)}, f32[128]{0:T(128)S(1)}, u32[]{:S(2)}) copy-start(f32[128]{0:T(128)S(1)} %get-tuple-element.109) | copy-start | bytes 1540
  34.1 16.3 %copy-start.11 = (f32[128]{0:T(128)}, f32[128]{0:T(128)S(1)}, u32[]{:S(2)}) copy-start(f32[128]{0:T(128)S(1)} %get-tuple-element.110) | copy-start | bytes 1540
  34.1 16.3 %copy-start.13 = (f32[128]{0:T(128)}, f32[128]{0:T(128)S(1)}, u32[]{:S(2)}) copy-start(f32[128]{0:T(128)S(1)} %get-tuple-element.111) | copy-start | bytes 1540
  34.1 16.3 %copy-start.15 = (f32[128]{0:T(128)}, f32[128]{0:T(128)S(1)}, u32[]{:S(2)}) copy-start(f32[128]{0:T(128)S(1)} %get-tuple-element.112) | copy-start | bytes 1540
  34.1 16.3 %copy-start.17 = (f32[128]{0:T(128)}, f32[128]{0:T(128)S(1)}, u32[]{:S(2)}) copy-start(f32[128]{0:T(128)S(1)} %get-tuple-element.113) | copy-start | bytes 1540
  34.1 16.3 %copy-start.19 = (f32[128]{0:T(128)}, f32[128]{0:T(128)S(1)}, u32[]{:S(2)}) copy-start(f32[128]{0:T(128)S(1)} %get-tuple-element.114) | copy-start | bytes 1540
  34.1 16.3 %copy-start.21 = (f32[128]{0:T(128)}, f32[128]{0:T(128)S(1)}, u32[]{:S(2)}) copy-start(f32[128]{0:T(128)S(1)} %get-tuple-element.115) | copy-start | bytes 1540
  35.0 5.7 collective-permute-start.2
  38.8 5.3 collective-permute-start.3
  64.3 128.5 %copy-start.26 = (pred[38]{0:T(512)(128)(4,1)S(1)}, pred[38]{0:T(512)(128)(4,1)}, u32[]{:S(2)}) copy-start(pred[38]{0:T(512)(128)(4,1)} %copy-done.25) | copy-start | bytes 118
  64.4 120.7 %collective-permute-start.4 = (bf16[32,3,128]{2,1,0:T(4,128)(2,1)S(1)}, bf16[32,3,128]{2,1,0:T(4,128)(2,1)S(1)}, u32[]{:S(2)}, u32[]{:S(2)}) collective-permute-start(bf16[32,3,128]{2,1,0:T(4,128)(2,1)S(1)} %get-tuple-element.64), channel_id=1, source_target_pairs={{0,8},{8,16},{16,24},{24,32},{32,40},{40,48},{48,56},{56,64},{64,7... | collective-permute-start | bytes 73736 | tf_op jit(solution)/shard_map/ppermute | solution.py:14
  66.3 118.7 %collective-permute-start.5 = (bf16[32,3,128]{2,1,0:T(4,128)(2,1)S(1)}, bf16[32,3,128]{2,1,0:T(4,128)(2,1)S(1)}, u32[]{:S(2)}, u32[]{:S(2)}) collective-permute-start(bf16[32,3,128]{2,1,0:T(4,128)(2,1)S(1)} %get-tuple-element.65), channel_id=1, source_target_pairs={{8,0},{16,8},{24,16},{32,24},{40,32},{48,40},{56,48},{64,56},{72,6... | collective-permute-start | bytes 73736 | tf_op jit(solution)/shard_map/ppermute | solution.py:16
  78.5 114.5 %copy-start.2 = (bf16[32,48,128]{2,1,0:T(8,128)(2,1)S(1)}, bf16[32,48,128]{2,1,0:T(8,128)(2,1)}, u32[]{:S(2)}) copy-start(bf16[32,48,128]{2,1,0:T(8,128)(2,1)} %param.10) | copy-start | bytes 1179652
  78.5 114.5 %copy-start.6 = (f32[128]{0:T(128)S(1)}, f32[128]{0:T(128)}, u32[]{:S(2)}) copy-start(f32[128]{0:T(128)} %copy-done.5) | copy-start | bytes 1540
  78.6 114.5 %copy-start.8 = (f32[128]{0:T(128)S(1)}, f32[128]{0:T(128)}, u32[]{:S(2)}) copy-start(f32[128]{0:T(128)} %copy-done.7) | copy-start | bytes 1540
  78.6 114.5 %copy-start.10 = (f32[128]{0:T(128)S(1)}, f32[128]{0:T(128)}, u32[]{:S(2)}) copy-start(f32[128]{0:T(128)} %copy-done.9) | copy-start | bytes 1540
  78.6 114.5 %copy-start.12 = (f32[128]{0:T(128)S(1)}, f32[128]{0:T(128)}, u32[]{:S(2)}) copy-start(f32[128]{0:T(128)} %copy-done.11) | copy-start | bytes 1540
  78.6 114.5 %copy-start.14 = (f32[128]{0:T(128)S(1)}, f32[128]{0:T(128)}, u32[]{:S(2)}) copy-start(f32[128]{0:T(128)} %copy-done.13) | copy-start | bytes 1540
  78.6 114.5 %copy-start.16 = (f32[128]{0:T(128)S(1)}, f32[128]{0:T(128)}, u32[]{:S(2)}) copy-start(f32[128]{0:T(128)} %copy-done.15) | copy-start | bytes 1540
  78.6 114.5 %copy-start.18 = (f32[128]{0:T(128)S(1)}, f32[128]{0:T(128)}, u32[]{:S(2)}) copy-start(f32[128]{0:T(128)} %copy-done.17) | copy-start | bytes 1540
  78.6 114.5 %copy-start.20 = (f32[128]{0:T(128)S(1)}, f32[128]{0:T(128)}, u32[]{:S(2)}) copy-start(f32[128]{0:T(128)} %copy-done.19) | copy-start | bytes 1540
  78.6 114.5 %copy-start.22 = (f32[128]{0:T(128)S(1)}, f32[128]{0:T(128)}, u32[]{:S(2)}) copy-start(f32[128]{0:T(128)} %copy-done.21) | copy-start | bytes 1540
  78.6 114.5 %copy-start.24 = (f32[128]{0:T(128)S(1)}, f32[128]{0:T(128)}, u32[]{:S(2)}) copy-start(f32[128]{0:T(128)} %copy-done.23) | copy-start | bytes 1540
  185.1 5.2 collective-permute-start.6
  187.0 5.8 collective-permute-start.7
  (6 other events, 45.8 us)
Sparse Core Ops, SparseCore 0:
  190.4 465.1 all-reduce.2
where the time goes:
time: 666 us
  waiting for transfers between devices  463 us (70%)
  blocking collectives  105 us (16%)
  starting transfers between devices  48.8 us (7%)
  other arithmetic  27.5 us (4%)
  between operations  14.7 us (2%)
    psum x1, waiting for transfers between devices, shards(): lax.psum((kernel_term, w_in_term, w_out_term), ('lon', 'lat'))  456 us
    psum x1, blocking collectives, shards(): lax.psum((kernel_term, w_in_term, w_out_term), ('lon', 'lat'))  105 us
    ppermute x4, starting transfers between devices, with_halo(): lax.ppermute(head, axis, [((i + 1) % count, i) for i in range(count)])  36.4 us
  transfers between devices with their start and end apart: 9, of which 4 were waited for; matrix products, arithmetic and copies ran while one was open for 1% of the time, Pallas kernels for 0%

commit v1 on v0

--- a/solution.py
+++ b/solution.py
@@ -1,7 +1,14 @@
 import jax
 import jax.numpy as jnp
 from jax import lax
+from jax.sharding import Mesh
 from jax.sharding import PartitionSpec as P
+
+LINK = jnp.bfloat16
+LON = ("x", "yh", "z")
+LAT = ("yl", "core")
+OUTER = ("x", "yh", "yl", "core")
+INNER = ("z",)
 
 
 def with_halo(cells, sides, width):
@@ -109,12 +116,50 @@
 
 
 def zero_poles(padded, width):
-    position = lax.axis_index("lat")
-    count = lax.axis_size("lat")
+    position = lax.axis_index(LAT)
+    count = lax.axis_size(LAT)
     row_ids = lax.broadcasted_iota(jnp.int32, (padded.shape[0], 1, 1), 0)
     north = jnp.logical_and(position == 0, row_ids < width)
     south = jnp.logical_and(position == count - 1, row_ids >= padded.shape[0] - width)
     return jnp.where(jnp.logical_or(north, south), jnp.zeros_like(padded), padded)
+
+
+def group_size(axes):
+    size = 1
+    for axis in axes:
+        size *= lax.axis_size(axis)
+    return size
+
+
+def grid_sum(block):
+    size = group_size(OUTER)
+    chunk = block.shape[0] // size
+    parts = lax.all_to_all(
+        block.astype(LINK).reshape(size, chunk, 128), OUTER, 0, 0, tiled=True
+    )
+    own = jnp.sum(parts.astype(jnp.float32), axis=0)
+    count = group_size(INNER)
+    copies = jnp.broadcast_to(own[None], (count, chunk, 128))
+    total = jnp.sum(lax.all_to_all(copies, INNER, 0, 0, tiled=True), axis=0)
+    spread = jnp.broadcast_to(total.astype(LINK)[None], (size, chunk, 128))
+    return lax.all_to_all(spread, OUTER, 0, 0, tiled=True).reshape(size * chunk, 128)
+
+
+def sum_terms(kernel_term, w_in_term, w_out_term):
+    block = jnp.concatenate(
+        [
+            w_in_term.reshape(-1, 128),
+            w_out_term,
+            kernel_term.reshape(49, 128),
+            jnp.zeros((15, 128), jnp.float32),
+        ]
+    )
+    total = grid_sum(block).astype(jnp.float32)
+    return (
+        total[512:561].reshape(7, 7, 128),
+        total[0:256].reshape(128, 256),
+        total[256:512],
+    )
 
 
 def shards(fields, ocean, cotangent, kernel, ln_gain, w_in, b_in, w_out):
@@ -124,33 +169,26 @@
     ocean_f = ocean.astype(jnp.float32)[..., None]
     masked = fields * ocean_b
     gmask = cotangent * ocean_b
-    padded = zero_poles(with_halo(masked, (("lon", 1), ("lat", 0)), 3), 3)
+    padded = zero_poles(with_halo(masked, ((LON, 1), (LAT, 0)), 3), 3)
     z_cells = depthwise(padded, kernel, row_count, col_count)
     out_term, dz_cells, w_in_term, w_out_term = pointwise(
         z_cells, gmask, ln_gain, w_in, b_in, w_out
     )
     kernel_term = kernel_terms(padded, dz_cells, row_count, col_count)
-    dz_padded = zero_poles(with_halo(dz_cells, (("lon", 1), ("lat", 0)), 3), 3)
+    dz_padded = zero_poles(with_halo(dz_cells, ((LON, 1), (LAT, 0)), 3), 3)
     advanced = (ocean_f * (fields.astype(jnp.float32) + out_term)).astype(jnp.bfloat16)
     back = depthwise_back(dz_padded, kernel, row_count, col_count)
     field_grad = (ocean_f * (cotangent.astype(jnp.float32) + back)).astype(jnp.bfloat16)
-    kernel_sum, w_in_sum, w_out_sum = lax.psum((kernel_term, w_in_term, w_out_term), ("lon", "lat"))
+    kernel_sum, w_in_sum, w_out_sum = sum_terms(kernel_term, w_in_term, w_out_term)
     factor = 1.0 / jnp.sqrt(
-        jnp.float32(row_count * col_count * lax.axis_size("lat") * lax.axis_size("lon"))
+        jnp.float32(row_count * col_count * lax.axis_size(LAT) * lax.axis_size(LON))
     )
     return (advanced, field_grad, kernel_sum * factor, w_in_sum * factor, w_out_sum * factor)
 
 
 def solution(mesh):
-    in_specs = (
-        P("lat", "lon", None),
-        P("lat", "lon"),
-        P("lat", "lon", None),
-        P(),
-        P(),
-        P(),
-        P(),
-        P(),
-    )
-    out_specs = (P("lat", "lon", None), P("lat", "lon", None), P(), P(), P())
-    return jax.shard_map(shards, mesh=mesh, in_specs=in_specs, out_specs=out_specs, check_vma=False)
+    torus = Mesh(mesh.devices.reshape(4, 2, 12, 4, 2), LON + LAT)
+    cells = P(LAT, LON, None)
+    in_specs = (cells, P(LAT, LON), cells, P(), P(), P(), P(), P())
+    out_specs = (cells, cells, P(), P(), P())
+    return jax.shard_map(shards, mesh=torus, in_specs=in_specs, out_specs=out_specs, check_vma=False)

time: 666 us -> 134 us (0.20)
  waiting for transfers between devices: 463 us -> 19.7 us
  blocking collectives: 105 us -> 0 us
  starting transfers between devices: 48.8 us -> 79.4 us
  between operations: 14.7 us -> 1.04 us
    psum x1 -> x0, waiting for transfers between devices: 456 us -> none  [shards(): lax.psum((kernel_term, w_in_term, w_out_term), ('lon', 'lat'))]
    psum x1 -> x0, blocking collectives: 105 us -> none  [shards(): lax.psum((kernel_term, w_in_term, w_out_term), ('lon', 'lat'))]
    all_to_all x0 -> x3, starting transfers between devices: none -> 25.7 us  [the longest x1 14.9 us: grid_sum(): lax.all_to_all(spread, OUTER, 0, 0, tiled=True).reshape(size * chunk, 128)]
    all_to_all x0 -> x3, waiting for transfers between devices: none -> 15.5 us  [the longest x1 10.1 us: grid_sum(): total = jnp.sum(lax.all_to_all(copies, INNER, 0, 0, tiled=True), axis=0)]
  transfers between devices with their start and end apart: 9 -> 11, of which waited for: 4 -> 4; matrix products, arithmetic and copies ran while one was open for 1% -> 7% of each run, Pallas kernels for 0% -> 0%
where the time goes in v1:
time: 134 us
  starting transfers between devices  79.4 us (59%)
  other arithmetic  24.7 us (18%)
  waiting for transfers between devices  19.7 us (15%)
  local copies, waits for them, and re-layouts  4.55 us (3%)
  matrix products  4.25 us (3%)
    ppermute x4, starting transfers between devices, with_halo(): lax.ppermute(head, axis, [((i + 1) % count, i) for i in range(count)])  40 us
    all_to_all x1, starting transfers between devices, grid_sum(): lax.all_to_all(spread, OUTER, 0, 0, tiled=True).reshape(size * chunk, 128)  14.9 us
    ppermute x4, starting transfers between devices, with_halo(): lax.ppermute(tail, axis, [(i, (i + 1) % count) for i in range(count)])  13.7 us
    all_to_all x1, waiting for transfers between devices, grid_sum(): total = jnp.sum(lax.all_to_all(copies, INNER, 0, 0, tiled=True), axis=0)  10.1 us
    all_to_all x1, starting transfers between devices, grid_sum(): lax.all_to_all(block.astype(LINK).reshape(size, chunk, 128), OUTER, 0, 0,...  7.13 us
    convert_element_type x1, other arithmetic, shards(): (ocean_f * (cotangent.astype(jnp.float32) + back)).astype(jnp.bfloat16)  6.68 us
    reduce_sum x1, other arithmetic, pointwise(): average = jnp.mean(flat_cells, axis=-1, keepdims=True)  6.03 us
    all_to_all x1, waiting for transfers between devices, grid_sum(): lax.all_to_all(spread, OUTER, 0, 0, tiled=True).reshape(size * chunk, 128)  5.31 us
  transfers between devices with their start and end apart: 11, of which 4 were waited for; matrix products, arithmetic and copies ran while one was open for 7% of the time, Pallas kernels for 0%

profile of v1, /device:TPU:1, one launch (start us, length us, event | category | flops | bytes accessed | tf_op | source)
XLA Modules:
  0.0 133.7 jit_solution(11723050758512991643)
XLA Ops:
  0.7 0.8 fusion.108
  1.5 1.4 %broadcast_multiply_fusion = (bf16[32,48,128]{2,1,0:T(8,128)(2,1)S(1)}, bf16[32,48,128]{2,1,0:T(8,128)(2,1)S(1)}) fusion(bf16[32,48,128]{2,1,0:T(8,128)(2,1)} %param.10, bf16[32,48]{1,0:T(8,128)(2,1)S(1)} %get-tuple-element.118, bf16[32,48,128]{2,1,0:T(8,128)(2,1)} %param.8), kind=kLoop, calls=%fused_computation.219 | loop fusion | flops 393216 | bytes 1575936 | tf_op jit(solution)/shard_map/mul | solution.py:171
  2.9 4.8 %collective-permute-start = (bf16[32,3,128]{2,1,0:T(4,128)(2,1)S(1)}, bf16[32,3,128]{2,1,0:T(4,128)(2,1)S(1)}, u32[]{:S(2)}, u32[]{:S(2)}) collective-permute-start(bf16[32,3,128]{2,1,0:T(4,128)(2,1)S(1)} %get-tuple-element.64), channel_id=1, source_target_pairs={{0,8},{8,16},{16,24},{24,32},{32,40},{40,48},{48,56},{56,64},{64,7... | collective-permute-start | bytes 73736 | tf_op jit(solution)/shard_map/ppermute | solution.py:21
  7.7 19.7 %collective-permute-start.1 = (bf16[32,3,128]{2,1,0:T(4,128)(2,1)S(1)}, bf16[32,3,128]{2,1,0:T(4,128)(2,1)S(1)}, u32[]{:S(2)}, u32[]{:S(2)}) collective-permute-start(bf16[32,3,128]{2,1,0:T(4,128)(2,1)S(1)} %get-tuple-element.65), channel_id=1, source_target_pairs={{8,0},{16,8},{24,16},{32,24},{40,32},{48,40},{56,48},{64,56},{72,6... | collective-permute-start | bytes 73736 | tf_op jit(solution)/shard_map/ppermute | solution.py:23
  27.5 0.9 collective-permute-done.1
  28.4 3.7 %collective-permute-start.2 = (bf16[3,54,128]{2,1,0:T(8,128)(2,1)S(1)}, bf16[3,54,128]{2,1,0:T(8,128)(2,1)S(1)}, u32[]{:S(2)}, u32[]{:S(2)}) collective-permute-start(bf16[3,54,128]{2,1,0:T(8,128)(2,1)S(1)} %get-tuple-element.60), channel_id=1, source_target_pairs={{0,1},{1,2},{2,3},{3,4},{4,5},{5,6},{6,7},{7,0},{8,9},{9,10},{10,1... | collective-permute-start | bytes 124424 | tf_op jit(solution)/shard_map/ppermute | solution.py:21
  32.2 1.9 %collective-permute-start.3 = (bf16[3,54,128]{2,1,0:T(8,128)(2,1)S(1)}, bf16[3,54,128]{2,1,0:T(8,128)(2,1)S(1)}, u32[]{:S(2)}, u32[]{:S(2)}) collective-permute-start(bf16[3,54,128]{2,1,0:T(8,128)(2,1)S(1)} %get-tuple-element.61), channel_id=1, source_target_pairs={{1,0},{2,1},{3,2},{4,3},{5,4},{6,5},{7,6},{0,7},{9,8},{10,9},{11,1... | collective-permute-start | bytes 124424 | tf_op jit(solution)/shard_map/ppermute | solution.py:23
  34.2 3.3 %collective-permute-done.3 = bf16[3,54,128]{2,1,0:T(8,128)(2,1)S(1)} collective-permute-done((bf16[3,54,128]{2,1,0:T(8,128)(2,1)S(1)}, bf16[3,54,128]{2,1,0:T(8,128)(2,1)S(1)}, u32[]{:S(2)}, u32[]{:S(2)}) %collective-permute-start.3) | collective-permute-done | bytes 41504 | tf_op jit(solution)/shard_map/ppermute | solution.py:23
  37.8 6.0 %fusion.104 = (f32[32,48]{1,0:T(8,128)S(1)}, f32[32,48,128]{2,1,0:T(8,128)S(1)}) fusion(f32[128]{0:T(128)S(1)} %get-tuple-element.115, bf16[38,54,128]{2,1,0:T(8,128)(2,1)S(1)} %maximum_select_fusion, f32[128]{0:T(128)S(1)} %get-tuple-element.116, f32[128]{0:T(128)S(1)} %get-tuple-element.69, f32[128]{0:T(128)S(1)} %get-tuple-element.70, ...), kind=kLoop, calls=%fused_computation.342 | loop fusion | flops 28899840 | bytes 20085248 | tf_op jit(solution)/shard_map/reduce_sum | solution.py:81
  45.8 0.8 fusion
  46.9 1.9 %fusion.103 = (f32[1536]{0:T(1024)S(1)}, f32[1536]{0:T(1024)S(1)}, f32[1536,128]{1,0:T(8,128)S(1)}) fusion(f32[1536]{0:T(1024)S(1)} %rsqrt.12, f32[1536]{0:T(1024)S(1)} %div.15, f32[32,48,128]{2,1,0:T(8,128)S(1)} %get-tuple-element.57, f32[128]{0:T(128)S(1)} %copy-done.5, bf16[1536,256]{1,0:T(8,128)(2,1)S(1)} %fusion, bf16[128,256]{1,0:T(8,128)(2,1)S(1)} %copy-done), kind=kOutput, calls=%fused_computation.341 | convolution fusion | flops 101839872 | bytes 2449920 | tf_op jit(solution)/shard_map/dot_general | solution.py:101
  48.8 1.2 multiply_convert_fusion.2
  50.0 2.0 %fusion.100 = (bf16[128]{0:T(256)(128)(2,1)S(1)}, bf16[128]{0:T(256)(128)(2,1)S(1)}, bf16[128]{0:T(256)(128)(2,1)S(1)}, bf16[128]{0:T(256)(128)(2,1)S(1)}, bf16[...) fusion(bf16[32,48,128]{2,1,0:T(8,128)(2,1)S(1)} %bitcast.284, ...), kind=kLoop, calls=%fused_computation.206 | loop fusion | flops 10811136 | bytes 7475712 | tf_op jit(solution)/shard_map/reduce_sum | solution.py:65
  52.1 2.0 %fusion.101 = (bf16[128]{0:T(256)(128)(2,1)S(1)}, bf16[128]{0:T(256)(128)(2,1)S(1)}, bf16[128]{0:T(256)(128)(2,1)S(1)}, bf16[128]{0:T(256)(128)(2,1)S(1)}, bf16[...) fusion(bf16[32,48,128]{2,1,0:T(8,128)(2,1)S(1)} %bitcast.285, ...), kind=kLoop, calls=%fused_computation.207 | loop fusion | flops 10811136 | bytes 7475712 | tf_op jit(solution)/shard_map/reduce_sum | solution.py:65
  54.1 1.1 fusion.99
  56.6 0.8 convert_element_type.506
  57.3 7.1 %all-to-all-start = ((bf16[64,9,128]{2,1,0:T(8,128)(2,1)}), bf16[64,9,128]{2,1,0:T(8,128)(2,1)S(1)}, u32[]{:S(2)}, u32[]{:S(2)}) async-start(bf16[64,9,128]{2,1,0:T(8,128)(2,1)} %convert_element_type.506), calls=%async_computation | async-start | bytes 524288 | tf_op jit(solution)/shard_map/all_to_all | solution.py:137
  64.5 1.9 %collective-permute-start.4 = (bf16[32,3,128]{2,1,0:T(4,128)(2,1)S(1)}, bf16[32,3,128]{2,1,0:T(4,128)(2,1)S(1)}, u32[]{:S(2)}, u32[]{:S(2)}) collective-permute-start(bf16[32,3,128]{2,1,0:T(4,128)(2,1)S(1)} %get-tuple-element.62), channel_id=1, source_target_pairs={{0,8},{8,16},{16,24},{24,32},{32,40},{40,48},{48,56},{56,64},{64,7... | collective-permute-start | bytes 73736 | tf_op jit(solution)/shard_map/ppermute | solution.py:21
  66.4 16.5 %collective-permute-start.5 = (bf16[32,3,128]{2,1,0:T(4,128)(2,1)S(1)}, bf16[32,3,128]{2,1,0:T(4,128)(2,1)S(1)}, u32[]{:S(2)}, u32[]{:S(2)}) collective-permute-start(bf16[32,3,128]{2,1,0:T(4,128)(2,1)S(1)} %get-tuple-element.63), channel_id=1, source_target_pairs={{8,0},{16,8},{24,16},{32,24},{40,32},{48,40},{56,48},{64,56},{72,6... | collective-permute-start | bytes 73736 | tf_op jit(solution)/shard_map/ppermute | solution.py:23
  82.9 1.0 multiply_convert_fusion.3
  84.0 3.3 %collective-permute-start.6 = (bf16[3,54,128]{2,1,0:T(8,128)(2,1)S(1)}, bf16[3,54,128]{2,1,0:T(8,128)(2,1)S(1)}, u32[]{:S(2)}, u32[]{:S(2)}) collective-permute-start(bf16[3,54,128]{2,1,0:T(8,128)(2,1)S(1)} %get-tuple-element.58), channel_id=1, source_target_pairs={{0,1},{1,2},{2,3},{3,4},{4,5},{5,6},{6,7},{7,0},{8,9},{9,10},{10,1... | collective-permute-start | bytes 124424 | tf_op jit(solution)/shard_map/ppermute | solution.py:21
  87.3 1.9 %collective-permute-start.7 = (bf16[3,54,128]{2,1,0:T(8,128)(2,1)S(1)}, bf16[3,54,128]{2,1,0:T(8,128)(2,1)S(1)}, u32[]{:S(2)}, u32[]{:S(2)}) collective-permute-start(bf16[3,54,128]{2,1,0:T(8,128)(2,1)S(1)} %get-tuple-element.59), channel_id=1, source_target_pairs={{1,0},{2,1},{3,2},{4,3},{5,4},{6,5},{7,6},{0,7},{9,8},{10,9},{11,1... | collective-permute-start | bytes 124424 | tf_op jit(solution)/shard_map/ppermute | solution.py:23
  89.3 0.7 broadcast_in_dim.19
  89.9 3.7 %all-to-all-start.1 = ((f32[12,9,128]{2,1,0:T(8,128)}), f32[12,9,128]{2,1,0:T(8,128)S(1)}, u32[]{:S(2)}, u32[]{:S(2)}) async-start(f32[12,9,128]{2,1,0:T(8,128)} %broadcast_in_dim.19), calls=%async_computation.1 | async-start | bytes 196608 | tf_op jit(solution)/shard_map/all_to_all | solution.py:143
  93.9 10.1 %all-to-all-done.1 = f32[12,9,128]{2,1,0:T(8,128)S(1)} async-done(((f32[12,9,128]{2,1,0:T(8,128)}), f32[12,9,128]{2,1,0:T(8,128)S(1)}, u32[]{:S(2)}, u32[]{:S(2)}) %all-to-all-start.1) | async-done | bytes 55328 | tf_op jit(solution)/shard_map/all_to_all | solution.py:143
  104.0 0.7 broadcast_in_dim.20
  104.8 14.9 %all-to-all-start.2 = ((bf16[64,9,128]{2,1,0:T(8,128)(2,1)}), bf16[64,9,128]{2,1,0:T(8,128)(2,1)S(1)}, u32[]{:S(2)}, u32[]{:S(2)}) async-start(bf16[64,9,128]{2,1,0:T(8,128)(2,1)} %broadcast_in_dim.20), calls=%async_computation.2 | async-start | bytes 524288 | tf_op jit(solution)/shard_map/all_to_all | solution.py:145
  119.7 6.7 %multiply_convert_fusion.1 = bf16[32,48,128]{2,1,0:T(8,128)(2,1)} fusion(bf16[32,48,128]{2,1,0:T(8,128)(2,1)S(1)} %copy-done.2, bf16[38,54,128]{2,1,0:T(8,128)(2,1)S(1)} %maximum_select_fusion.1, f32[128]{0:T(128)S(1)} %get-tuple-element.115, f32[128]{0:T(128)S(1)} %get-tuple-element.116, f32[128]{0:T(128)S(1)} %get-tuple-element.69, ...), kind=kLoop, calls=%fused_computation.210 | loop fusion | flops 29491200 | bytes 20085248 | tf_op jit(solution)/shard_map/convert_element_type | solution.py:181
  126.3 5.3 %all-to-all-done.2 = bf16[64,9,128]{2,1,0:T(8,128)(2,1)S(1)} async-done(((bf16[64,9,128]{2,1,0:T(8,128)(2,1)}), bf16[64,9,128]{2,1,0:T(8,128)(2,1)S(1)}, u32[]{:S(2)}, u32[]{:S(2)}) %all-to-all-start.2) | async-done | bytes 147488 | tf_op jit(solution)/shard_map/all_to_all | solution.py:145
  131.7 0.7 slice_multiply_fusion
  132.4 0.7 mul.1343
  133.1 0.6 mul.1340
  (65 shorter events, 4.5 us)
Async XLA Ops:
  0.6 44.3 %copy-start = (bf16[128,256]{1,0:T(8,128)(2,1)S(1)}, bf16[128,256]{1,0:T(8,128)(2,1)}, u32[]{:S(2)}) copy-start(bf16[128,256]{1,0:T(8,128)(2,1)} %param.13) | copy-start | bytes 196612
  0.6 26.8 %copy-start.4 = (f32[7,7,128]{2,1,0:T(8,128)S(1)}, f32[7,7,128]{2,1,0:T(8,128)}, u32[]{:S(2)}) copy-start(f32[7,7,128]{2,1,0:T(8,128)} %param.11) | copy-start | bytes 75268
  2.9 24.6 %collective-permute-start = (bf16[32,3,128]{2,1,0:T(4,128)(2,1)S(1)}, bf16[32,3,128]{2,1,0:T(4,128)(2,1)S(1)}, u32[]{:S(2)}, u32[]{:S(2)}) collective-permute-start(bf16[32,3,128]{2,1,0:T(4,128)(2,1)S(1)} %get-tuple-element.64), channel_id=1, source_target_pairs={{0,8},{8,16},{16,24},{24,32},{32,40},{40,48},{48,56},{56,64},{64,7... | collective-permute-start | bytes 73736 | tf_op jit(solution)/shard_map/ppermute | solution.py:21
  7.7 20.7 %collective-permute-start.1 = (bf16[32,3,128]{2,1,0:T(4,128)(2,1)S(1)}, bf16[32,3,128]{2,1,0:T(4,128)(2,1)S(1)}, u32[]{:S(2)}, u32[]{:S(2)}) collective-permute-start(bf16[32,3,128]{2,1,0:T(4,128)(2,1)S(1)} %get-tuple-element.65), channel_id=1, source_target_pairs={{8,0},{16,8},{24,16},{32,24},{40,32},{48,40},{56,48},{64,56},{72,6... | collective-permute-start | bytes 73736 | tf_op jit(solution)/shard_map/ppermute | solution.py:23
  28.4 5.8 %collective-permute-start.2 = (bf16[3,54,128]{2,1,0:T(8,128)(2,1)S(1)}, bf16[3,54,128]{2,1,0:T(8,128)(2,1)S(1)}, u32[]{:S(2)}, u32[]{:S(2)}) collective-permute-start(bf16[3,54,128]{2,1,0:T(8,128)(2,1)S(1)} %get-tuple-element.60), channel_id=1, source_target_pairs={{0,1},{1,2},{2,3},{3,4},{4,5},{5,6},{6,7},{7,0},{8,9},{9,10},{10,1... | collective-permute-start | bytes 124424 | tf_op jit(solution)/shard_map/ppermute | solution.py:21
  32.2 5.3 %collective-permute-start.3 = (bf16[3,54,128]{2,1,0:T(8,128)(2,1)S(1)}, bf16[3,54,128]{2,1,0:T(8,128)(2,1)S(1)}, u32[]{:S(2)}, u32[]{:S(2)}) collective-permute-start(bf16[3,54,128]{2,1,0:T(8,128)(2,1)S(1)} %get-tuple-element.61), channel_id=1, source_target_pairs={{1,0},{2,1},{3,2},{4,3},{5,4},{6,5},{7,6},{0,7},{9,8},{10,9},{11,1... | collective-permute-start | bytes 124424 | tf_op jit(solution)/shard_map/ppermute | solution.py:23
  37.7 6.7 %copy-start.5 = (f32[128]{0:T(128)S(1)}, f32[128]{0:T(128)}, u32[]{:S(2)}) copy-start(f32[128]{0:T(128)} %param.12) | copy-start | bytes 1540
  43.8 1.2 copy-start.6
  45.0 0.8 copy-start.3
  55.7 27.2 %copy-start.1 = (bf16[32,48,128]{2,1,0:T(8,128)(2,1)S(1)}, bf16[32,48,128]{2,1,0:T(8,128)(2,1)}, u32[]{:S(2)}) copy-start(bf16[32,48,128]{2,1,0:T(8,128)(2,1)} %param.8) | copy-start | bytes 1179652
  57.3 31.9 %all-to-all-start = ((bf16[64,9,128]{2,1,0:T(8,128)(2,1)}), bf16[64,9,128]{2,1,0:T(8,128)(2,1)S(1)}, u32[]{:S(2)}, u32[]{:S(2)}) async-start(bf16[64,9,128]{2,1,0:T(8,128)(2,1)} %convert_element_type.506), calls=%async_computation | async-start | bytes 524288 | tf_op jit(solution)/shard_map/all_to_all | solution.py:137
  64.5 19.5 %collective-permute-start.4 = (bf16[32,3,128]{2,1,0:T(4,128)(2,1)S(1)}, bf16[32,3,128]{2,1,0:T(4,128)(2,1)S(1)}, u32[]{:S(2)}, u32[]{:S(2)}) collective-permute-start(bf16[32,3,128]{2,1,0:T(4,128)(2,1)S(1)} %get-tuple-element.62), channel_id=1, source_target_pairs={{0,8},{8,16},{16,24},{24,32},{32,40},{40,48},{48,56},{56,64},{64,7... | collective-permute-start | bytes 73736 | tf_op jit(solution)/shard_map/ppermute | solution.py:21
  66.4 17.5 %collective-permute-start.5 = (bf16[32,3,128]{2,1,0:T(4,128)(2,1)S(1)}, bf16[32,3,128]{2,1,0:T(4,128)(2,1)S(1)}, u32[]{:S(2)}, u32[]{:S(2)}) collective-permute-start(bf16[32,3,128]{2,1,0:T(4,128)(2,1)S(1)} %get-tuple-element.63), channel_id=1, source_target_pairs={{8,0},{16,8},{24,16},{32,24},{40,32},{48,40},{56,48},{64,56},{72,6... | collective-permute-start | bytes 73736 | tf_op jit(solution)/shard_map/ppermute | solution.py:23
  83.9 35.7 %copy-start.2 = (bf16[32,48,128]{2,1,0:T(8,128)(2,1)S(1)}, bf16[32,48,128]{2,1,0:T(8,128)(2,1)}, u32[]{:S(2)}) copy-start(bf16[32,48,128]{2,1,0:T(8,128)(2,1)} %param.10) | copy-start | bytes 1179652
  84.0 9.6 %collective-permute-start.6 = (bf16[3,54,128]{2,1,0:T(8,128)(2,1)S(1)}, bf16[3,54,128]{2,1,0:T(8,128)(2,1)S(1)}, u32[]{:S(2)}, u32[]{:S(2)}) collective-permute-start(bf16[3,54,128]{2,1,0:T(8,128)(2,1)S(1)} %get-tuple-element.58), channel_id=1, source_target_pairs={{0,1},{1,2},{2,3},{3,4},{4,5},{5,6},{6,7},{7,0},{8,9},{9,10},{10,1... | collective-permute-start | bytes 124424 | tf_op jit(solution)/shard_map/ppermute | solution.py:21
  87.3 6.4 %collective-permute-start.7 = (bf16[3,54,128]{2,1,0:T(8,128)(2,1)S(1)}, bf16[3,54,128]{2,1,0:T(8,128)(2,1)S(1)}, u32[]{:S(2)}, u32[]{:S(2)}) collective-permute-start(bf16[3,54,128]{2,1,0:T(8,128)(2,1)S(1)} %get-tuple-element.59), channel_id=1, source_target_pairs={{1,0},{2,1},{3,2},{4,3},{5,4},{6,5},{7,6},{0,7},{9,8},{10,9},{11,1... | collective-permute-start | bytes 124424 | tf_op jit(solution)/shard_map/ppermute | solution.py:23
  89.9 14.1 %all-to-all-start.1 = ((f32[12,9,128]{2,1,0:T(8,128)}), f32[12,9,128]{2,1,0:T(8,128)S(1)}, u32[]{:S(2)}, u32[]{:S(2)}) async-start(f32[12,9,128]{2,1,0:T(8,128)} %broadcast_in_dim.19), calls=%async_computation.1 | async-start | bytes 196608 | tf_op jit(solution)/shard_map/all_to_all | solution.py:143
  104.8 26.9 %all-to-all-start.2 = ((bf16[64,9,128]{2,1,0:T(8,128)(2,1)}), bf16[64,9,128]{2,1,0:T(8,128)(2,1)S(1)}, u32[]{:S(2)}, u32[]{:S(2)}) async-start(bf16[64,9,128]{2,1,0:T(8,128)(2,1)} %broadcast_in_dim.20), calls=%async_computation.2 | async-start | bytes 524288 | tf_op jit(solution)/shard_map/all_to_all | solution.py:145

commit v2 on v1

v2 whole, which is shorter than its diff:
```python
import jax
import jax.numpy as jnp
from jax import lax
from jax.experimental import pallas as pl
from jax.experimental.pallas import tpu as pltpu
from jax.sharding import Mesh
from jax.sharding import PartitionSpec as P

LINK = jnp.bfloat16
LON = ("x", "yh", "z")
LAT = ("yl", "core")
OUTER = ("x", "yh", "yl", "core")
INNER = ("z",)
ROWS = 32
COLS = 48
C = 128
FF = 256
LEFT = 8
STEP = 4
TERM_ROWS = 576


def fill(pad, own, west, east, north, south):
    f32 = jnp.float32
    pad[3 : 3 + ROWS, LEFT : LEFT + COLS, :] = own[...].astype(f32)
    pad[3 : 3 + ROWS, LEFT - 3 : LEFT, :] = west[...].astype(f32)
    pad[3 : 3 + ROWS, LEFT + COLS : LEFT + COLS + 3, :] = east[...].astype(f32)
    pad[0:3, LEFT - 3 : LEFT + COLS + 3, :] = north[...].astype(f32)
    pad[3 + ROWS : 6 + ROWS, LEFT - 3 : LEFT + COLS + 3, :] = south[...].astype(f32)


def conv_rows(pad, taps, first, flip):
    sums = [jnp.zeros((COLS, C), jnp.float32) for _ in range(STEP)]
    for row in range(STEP + 6):
        for col in range(7):
            cells = pad[first + row, LEFT - 3 + col : LEFT - 3 + col + COLS, :]
            for out in range(STEP):
                tap = row - out
                if 0 <= tap < 7:
                    at = tap * 7 + col
                    at = 48 - at if flip else at
                    sums[out] = sums[out] + cells * taps[at : at + 1, :]
    return jnp.concatenate(sums, axis=0)


def main_kernel(
    masked, west, east, north, south, gmask, ocean, taps, gain, w_in, b_in, w_out,
    advanced, dz_out, terms, pad, acc_in, acc_out, acc_tap,
):
    f32, bf16 = jnp.float32, jnp.bfloat16
    fill(pad, masked, west, east, north, south)
    acc_in[...] = jnp.zeros_like(acc_in)
    acc_out[...] = jnp.zeros_like(acc_out)
    acc_tap[...] = jnp.zeros_like(acc_tap)
    size = STEP * COLS

    def block(step, carry):
        first = step * STEP
        z = conv_rows(pad, taps, first, False)
        grad = gmask[pl.ds(first, STEP)].reshape(size, C)
        average = jnp.mean(z, axis=-1, keepdims=True)
        centre = z - average
        inverse = lax.rsqrt(jnp.mean(centre * centre, axis=-1, keepdims=True) + 1e-06)
        unit = centre * inverse
        normed = (unit * gain[...]).astype(bf16)
        preact = jnp.dot(normed, w_in[...], preferred_element_type=f32) + b_in[...]
        cdf = 0.5 * (1.0 + lax.erf(preact * 0.7071067811865476))
        hidden = (preact * cdf).astype(bf16)
        out = jnp.dot(hidden, w_out[...], preferred_element_type=f32)
        d_hidden = lax.dot_general(grad, w_out[...], (((1,), (1,)), ((), ())), preferred_element_type=f32)
        slopes = cdf + preact * jnp.exp(-0.5 * preact * preact) * 0.3989422804014327
        d_pre = (d_hidden * slopes).astype(bf16)
        contract = (((0,), (0,)), ((), ()))
        acc_out[...] += lax.dot_general(grad, hidden, contract, preferred_element_type=f32)
        acc_in[...] += lax.dot_general(normed, d_pre, contract, preferred_element_type=f32)
        d_norm = lax.dot_general(d_pre, w_in[...], (((1,), (1,)), ((), ())), preferred_element_type=f32)
        scaled = d_norm * gain[...]
        dz = inverse * (
            scaled
            - jnp.mean(scaled, axis=-1, keepdims=True)
            - unit * jnp.mean(scaled * unit, axis=-1, keepdims=True)
        )
        dz = dz.astype(bf16)
        dz_out[pl.ds(first, STEP)] = dz.reshape(STEP, COLS, C)
        own = masked[pl.ds(first, STEP)].reshape(size, C).astype(f32)
        keep = ocean[pl.ds(first, STEP)].reshape(size, C).astype(f32)
        advanced[pl.ds(first, STEP)] = (own + keep * out).astype(bf16).reshape(STEP, COLS, C)
        grads = dz.astype(f32)
        for tap in range(7):
            for col in range(7):
                total = jnp.zeros((COLS, C), f32)
                for row in range(STEP):
                    cells = pad[first + row + tap, LEFT - 3 + col : LEFT - 3 + col + COLS, :]
                    total = total + cells * grads[row * COLS : (row + 1) * COLS]
                acc_tap[tap * 7 + col] += jnp.sum(total.reshape(COLS // 8, 8, C), axis=0)
        return carry

    lax.fori_loop(0, ROWS // STEP, block, 0)
    terms[0:C, :] = acc_in[:, 0:C].astype(LINK)
    terms[C : 2 * C, :] = acc_in[:, C:].astype(LINK)
    terms[2 * C : 2 * C + FF, :] = acc_out[...].T.astype(LINK)
    tap_sums = jnp.sum(acc_tap[...], axis=1)
    terms[512:576, :] = jnp.concatenate([tap_sums, jnp.zeros((15, C), f32)], axis=0).astype(LINK)


def back_kernel(dz, west, east, north, south, gmask, ocean, taps, field_grad, pad):
    f32 = jnp.float32
    fill(pad, dz, west, east, north, south)
    size = STEP * COLS

    def block(step, carry):
        first = step * STEP
        back = conv_rows(pad, taps, first, True)
        own = gmask[pl.ds(first, STEP)].reshape(size, C).astype(f32)
        keep = ocean[pl.ds(first, STEP)].reshape(size, C).astype(f32)
        field_grad[pl.ds(first, STEP)] = (own + keep * back).astype(jnp.bfloat16).reshape(STEP, COLS, C)
        return carry

    lax.fori_loop(0, ROWS // STEP, block, 0)


def call(body, args, outs, scratch, flops):
    vmem = pl.BlockSpec(memory_space=pltpu.VMEM)
    return pl.pallas_call(
        body,
        out_shape=outs,
        in_specs=[vmem] * len(args),
        out_specs=[vmem] * len(outs),
        scratch_shapes=scratch,
        compiler_params=pltpu.CompilerParams(vmem_limit_bytes=40 << 20),
        cost_estimate=pl.CostEstimate(flops=flops, bytes_accessed=2 << 20, transcendentals=1 << 19),
    )(*args)


def cells_type():
    return jax.ShapeDtypeStruct((ROWS, COLS, C), jnp.bfloat16)


def pad_type():
    return pltpu.VMEM((ROWS + 6, COLS + 16, C), jnp.float32)


def group_size(axes):
    size = 1
    for axis in axes:
        size *= lax.axis_size(axis)
    return size


def halo(cells):
    lon = group_size(LON)
    lat = group_size(LAT)
    west = lax.ppermute(cells[:, COLS - 3 :], LON, [(i, (i + 1) % lon) for i in range(lon)])
    east = lax.ppermute(cells[:, :3], LON, [((i + 1) % lon, i) for i in range(lon)])
    top = jnp.concatenate([west[:3], cells[:3], east[:3]], axis=1)
    bottom = jnp.concatenate([west[ROWS - 3 :], cells[ROWS - 3 :], east[ROWS - 3 :]], axis=1)
    north = lax.ppermute(bottom, LAT, [(i, i + 1) for i in range(lat - 1)])
    south = lax.ppermute(top, LAT, [(i + 1, i) for i in range(lat - 1)])
    return west, east, north, south


def grid_sum(block):
    size = group_size(OUTER)
    chunk = TERM_ROWS // size
    parts = lax.all_to_all(block.reshape(size, chunk, C), OUTER, 0, 0, tiled=True)
    own = jnp.sum(parts.astype(jnp.float32), axis=0)
    count = group_size(INNER)
    copies = jnp.broadcast_to(own[None], (count, chunk, C))
    total = jnp.sum(lax.all_to_all(copies, INNER, 0, 0, tiled=True), axis=0)
    spread = jnp.broadcast_to(total.astype(LINK)[None], (size, chunk, C))
    return lax.all_to_all(spread, OUTER, 0, 0, tiled=True).reshape(TERM_ROWS, C)


def shards(fields, ocean, cotangent, kernel, ln_gain, w_in, b_in, w_out):
    ocean_b = jnp.broadcast_to(ocean.astype(jnp.bfloat16)[..., None], fields.shape)
    masked = fields * ocean_b
    gmask = cotangent * ocean_b
    taps = kernel.reshape(49, C)
    advanced, dz, terms = call(
        main_kernel,
        (masked, *halo(masked), gmask, ocean_b, taps, ln_gain.reshape(1, C), w_in, b_in.reshape(1, FF), w_out),
        [cells_type(), cells_type(), jax.ShapeDtypeStruct((TERM_ROWS, C), LINK)],
        [
            pad_type(),
            pltpu.VMEM((C, FF), jnp.float32),
            pltpu.VMEM((C, FF), jnp.float32),
            pltpu.VMEM((49, 8, C), jnp.float32),
        ],
        500_000_000,
    )
    sums = grid_sum(terms).astype(jnp.float32)
    (field_grad,) = call(
        back_kernel, (dz, *halo(dz), gmask, ocean_b, taps), [cells_type()], [pad_type()], 20_000_000
    )
    factor = 1.0 / jnp.sqrt(
        jnp.float32(ROWS * COLS * group_size(LAT) * group_size(LON))
    )
    sums = sums * factor
    w_in_sum = jnp.concatenate([sums[:C], sums[C : 2 * C]], axis=1)
    return (advanced, field_grad, sums[512:561].reshape(7, 7, C), w_in_sum, sums[256:512])


def solution(mesh):
    torus = Mesh(mesh.devices.reshape(4, 2, 12, 4, 2), LON + LAT)
    cells = P(LAT, LON, None)
    in_specs = (cells, P(LAT, LON), cells, P(), P(), P(), P(), P())
    out_specs = (cells, cells, P(), P(), P())
    return jax.shard_map(shards, mesh=torus, in_specs=in_specs, out_specs=out_specs, check_vma=False)
```

time: 134 us -> 117 us (0.87)
  other arithmetic: 24.7 us -> 2.99 us
  starting transfers between devices: 79.4 us -> 63.3 us
  Pallas kernels: 0 us -> 14.3 us
  waiting for transfers between devices: 19.7 us -> 30.1 us
  matrix products: 4.25 us -> 0 us
    pallas_call x0 -> x2, Pallas kernels: none -> 14.3 us  [call(): pl.pallas_call(body, out_shape=outs, in_specs=[vmem] * len(args), out_spe...]
    ppermute x8, waiting for transfers between devices: 4.24 us -> 18.1 us  [the longest x2 11 us: halo(): lax.ppermute(cells[:, COLS - 3:], LON, [(i, (i + 1) % lon) for i in range...]
    reduce_sum x5 -> x0, other arithmetic: 11.7 us -> none  [the longest x1 6.03 us: pointwise(): average = jnp.mean(flat_cells, axis=-1, keepdims=True)]
    convert_element_type x5 -> x1, other arithmetic: 10.2 us -> 0.72 us  [shards(): ocean.astype(jnp.bfloat16)[..., None]]
    ppermute x8, starting transfers between devices: 53.7 us -> 45 us  [the longest x2 29.5 us: halo(): lax.ppermute(cells[:, :3], LON, [((i + 1) % lon, i) for i in range(lon)])]
    all_to_all x2, starting transfers between devices: 22 us -> 14.9 us  [the longest x1 10.7 us: grid_sum(): return lax.all_to_all(spread, OUTER, 0, 0, tiled=True).reshape(TERM_ROWS, C)]
    dot_general x6 -> x0, matrix products: 4.25 us -> none  [the longest x1 1.92 us: pointwise(): lax.dot_general(d_pre, w_in, (((1,), (1,)), ((), ())), preferred_element_...]
    all_to_all x2, waiting for transfers between devices: 5.31 us -> 1.6 us  [the longest x1 1.59 us: grid_sum(): lax.all_to_all(block.reshape(size, chunk, C), OUTER, 0, 0, tiled=True)]
  transfers between devices with their start and end apart: 11 -> 11, of which waited for: 4 -> 5; matrix products, arithmetic and copies ran while one was open for 7% -> 1% of each run, Pallas kernels for 0% -> 3%
where the time goes in v2:
time: 117 us; the launch traced here: 116 us
  starting transfers between devices  63.3 us (54%)
  waiting for transfers between devices  30.1 us (26%)
  Pallas kernels  14.3 us (12%)
  local copies, waits for them, and re-layouts  4.56 us (4%)
  other arithmetic  2.99 us (3%)
    ppermute x2, starting transfers between devices, halo(): lax.ppermute(cells[:, :3], LON, [((i + 1) % lon, i) for i in range(lon)])  29.5 us
    pallas_call x2, Pallas kernels, call(): pl.pallas_call(body, out_shape=outs, in_specs=[vmem] * len(args), out_spe...  14.3 us
    ppermute x2, waiting for transfers between devices, halo(): lax.ppermute(cells[:, COLS - 3:], LON, [(i, (i + 1) % lon) for i in range...  11 us
    all_to_all x1, starting transfers between devices, grid_sum(): return lax.all_to_all(spread, OUTER, 0, 0, tiled=True).reshape(TERM_ROWS, C)  10.7 us
    all_to_all x1, waiting for transfers between devices, grid_sum(): total = jnp.sum(lax.all_to_all(copies, INNER, 0, 0, tiled=True), axis=0)  10.4 us
    ppermute x2, starting transfers between devices, halo(): north = lax.ppermute(bottom, LAT, [(i, i + 1) for i in range(lat - 1)])  7.76 us
    ppermute x2, waiting for transfers between devices, halo(): south = lax.ppermute(top, LAT, [(i + 1, i) for i in range(lat - 1)])  7.08 us
    all_to_all x1, starting transfers between devices, grid_sum(): lax.all_to_all(block.reshape(size, chunk, C), OUTER, 0, 0, tiled=True)  4.19 us
  transfers between devices with their start and end apart: 11, of which 5 were waited for; matrix products, arithmetic and copies ran while one was open for 1% of the time, Pallas kernels for 3%

profile of v2, /device:TPU:1, one launch (start us, length us, event | category | flops | bytes accessed | tf_op | source)
XLA Modules:
  0.0 116.2 jit_solution(10332253703410500229)
XLA Ops:
  0.6 0.7 convert_element_type.17
  1.4 1.4 %broadcast_multiply_fusion = (bf16[32,48,128]{2,1,0:T(8,128)(2,1)S(1)}, bf16[32,48,128]{2,1,0:T(8,128)(2,1)S(1)}) fusion(bf16[32,48,128]{2,1,0:T(8,128)(2,1)} %param.10, bf16[32,48]{1,0:T(8,128)(2,1)S(1)} %convert_element_type.17, bf16[32,48,128]{2,1,0:T(8,128)(2,1)} %param.8), kind=kLoop, calls=%fused_computation.2 | loop fusion | flops 393216 | bytes 1575936 | tf_op jit(solution)/shard_map/mul | solution.py:177
  2.8 22.6 %collective-permute-start.1 = (bf16[32,3,128]{2,1,0:T(4,128)(2,1)S(1)}, bf16[32,3,128]{2,1,0:T(4,128)(2,1)S(1)}, u32[]{:S(2)}, u32[]{:S(2)}) collective-permute-start(bf16[32,3,128]{2,1,0:T(4,128)(2,1)S(1)} %get-tuple-element.17), channel_id=1, source_target_pairs={{8,0},{16,8},{24,16},{32,24},{40,32},{48,40},{56,48},{64,56},{72,6... | collective-permute-start | bytes 73736 | tf_op jit(solution)/shard_map/ppermute | solution.py:154
  25.4 1.9 %collective-permute-start = (bf16[32,3,128]{2,1,0:T(4,128)(2,1)S(1)}, bf16[32,3,128]{2,1,0:T(4,128)(2,1)S(1)}, u32[]{:S(2)}, u32[]{:S(2)}) collective-permute-start(bf16[32,3,128]{2,1,0:T(4,128)(2,1)S(1)} %get-tuple-element.18), channel_id=1, source_target_pairs={{0,8},{8,16},{16,24},{24,32},{32,40},{40,48},{48,56},{56,64},{64,7... | collective-permute-start | bytes 73736 | tf_op jit(solution)/shard_map/ppermute | solution.py:153
  27.3 11.0 %collective-permute-done.west = bf16[32,3,128]{2,1,0:T(4,128)(2,1)S(1)} collective-permute-done((bf16[32,3,128]{2,1,0:T(4,128)(2,1)S(1)}, bf16[32,3,128]{2,1,0:T(4,128)(2,1)S(1)}, u32[]{:S(2)}, u32[]{:S(2)}) %collective-permute-start) | collective-permute-done | bytes 24608 | tf_op jit(solution)/shard_map/ppermute | solution.py:153
  38.4 4.2 %collective-permute-start.2 = (bf16[3,54,128]{2,1,0:T(8,128)(2,1)S(1)}, bf16[3,54,128]{2,1,0:T(8,128)(2,1)S(1)}, u32[]{:S(2)}, u32[]{:S(2)}) collective-permute-start(bf16[3,54,128]{2,1,0:T(8,128)(2,1)S(1)} %pad_maximum_fusion.1), channel_id=1, source_target_pairs={{0,1},{1,2},{2,3},{3,4},{4,5},{5,6},{6,7},{8,9},{9,10},{10,11},{11... | collective-permute-start | bytes 124424 | tf_op jit(solution)/shard_map/ppermute | solution.py:157
  42.6 0.0 copy-start.4
  42.7 1.9 %collective-permute-start.3 = (bf16[3,54,128]{2,1,0:T(8,128)(2,1)S(1)}, bf16[3,54,128]{2,1,0:T(8,128)(2,1)S(1)}, u32[]{:S(2)}, u32[]{:S(2)}) collective-permute-start(bf16[3,54,128]{2,1,0:T(8,128)(2,1)S(1)} %pad_maximum_fusion.2), channel_id=1, source_target_pairs={{1,0},{2,1},{3,2},{4,3},{5,4},{6,5},{7,6},{9,8},{10,9},{11,10},{12... | collective-permute-start | bytes 124424 | tf_op jit(solution)/shard_map/ppermute | solution.py:158
  44.6 3.4 %collective-permute-done.3.south = bf16[3,54,128]{2,1,0:T(8,128)(2,1)S(1)} collective-permute-done((bf16[3,54,128]{2,1,0:T(8,128)(2,1)S(1)}, bf16[3,54,128]{2,1,0:T(8,128)(2,1)S(1)}, u32[]{:S(2)}, u32[]{:S(2)}) %collective-permute-start.3) | collective-permute-done | bytes 41504 | tf_op jit(solution)/shard_map/ppermute | solution.py:158
  48.0 0.3 broadcast_in_dim.6.ocean
  48.3 0.5 copy-done
  48.8 0.0 copy-done.1
  48.9 0.1 copy-done.2
  49.0 10.8 %shard_map.119 = (bf16[32,48,128]{2,1,0:T(8,128)(2,1)}, bf16[32,48,128]{2,1,0:T(8,128)(2,1)S(1)}, bf16[576,128]{1,0:T(8,128)(2,1)S(1)}) custom-call(bf16[32,48,128]{2,1,0:T(8,128)(2,1)S(1)} %get-tuple-element.30.masked, bf16[32,3,128]{2,1,0:T(4,128)(2,1)S(1)} %collective-permute-done.west, bf16[32,3,128]{2,1,0:T(4,128)(2,1)S(1)} %collective-permute-done.1.east, ...), custom_call_target="tpu_custom_call" | custom-call | flops 500000000 | bytes 2097152 | tf_op jit(solution)/shard_map/pallas_call | solution.py:124
  59.7 0.8 reshape.37
  60.5 4.2 %all-to-all-start = ((bf16[64,9,128]{2,1,0:T(8,128)(2,1)}), bf16[64,9,128]{2,1,0:T(8,128)(2,1)S(1)}, u32[]{:S(2)}, u32[]{:S(2)}) async-start(bf16[64,9,128]{2,1,0:T(8,128)(2,1)} %reshape.37), calls=%async_computation | async-start | bytes 524288 | tf_op jit(solution)/shard_map/all_to_all | solution.py:165
  64.8 6.9 %collective-permute-start.5 = (bf16[32,3,128]{2,1,0:T(4,128)(2,1)S(1)}, bf16[32,3,128]{2,1,0:T(4,128)(2,1)S(1)}, u32[]{:S(2)}, u32[]{:S(2)}) collective-permute-start(bf16[32,3,128]{2,1,0:T(4,128)(2,1)S(1)} %get-tuple-element.13), channel_id=1, source_target_pairs={{8,0},{16,8},{24,16},{32,24},{40,32},{48,40},{56,48},{64,56},{72,6... | collective-permute-start | bytes 73736 | tf_op jit(solution)/shard_map/ppermute | solution.py:154
  71.7 1.9 %collective-permute-start.4 = (bf16[32,3,128]{2,1,0:T(4,128)(2,1)S(1)}, bf16[32,3,128]{2,1,0:T(4,128)(2,1)S(1)}, u32[]{:S(2)}, u32[]{:S(2)}) collective-permute-start(bf16[32,3,128]{2,1,0:T(4,128)(2,1)S(1)} %get-tuple-element.14), channel_id=1, source_target_pairs={{0,8},{8,16},{16,24},{24,32},{32,40},{40,48},{48,56},{56,64},{64,7... | collective-permute-start | bytes 73736 | tf_op jit(solution)/shard_map/ppermute | solution.py:153
  73.6 1.6 %all-to-all-done = bf16[64,9,128]{2,1,0:T(8,128)(2,1)S(1)} async-done(((bf16[64,9,128]{2,1,0:T(8,128)(2,1)}), bf16[64,9,128]{2,1,0:T(8,128)(2,1)S(1)}, u32[]{:S(2)}, u32[]{:S(2)}) %all-to-all-start) | async-done | bytes 147488 | tf_op jit(solution)/shard_map/all_to_all | solution.py:165
  75.2 0.1 convert_reduce_fusion
  75.3 0.7 broadcast_in_dim.7
  76.0 3.5 %all-to-all-start.1 = ((f32[12,9,128]{2,1,0:T(8,128)}), f32[12,9,128]{2,1,0:T(8,128)S(1)}, u32[]{:S(2)}, u32[]{:S(2)}) async-start(f32[12,9,128]{2,1,0:T(8,128)} %broadcast_in_dim.7), calls=%async_computation.1 | async-start | bytes 196608 | tf_op jit(solution)/shard_map/all_to_all | solution.py:169
  79.5 10.4 %all-to-all-done.1 = f32[12,9,128]{2,1,0:T(8,128)S(1)} async-done(((f32[12,9,128]{2,1,0:T(8,128)}), f32[12,9,128]{2,1,0:T(8,128)S(1)}, u32[]{:S(2)}, u32[]{:S(2)}) %all-to-all-start.1) | async-done | bytes 55328 | tf_op jit(solution)/shard_map/all_to_all | solution.py:169
  89.9 0.8 broadcast_in_dim.8
  90.7 10.7 %all-to-all-start.2 = ((bf16[64,9,128]{2,1,0:T(8,128)(2,1)}), bf16[64,9,128]{2,1,0:T(8,128)(2,1)S(1)}, u32[]{:S(2)}, u32[]{:S(2)}) async-start(bf16[64,9,128]{2,1,0:T(8,128)(2,1)} %broadcast_in_dim.8), calls=%async_computation.2 | async-start | bytes 524288 | tf_op jit(solution)/shard_map/all_to_all | solution.py:171
  101.4 3.5 %collective-permute-start.6 = (bf16[3,54,128]{2,1,0:T(8,128)(2,1)S(1)}, bf16[3,54,128]{2,1,0:T(8,128)(2,1)S(1)}, u32[]{:S(2)}, u32[]{:S(2)}) collective-permute-start(bf16[3,54,128]{2,1,0:T(8,128)(2,1)S(1)} %pad_maximum_fusion.3), channel_id=1, source_target_pairs={{0,1},{1,2},{2,3},{3,4},{4,5},{5,6},{6,7},{8,9},{9,10},{10,11},{11... | collective-permute-start | bytes 124424 | tf_op jit(solution)/shard_map/ppermute | solution.py:157
  105.0 1.9 %collective-permute-start.7 = (bf16[3,54,128]{2,1,0:T(8,128)(2,1)S(1)}, bf16[3,54,128]{2,1,0:T(8,128)(2,1)S(1)}, u32[]{:S(2)}, u32[]{:S(2)}) collective-permute-start(bf16[3,54,128]{2,1,0:T(8,128)(2,1)S(1)} %pad_maximum_fusion.4), channel_id=1, source_target_pairs={{1,0},{2,1},{3,2},{4,3},{5,4},{6,5},{7,6},{9,8},{10,9},{11,10},{12... | collective-permute-start | bytes 124424 | tf_op jit(solution)/shard_map/ppermute | solution.py:158
  106.9 3.7 %collective-permute-done.7.south = bf16[3,54,128]{2,1,0:T(8,128)(2,1)S(1)} collective-permute-done((bf16[3,54,128]{2,1,0:T(8,128)(2,1)S(1)}, bf16[3,54,128]{2,1,0:T(8,128)(2,1)S(1)}, u32[]{:S(2)}, u32[]{:S(2)}) %collective-permute-start.7) | collective-permute-done | bytes 41504 | tf_op jit(solution)/shard_map/ppermute | solution.py:158
  110.6 3.5 %shard_map.120 = bf16[32,48,128]{2,1,0:T(8,128)(2,1)} custom-call(bf16[32,48,128]{2,1,0:T(8,128)(2,1)S(1)} %get-tuple-element.9.dz, bf16[32,3,128]{2,1,0:T(4,128)(2,1)S(1)} %collective-permute-done.4.west, bf16[32,3,128]{2,1,0:T(4,128)(2,1)S(1)} %collective-permute-done.5.east, bf16[3,54,128]{2,1,0:T(8,128)(2,1)S(1)} %collective-permute-done.6.north, ...), custom_call_target="tpu_custom_call" | custom-call | flops 20000000 | bytes 2097152 | tf_op jit(solution)/shard_map/pallas_call | solution.py:124
  114.2 0.7 slice.95
  114.9 0.6 reshape.38
  115.5 0.7 pad_maximum_fusion
  (30 shorter events, 0.3 us)
Async XLA Ops:
  2.8 24.5 %collective-permute-start.1 = (bf16[32,3,128]{2,1,0:T(4,128)(2,1)S(1)}, bf16[32,3,128]{2,1,0:T(4,128)(2,1)S(1)}, u32[]{:S(2)}, u32[]{:S(2)}) collective-permute-start(bf16[32,3,128]{2,1,0:T(4,128)(2,1)S(1)} %get-tuple-element.17), channel_id=1, source_target_pairs={{8,0},{16,8},{24,16},{32,24},{40,32},{48,40},{56,48},{64,56},{72,6... | collective-permute-start | bytes 73736 | tf_op jit(solution)/shard_map/ppermute | solution.py:154
  25.4 13.0 %collective-permute-start = (bf16[32,3,128]{2,1,0:T(4,128)(2,1)S(1)}, bf16[32,3,128]{2,1,0:T(4,128)(2,1)S(1)}, u32[]{:S(2)}, u32[]{:S(2)}) collective-permute-start(bf16[32,3,128]{2,1,0:T(4,128)(2,1)S(1)} %get-tuple-element.18), channel_id=1, source_target_pairs={{0,8},{8,16},{16,24},{24,32},{32,40},{40,48},{48,56},{56,64},{64,7... | collective-permute-start | bytes 73736 | tf_op jit(solution)/shard_map/ppermute | solution.py:153
  38.4 6.2 %collective-permute-start.2 = (bf16[3,54,128]{2,1,0:T(8,128)(2,1)S(1)}, bf16[3,54,128]{2,1,0:T(8,128)(2,1)S(1)}, u32[]{:S(2)}, u32[]{:S(2)}) collective-permute-start(bf16[3,54,128]{2,1,0:T(8,128)(2,1)S(1)} %pad_maximum_fusion.1), channel_id=1, source_target_pairs={{0,1},{1,2},{2,3},{3,4},{4,5},{5,6},{6,7},{8,9},{9,10},{10,11},{11... | collective-permute-start | bytes 124424 | tf_op jit(solution)/shard_map/ppermute | solution.py:157
  42.6 2.0 %copy-start.4 = (f32[7,7,128]{2,1,0:T(8,128)S(1)}, f32[7,7,128]{2,1,0:T(8,128)}, u32[]{:S(2)}) copy-start(f32[7,7,128]{2,1,0:T(8,128)} %param.11) | copy-start | bytes 75268
  42.7 5.3 %collective-permute-start.3 = (bf16[3,54,128]{2,1,0:T(8,128)(2,1)S(1)}, bf16[3,54,128]{2,1,0:T(8,128)(2,1)S(1)}, u32[]{:S(2)}, u32[]{:S(2)}) collective-permute-start(bf16[3,54,128]{2,1,0:T(8,128)(2,1)S(1)} %pad_maximum_fusion.2), channel_id=1, source_target_pairs={{1,0},{2,1},{3,2},{4,3},{5,4},{6,5},{7,6},{9,8},{10,9},{11,10},{12... | collective-permute-start | bytes 124424 | tf_op jit(solution)/shard_map/ppermute | solution.py:158
  48.0 0.8 copy-start
  48.0 0.9 copy-start.1
  48.3 0.7 copy-start.2
  48.3 0.7 copy-start.3
  60.5 14.7 %all-to-all-start = ((bf16[64,9,128]{2,1,0:T(8,128)(2,1)}), bf16[64,9,128]{2,1,0:T(8,128)(2,1)S(1)}, u32[]{:S(2)}, u32[]{:S(2)}) async-start(bf16[64,9,128]{2,1,0:T(8,128)(2,1)} %reshape.37), calls=%async_computation | async-start | bytes 524288 | tf_op jit(solution)/shard_map/all_to_all | solution.py:165
  64.8 14.7 %collective-permute-start.5 = (bf16[32,3,128]{2,1,0:T(4,128)(2,1)S(1)}, bf16[32,3,128]{2,1,0:T(4,128)(2,1)S(1)}, u32[]{:S(2)}, u32[]{:S(2)}) collective-permute-start(bf16[32,3,128]{2,1,0:T(4,128)(2,1)S(1)} %get-tuple-element.13), channel_id=1, source_target_pairs={{8,0},{16,8},{24,16},{32,24},{40,32},{48,40},{56,48},{64,56},{72,6... | collective-permute-start | bytes 73736 | tf_op jit(solution)/shard_map/ppermute | solution.py:154
  71.7 29.7 %collective-permute-start.4 = (bf16[32,3,128]{2,1,0:T(4,128)(2,1)S(1)}, bf16[32,3,128]{2,1,0:T(4,128)(2,1)S(1)}, u32[]{:S(2)}, u32[]{:S(2)}) collective-permute-start(bf16[32,3,128]{2,1,0:T(4,128)(2,1)S(1)} %get-tuple-element.14), channel_id=1, source_target_pairs={{0,8},{8,16},{16,24},{24,32},{32,40},{40,48},{48,56},{56,64},{64,7... | collective-permute-start | bytes 73736 | tf_op jit(solution)/shard_map/ppermute | solution.py:153
  76.0 13.9 %all-to-all-start.1 = ((f32[12,9,128]{2,1,0:T(8,128)}), f32[12,9,128]{2,1,0:T(8,128)S(1)}, u32[]{:S(2)}, u32[]{:S(2)}) async-start(f32[12,9,128]{2,1,0:T(8,128)} %broadcast_in_dim.7), calls=%async_computation.1 | async-start | bytes 196608 | tf_op jit(solution)/shard_map/all_to_all | solution.py:169
  90.7 23.4 %all-to-all-start.2 = ((bf16[64,9,128]{2,1,0:T(8,128)(2,1)}), bf16[64,9,128]{2,1,0:T(8,128)(2,1)S(1)}, u32[]{:S(2)}, u32[]{:S(2)}) async-start(bf16[64,9,128]{2,1,0:T(8,128)(2,1)} %broadcast_in_dim.8), calls=%async_computation.2 | async-start | bytes 524288 | tf_op jit(solution)/shard_map/all_to_all | solution.py:171
  101.4 5.5 %collective-permute-start.6 = (bf16[3,54,128]{2,1,0:T(8,128)(2,1)S(1)}, bf16[3,54,128]{2,1,0:T(8,128)(2,1)S(1)}, u32[]{:S(2)}, u32[]{:S(2)}) collective-permute-start(bf16[3,54,128]{2,1,0:T(8,128)(2,1)S(1)} %pad_maximum_fusion.3), channel_id=1, source_target_pairs={{0,1},{1,2},{2,3},{3,4},{4,5},{5,6},{6,7},{8,9},{9,10},{10,11},{11... | collective-permute-start | bytes 124424 | tf_op jit(solution)/shard_map/ppermute | solution.py:157
  105.0 5.6 %collective-permute-start.7 = (bf16[3,54,128]{2,1,0:T(8,128)(2,1)S(1)}, bf16[3,54,128]{2,1,0:T(8,128)(2,1)S(1)}, u32[]{:S(2)}, u32[]{:S(2)}) collective-permute-start(bf16[3,54,128]{2,1,0:T(8,128)(2,1)S(1)} %pad_maximum_fusion.4), channel_id=1, source_target_pairs={{1,0},{2,1},{3,2},{4,3},{5,4},{6,5},{7,6},{9,8},{10,9},{11,10},{12... | collective-permute-start | bytes 124424 | tf_op jit(solution)/shard_map/ppermute | solution.py:158

commit v3 on v2

v3 whole, which is shorter than its diff:
```python
import functools

import jax
import jax.numpy as jnp
from jax import lax
from jax.experimental import pallas as pl
from jax.experimental.pallas import tpu as pltpu
from jax.sharding import Mesh
from jax.sharding import PartitionSpec as P

LINK = jnp.bfloat16
LON = ("x", "yh", "z")
LAT = ("yl", "core")
OUTER = ("x", "yh", "yl", "core")
INNER = ("z",)
ROWS = 32
COLS = 48
C = 128
FF = 256
TERM_ROWS = 576


INSIDE = ((8, 32),)
STRIPS = ((0, 8), (40, 8))


def fill_rows(pad, own, flags, halo_a, halo_b, first, last, at):
    f32 = jnp.float32
    even = flags[0] == 0
    pad[3 : 3 + ROWS, at : at + last - first, :] = own[:, first:last, :].astype(f32)
    from_a = halo_a[:, first:last, :].astype(f32)
    from_b = halo_b[:, first:last, :].astype(f32)
    pad[0:3, at : at + last - first, :] = jnp.where(even, from_b, from_a)
    pad[3 + ROWS : 6 + ROWS, at : at + last - first, :] = jnp.where(even, from_a, from_b)


def fill_strips(left, right, own, flags, lat_a, lat_b, lon_a, lon_b):
    f32 = jnp.float32
    even = flags[1] == 0
    fill_rows(left, own, flags, lat_a, lat_b, 0, 16, 8)
    fill_rows(right, own, flags, lat_a, lat_b, 32, 48, 0)
    from_a, from_b = lon_a[...].astype(f32), lon_b[...].astype(f32)
    left[:, 5:8, :] = jnp.where(even, from_b, from_a)
    right[:, 16:19, :] = jnp.where(even, from_a, from_b)


def conv_rows(pads, taps, first, step, flip):
    sums = [[jnp.zeros((width, C), jnp.float32) for _, _, width in pads] for _ in range(step)]
    for row in range(step + 6):
        for col in range(7):
            for seg, (pad, start, width) in enumerate(pads):
                cells = pad[first + row, start + col : start + col + width, :]
                for out in range(step):
                    tap = row - out
                    if 0 <= tap < 7:
                        at = tap * 7 + col
                        at = 48 - at if flip else at
                        sums[out][seg] = sums[out][seg] + cells * taps[at : at + 1, :]
    return jnp.concatenate([part for line in sums for part in line], axis=0)


def read_cells(ref, first, step, segs):
    return jnp.concatenate(
        [ref[first + row, c : c + w, :].astype(jnp.float32) for row in range(step) for c, w in segs], axis=0
    )


def write_cells(ref, first, step, segs, values):
    at = 0
    for row in range(step):
        for c, w in segs:
            ref[first + row, c : c + w, :] = values[at : at + w].astype(jnp.bfloat16)
            at += w


def main_rows(step, segs, pads, masked, gmask, ocean, params, advanced, dz_out, sums, index):
    f32, bf16 = jnp.float32, jnp.bfloat16
    taps, gain, w_in, b_in, w_out = params
    acc_in, acc_out, acc_tap = sums
    first = index * step
    z = conv_rows(pads, taps, first, step, False)
    grad = read_cells(gmask, first, step, segs).astype(bf16)
    average = jnp.mean(z, axis=-1, keepdims=True)
    centre = z - average
    inverse = lax.rsqrt(jnp.mean(centre * centre, axis=-1, keepdims=True) + 1e-06)
    unit = centre * inverse
    normed = (unit * gain[...]).astype(bf16)
    preact = jnp.dot(normed, w_in[...], preferred_element_type=f32) + b_in[...]
    cdf = 0.5 * (1.0 + lax.erf(preact * 0.7071067811865476))
    hidden = (preact * cdf).astype(bf16)
    out = jnp.dot(hidden, w_out[...], preferred_element_type=f32)
    d_hidden = lax.dot_general(grad, w_out[...], (((1,), (1,)), ((), ())), preferred_element_type=f32)
    slopes = cdf + preact * jnp.exp(-0.5 * preact * preact) * 0.3989422804014327
    d_pre = (d_hidden * slopes).astype(bf16)
    contract = (((0,), (0,)), ((), ()))
    acc_out[...] += lax.dot_general(grad, hidden, contract, preferred_element_type=f32)
    acc_in[...] += lax.dot_general(normed, d_pre, contract, preferred_element_type=f32)
    d_norm = lax.dot_general(d_pre, w_in[...], (((1,), (1,)), ((), ())), preferred_element_type=f32)
    scaled = d_norm * gain[...]
    dz = inverse * (
        scaled
        - jnp.mean(scaled, axis=-1, keepdims=True)
        - unit * jnp.mean(scaled * unit, axis=-1, keepdims=True)
    )
    write_cells(dz_out, first, step, segs, dz)
    own = read_cells(masked, first, step, segs)
    keep = read_cells(ocean, first, step, segs)
    write_cells(advanced, first, step, segs, own + keep * out)
    grads = dz.astype(bf16).astype(f32)
    per_row = sum(w for _, w in segs)
    for tap in range(7):
        for col in range(7):
            total = None
            for row in range(step):
                at = row * per_row
                for pad, start, width in pads:
                    cells = pad[first + row + tap, start + col : start + col + width, :]
                    product = cells * grads[at : at + width]
                    at += width
                    for part in range(0, width, 8):
                        piece = product[part : part + 8]
                        total = piece if total is None else total + piece
            acc_tap[tap * 7 + col] += total


def inside_kernel(
    flags, masked, lat_a, lat_b, gmask, ocean, taps, gain, w_in, b_in, w_out,
    advanced, dz_out, acc_in, acc_out, acc_tap, pad,
):
    fill_rows(pad, masked, flags, lat_a, lat_b, 0, COLS, 0)
    for acc in (acc_in, acc_out, acc_tap):
        acc[...] = jnp.zeros_like(acc)
    params = (taps, gain, w_in, b_in, w_out)

    def block(index, carry):
        main_rows(4, INSIDE, ((pad, 5, 32),), masked, gmask, ocean, params, advanced, dz_out, (acc_in, acc_out, acc_tap), index)
        return carry

    lax.fori_loop(0, ROWS // 4, block, 0)


def strips_kernel(
    flags, masked, lat_a, lat_b, lon_a, lon_b, gmask, ocean, taps, gain, w_in, b_in, w_out,
    had_advanced, had_dz, had_in, had_out, had_tap,
    advanced, dz_out, terms, left, right, acc_in, acc_out, acc_tap, lines,
):
    fill_strips(left, right, masked, flags, lat_a, lat_b, lon_a, lon_b)
    advanced[:, 8:40, :] = had_advanced[:, 8:40, :]
    dz_out[:, 8:40, :] = had_dz[:, 8:40, :]
    acc_in[...] = had_in[...]
    acc_out[...] = had_out[...]
    acc_tap[...] = had_tap[...]
    params = (taps, gain, w_in, b_in, w_out)

    def block(index, carry):
        main_rows(8, STRIPS, ((left, 5, 8), (right, 5, 8)), masked, gmask, ocean, params, advanced, dz_out, (acc_in, acc_out, acc_tap), index)
        return carry

    lax.fori_loop(0, ROWS // 8, block, 0)
    lines[0:C, :] = acc_in[:, 0:C]
    lines[C : 2 * C, :] = acc_in[:, C:]
    lines[2 * C : 2 * C + FF, :] = acc_out[...].T
    lines[512:561, :] = jnp.sum(acc_tap[...], axis=1)
    lines[561:576, :] = jnp.zeros((15, C), jnp.float32)
    chunk = terms.shape[1]
    for part in range(terms.shape[0]):
        terms[part] = lines[part * chunk : (part + 1) * chunk, :].astype(LINK)


def back_inside_kernel(flags, dz, lat_a, lat_b, gmask, ocean, taps, field_grad, pad):
    fill_rows(pad, dz, flags, lat_a, lat_b, 0, COLS, 0)

    def block(index, carry):
        back_rows(4, INSIDE, ((pad, 5, 32),), gmask, ocean, taps, field_grad, index)
        return carry

    lax.fori_loop(0, ROWS // 4, block, 0)


def back_strips_kernel(
    flags, dz, lat_a, lat_b, lon_a, lon_b, gmask, ocean, taps, had, field_grad, left, right
):
    fill_strips(left, right, dz, flags, lat_a, lat_b, lon_a, lon_b)
    field_grad[:, 8:40, :] = had[:, 8:40, :]

    def block(index, carry):
        back_rows(8, STRIPS, ((left, 5, 8), (right, 5, 8)), gmask, ocean, taps, field_grad, index)
        return carry

    lax.fori_loop(0, ROWS // 8, block, 0)


def back_rows(step, segs, pads, gmask, ocean, taps, field_grad, index):
    first = index * step
    back = conv_rows(pads, taps, first, step, True)
    own = read_cells(gmask, first, step, segs)
    keep = read_cells(ocean, first, step, segs)
    write_cells(field_grad, first, step, segs, own + keep * back)


def final_kernel(parts, kernel_grad, w_in_grad, w_out_grad, lines, *, factor):
    chunk = parts.shape[1]
    for part in range(parts.shape[0]):
        lines[part * chunk : (part + 1) * chunk, :] = parts[part].astype(jnp.float32) * factor
    w_in_grad[:, 0:C] = lines[0:C, :]
    w_in_grad[:, C:] = lines[C : 2 * C, :]
    w_out_grad[...] = lines[2 * C : 2 * C + FF, :]
    kernel_grad[...] = lines[512:561, :]


def call(body, args, outs, scratch, flops):
    vmem = pl.BlockSpec(memory_space=pltpu.VMEM)
    smem = pl.BlockSpec(memory_space=pltpu.SMEM)
    return pl.pallas_call(
        body,
        out_shape=outs,
        in_specs=[smem if a.dtype == jnp.int32 else vmem for a in args],
        out_specs=[vmem] * len(outs),
        scratch_shapes=scratch,
        compiler_params=pltpu.CompilerParams(vmem_limit_bytes=40 << 20),
        cost_estimate=pl.CostEstimate(flops=flops, bytes_accessed=2 << 20, transcendentals=1 << 19),
    )(*args)


def kind(*shape, dtype=jnp.float32):
    return jax.ShapeDtypeStruct(shape, dtype)


CELLS = kind(ROWS, COLS, C, dtype=jnp.bfloat16)
WIDE = pltpu.VMEM((ROWS + 6, COLS, C), jnp.float32)
NARROW = pltpu.VMEM((ROWS + 6, 24, C), jnp.float32)
SUMS = ((C, FF), (C, FF), (49, 8, C))


def group_size(axes):
    size = 1
    for axis in axes:
        size *= lax.axis_size(axis)
    return size


def exchange(low, high, axes, count, wraps):
    even = lax.axis_index(axes[-1]) % 2 == 0
    joins = [i for i in range(1, count, 2) if wraps or i + 1 < count]
    pairs_b = [(i, (i + 1) % count) for i in joins] + [((i + 1) % count, i) for i in joins]
    pairs_a = [(i, i + 1) for i in range(0, count, 2)] + [(i + 1, i) for i in range(0, count, 2)]
    from_b = lax.ppermute(jnp.where(even, low, high), axes, pairs_b)
    from_a = lax.ppermute(jnp.where(even, high, low), axes, pairs_a)
    return from_a, from_b


def lat_halo(top, bottom):
    return exchange(top, bottom, LAT, group_size(LAT), False)


def lon_halo(head, tail, lat_a, lat_b):
    even = lax.axis_index(LAT[-1]) % 2 == 0
    north = jnp.where(even, lat_b, lat_a)
    south = jnp.where(even, lat_a, lat_b)
    head = jnp.concatenate([north[:, :3], head, south[:, :3]])
    tail = jnp.concatenate([north[:, COLS - 3 :], tail, south[:, COLS - 3 :]])
    return exchange(head, tail, LON, group_size(LON), True)


def grid_sum(parts):
    size, chunk, _ = parts.shape
    parts = lax.all_to_all(parts, OUTER, 0, 0, tiled=True)
    own = jnp.sum(parts.astype(jnp.float32), axis=0)
    count = group_size(INNER)
    copies = jnp.broadcast_to(own[None], (count, chunk, C))
    total = jnp.sum(lax.all_to_all(copies, INNER, 0, 0, tiled=True), axis=0)
    spread = jnp.broadcast_to(total.astype(LINK)[None], (size, chunk, C))
    return lax.all_to_all(spread, OUTER, 0, 0, tiled=True)


def shards(fields, ocean, cotangent, kernel, ln_gain, w_in, b_in, w_out):
    flags = jnp.stack([lax.axis_index(LAT[-1]) % 2, lax.axis_index(LON[-1]) % 2]).astype(jnp.int32)
    taps = kernel.reshape(49, C)
    params = (taps, ln_gain.reshape(1, C), w_in, b_in.reshape(1, FF), w_out)

    def edge(rows, cols):
        return fields[rows, cols] * ocean[rows, cols].astype(jnp.bfloat16)[..., None]

    every = slice(None)
    top, bottom = edge(slice(0, 3), every), edge(slice(ROWS - 3, ROWS), every)
    head, tail = edge(every, slice(0, 3)), edge(every, slice(COLS - 3, COLS))
    lat = lat_halo(top, bottom)
    lon = lon_halo(head, tail, *lat)
    ocean_b = jnp.broadcast_to(ocean.astype(jnp.bfloat16)[..., None], fields.shape)
    masked = fields * ocean_b
    gmask = cotangent * ocean_b
    scratch = [pltpu.VMEM(shape, jnp.float32) for shape in SUMS]
    inside = call(
        inside_kernel,
        (flags, masked, *lat, gmask, ocean_b, *params),
        [CELLS, CELLS, *(kind(*shape) for shape in SUMS)],
        [WIDE],
        350_000_000,
    )
    parts = group_size(OUTER)
    advanced, dz, terms = call(
        strips_kernel,
        (flags, masked, *lat, *lon, gmask, ocean_b, *params, *inside),
        [CELLS, CELLS, kind(parts, TERM_ROWS // parts, C, dtype=LINK)],
        [NARROW, NARROW, *scratch, pltpu.VMEM((TERM_ROWS, C), jnp.float32)],
        170_000_000,
    )
    sums = grid_sum(terms)
    lat = lat_halo(dz[:3], dz[ROWS - 3 :])
    lon = lon_halo(dz[:, :3], dz[:, COLS - 3 :], *lat)
    (field_grad,) = call(
        back_inside_kernel, (flags, dz, *lat, gmask, ocean_b, taps), [CELLS], [WIDE], 100_000_000
    )
    (field_grad,) = call(
        back_strips_kernel,
        (flags, dz, *lat, *lon, gmask, ocean_b, taps, field_grad),
        [CELLS],
        [NARROW, NARROW],
        50_000_000,
    )
    cells = ROWS * COLS * group_size(LAT) * group_size(LON)
    kernel_grad, w_in_grad, w_out_grad = call(
        functools.partial(final_kernel, factor=cells**-0.5),
        (sums,),
        [kind(49, C), kind(C, FF), kind(FF, C)],
        [pltpu.VMEM((TERM_ROWS, C), jnp.float32)],
        1_000_000,
    )
    return (advanced, field_grad, kernel_grad.reshape(7, 7, C), w_in_grad, w_out_grad)


def solution(mesh):
    torus = Mesh(mesh.devices.reshape(4, 2, 12, 4, 2), LON + LAT)
    cells = P(LAT, LON, None)
    in_specs = (cells, P(LAT, LON), cells, P(), P(), P(), P(), P())
    out_specs = (cells, cells, P(), P(), P())
    return jax.shard_map(shards, mesh=torus, in_specs=in_specs, out_specs=out_specs, check_vma=False)
```

time: 117 us -> 109 us (0.932)
  waiting for transfers between devices: 30.1 us -> 17 us
  Pallas kernels: 14.3 us -> 20.1 us
    ppermute x8, waiting for transfers between devices: 18.1 us -> 3.4 us  [the longest x4 2.96 us: exchange(): from_b = lax.ppermute(jnp.where(even, low, high), axes, pairs_b)]
    pallas_call x2 -> x5, Pallas kernels: 14.3 us -> 20.1 us  [call(): pl.pallas_call(body, out_shape=outs, in_specs=[smem if a.dtype == jnp.int...]
    all_to_all x2, waiting for transfers between devices: 1.6 us -> 3.52 us  [the longest x1 3.52 us: grid_sum(): parts = lax.all_to_all(parts, OUTER, 0, 0, tiled=True)]
    all_to_all x2, starting transfers between devices: 14.9 us -> 13 us  [the longest x1 8.14 us: grid_sum(): return lax.all_to_all(spread, OUTER, 0, 0, tiled=True)]
  transfers between devices with their start and end apart: 11 -> 11, of which waited for: 5 -> 4; matrix products, arithmetic and copies ran while one was open for 1% -> 3% of each run, Pallas kernels for 3% -> 12%
where the time goes in v3:
time: 109 us; the launch traced here: 108 us
  starting transfers between devices  62.6 us (57%)
  Pallas kernels  20.1 us (18%)
  waiting for transfers between devices  17 us (16%)
  local copies, waits for them, and re-layouts  3.81 us (3%)
  other arithmetic  3.64 us (3%)
    ppermute x4, starting transfers between devices, exchange(): from_b = lax.ppermute(jnp.where(even, low, high), axes, pairs_b)  31.7 us
    pallas_call x5, Pallas kernels, call(): pl.pallas_call(body, out_shape=outs, in_specs=[smem if a.dtype == jnp.int...  20.1 us
    ppermute x4, starting transfers between devices, exchange(): from_a = lax.ppermute(jnp.where(even, high, low), axes, pairs_a)  14.3 us
    all_to_all x1, waiting for transfers between devices, grid_sum(): total = jnp.sum(lax.all_to_all(copies, INNER, 0, 0, tiled=True), axis=0)  10.1 us
    all_to_all x1, starting transfers between devices, grid_sum(): return lax.all_to_all(spread, OUTER, 0, 0, tiled=True)  8.14 us
    all_to_all x1, starting transfers between devices, grid_sum(): parts = lax.all_to_all(parts, OUTER, 0, 0, tiled=True)  4.83 us
    all_to_all x1, starting transfers between devices, grid_sum(): total = jnp.sum(lax.all_to_all(copies, INNER, 0, 0, tiled=True), axis=0)  3.68 us
    all_to_all x1, waiting for transfers between devices, grid_sum(): parts = lax.all_to_all(parts, OUTER, 0, 0, tiled=True)  3.52 us
  transfers between devices with their start and end apart: 11, of which 4 were waited for; matrix products, arithmetic and copies ran while one was open for 3% of the time, Pallas kernels for 12%

profile of v3, /device:TPU:1, one launch (start us, length us, event | category | flops | bytes accessed | tf_op | source)
XLA Modules:
  0.0 108.1 jit_solution(3353850024713509609)
XLA Ops:
  0.7 0.7 copy-done.5
  1.4 0.9 broadcast_select_fusion.10
  2.3 4.6 %collective-permute-start.1 = (bf16[3,48,128]{2,1,0:T(8,128)(2,1)S(1)}, bf16[3,48,128]{2,1,0:T(8,128)(2,1)S(1)}, u32[]{:S(2)}, u32[]{:S(2)}) collective-permute-start(bf16[3,48,128]{2,1,0:T(8,128)(2,1)S(1)} %get-tuple-element.27), channel_id=1, source_target_pairs={{1,2},{3,4},{5,6},{2,1},{4,3},{6,5},{9,10},{11,12},{13,14},{10,9},... | collective-permute-start | bytes 110600 | tf_op jit(solution)/shard_map/ppermute | solution.py:247
  6.9 8.5 %collective-permute-start = (bf16[3,48,128]{2,1,0:T(8,128)(2,1)S(1)}, bf16[3,48,128]{2,1,0:T(8,128)(2,1)S(1)}, u32[]{:S(2)}, u32[]{:S(2)}) collective-permute-start(bf16[3,48,128]{2,1,0:T(8,128)(2,1)S(1)} %get-tuple-element.28), channel_id=1, source_target_pairs={{0,1},{2,3},{4,5},{6,7},{1,0},{3,2},{5,4},{7,6},{8,9},{10,11},{12,... | collective-permute-start | bytes 110600 | tf_op jit(solution)/shard_map/ppermute | solution.py:248
  15.5 1.4 %broadcast_multiply_fusion = (bf16[32,48,128]{2,1,0:T(8,128)(2,1)S(1)}, bf16[32,48,128]{2,1,0:T(8,128)(2,1)S(1)}) fusion(bf16[32,48,128]{2,1,0:T(8,128)(2,1)} %param.10, bf16[32,48]{1,0:T(8,128)(2,1)S(1)} %convert_element_type.17, bf16[32,48,128]{2,1,0:T(8,128)(2,1)} %param.8), kind=kLoop, calls=%fused_computation.1 | loop fusion | flops 393216 | bytes 1575936 | tf_op jit(solution)/shard_map/mul | solution.py:291
  16.9 1.0 slice_multiply_fusion.3
  17.9 0.1 pad_add_fusion.flags
  18.1 14.3 %collective-permute-start.3 = (bf16[38,3,128]{2,1,0:T(4,128)(2,1)S(1)}, bf16[38,3,128]{2,1,0:T(4,128)(2,1)S(1)}, u32[]{:S(2)}, u32[]{:S(2)}) collective-permute-start(bf16[38,3,128]{2,1,0:T(4,128)(2,1)S(1)} %get-tuple-element.37), channel_id=1, source_target_pairs={{8,16},{24,32},{40,48},{56,64},{72,80},{88,96},{104,112},{120,128}... | collective-permute-start | bytes 87560 | tf_op jit(solution)/shard_map/ppermute | solution.py:247
  32.4 1.9 %collective-permute-start.2 = (bf16[38,3,128]{2,1,0:T(4,128)(2,1)S(1)}, bf16[38,3,128]{2,1,0:T(4,128)(2,1)S(1)}, u32[]{:S(2)}, u32[]{:S(2)}) collective-permute-start(bf16[38,3,128]{2,1,0:T(4,128)(2,1)S(1)} %get-tuple-element.38), channel_id=1, source_target_pairs={{0,8},{16,24},{32,40},{48,56},{64,72},{80,88},{96,104},{112,120},{... | collective-permute-start | bytes 87560 | tf_op jit(solution)/shard_map/ppermute | solution.py:248
  34.3 0.3 broadcast_in_dim.6.ocean
  34.6 0.5 copy-done
  35.2 0.1 copy-done.2
  35.3 8.6 %shard_map.119 = (bf16[32,48,128]{2,1,0:T(8,128)(2,1)S(1)}, bf16[32,48,128]{2,1,0:T(8,128)(2,1)S(1)}, f32[128,256]{1,0:T(8,128)S(1)}, f32[128,256]{1,0:T(8,128)S(1)}, f32[49,8,128]{2,1,0:T(8,128)S(1)}) custom-call(s32[2]{0:T(128)S(1)} %pad_add_fusion.flags, bf16[32,48,128]{2,1,0:T(8,128)(2,1)S(1)} %get-tuple-element.52.masked, ...), custom_call_target="tpu_custom_call" | custom-call | flops 350000000 | bytes 2097152 | tf_op jit(solution)/shard_map/pallas_call | solution.py:214
  44.0 5.9 %shard_map.120 = (bf16[32,48,128]{2,1,0:T(8,128)(2,1)}, bf16[32,48,128]{2,1,0:T(8,128)(2,1)S(1)}, bf16[64,9,128]{2,1,0:T(8,128)(2,1)}) custom-call(s32[2]{0:T(128)S(1)} %pad_add_fusion.flags, bf16[32,48,128]{2,1,0:T(8,128)(2,1)S(1)} %get-tuple-element.52.masked, bf16[3,48,128]{2,1,0:T(8,128)(2,1)S(1)} %collective-permute-done.lat_a, ...), custom_call_target="tpu_custom_call" | custom-call | flops 170000000 | bytes 2097152 | tf_op jit(solution)/shard_map/pallas_call | solution.py:214
  49.9 4.8 %all-to-all-start = ((bf16[64,9,128]{2,1,0:T(8,128)(2,1)}), bf16[64,9,128]{2,1,0:T(8,128)(2,1)S(1)}, u32[]{:S(2)}, u32[]{:S(2)}) async-start(bf16[64,9,128]{2,1,0:T(8,128)(2,1)} %get-tuple-element.23), calls=%async_computation | async-start | bytes 524288 | tf_op jit(solution)/shard_map/all_to_all | solution.py:267
  54.7 3.5 %collective-permute-start.5 = (bf16[3,48,128]{2,1,0:T(8,128)(2,1)S(1)}, bf16[3,48,128]{2,1,0:T(8,128)(2,1)S(1)}, u32[]{:S(2)}, u32[]{:S(2)}) collective-permute-start(bf16[3,48,128]{2,1,0:T(8,128)(2,1)S(1)} %get-tuple-element.31), channel_id=1, source_target_pairs={{1,2},{3,4},{5,6},{2,1},{4,3},{6,5},{9,10},{11,12},{13,14},{10,9},... | collective-permute-start | bytes 110600 | tf_op jit(solution)/shard_map/ppermute | solution.py:247
  58.3 1.9 %collective-permute-start.4 = (bf16[3,48,128]{2,1,0:T(8,128)(2,1)S(1)}, bf16[3,48,128]{2,1,0:T(8,128)(2,1)S(1)}, u32[]{:S(2)}, u32[]{:S(2)}) collective-permute-start(bf16[3,48,128]{2,1,0:T(8,128)(2,1)S(1)} %get-tuple-element.32), channel_id=1, source_target_pairs={{0,1},{2,3},{4,5},{6,7},{1,0},{3,2},{5,4},{7,6},{8,9},{10,11},{12,... | collective-permute-start | bytes 110600 | tf_op jit(solution)/shard_map/ppermute | solution.py:248
  60.3 3.0 %collective-permute-done.5.lat_b = bf16[3,48,128]{2,1,0:T(8,128)(2,1)S(1)} collective-permute-done((bf16[3,48,128]{2,1,0:T(8,128)(2,1)S(1)}, bf16[3,48,128]{2,1,0:T(8,128)(2,1)S(1)}, u32[]{:S(2)}, u32[]{:S(2)}) %collective-permute-start.5) | collective-permute-done | bytes 36896 | tf_op jit(solution)/shard_map/ppermute | solution.py:247
  63.2 3.5 %all-to-all-done = bf16[64,9,128]{2,1,0:T(8,128)(2,1)S(1)} async-done(((bf16[64,9,128]{2,1,0:T(8,128)(2,1)}), bf16[64,9,128]{2,1,0:T(8,128)(2,1)S(1)}, u32[]{:S(2)}, u32[]{:S(2)}) %all-to-all-start) | async-done | bytes 147488 | tf_op jit(solution)/shard_map/all_to_all | solution.py:267
  66.8 0.1 convert_reduce_fusion
  66.8 0.7 broadcast_in_dim.7
  67.5 3.7 %all-to-all-start.1 = ((f32[12,9,128]{2,1,0:T(8,128)}), f32[12,9,128]{2,1,0:T(8,128)S(1)}, u32[]{:S(2)}, u32[]{:S(2)}) async-start(f32[12,9,128]{2,1,0:T(8,128)} %broadcast_in_dim.7), calls=%async_computation.1 | async-start | bytes 196608 | tf_op jit(solution)/shard_map/all_to_all | solution.py:271
  71.2 10.1 %all-to-all-done.1 = f32[12,9,128]{2,1,0:T(8,128)S(1)} async-done(((f32[12,9,128]{2,1,0:T(8,128)}), f32[12,9,128]{2,1,0:T(8,128)S(1)}, u32[]{:S(2)}, u32[]{:S(2)}) %all-to-all-start.1) | async-done | bytes 55328 | tf_op jit(solution)/shard_map/all_to_all | solution.py:271
  81.3 0.7 broadcast_in_dim.8
  82.0 8.1 %all-to-all-start.2 = ((bf16[64,9,128]{2,1,0:T(8,128)(2,1)}), bf16[64,9,128]{2,1,0:T(8,128)(2,1)S(1)}, u32[]{:S(2)}, u32[]{:S(2)}) async-start(bf16[64,9,128]{2,1,0:T(8,128)(2,1)} %broadcast_in_dim.8), calls=%async_computation.2 | async-start | bytes 524288 | tf_op jit(solution)/shard_map/all_to_all | solution.py:273
  90.3 9.3 %collective-permute-start.7 = (bf16[38,3,128]{2,1,0:T(4,128)(2,1)S(1)}, bf16[38,3,128]{2,1,0:T(4,128)(2,1)S(1)}, u32[]{:S(2)}, u32[]{:S(2)}) collective-permute-start(bf16[38,3,128]{2,1,0:T(4,128)(2,1)S(1)} %get-tuple-element.35), channel_id=1, source_target_pairs={{8,16},{24,32},{40,48},{56,64},{72,80},{88,96},{104,112},{120,128}... | collective-permute-start | bytes 87560 | tf_op jit(solution)/shard_map/ppermute | solution.py:247
  99.6 1.9 %collective-permute-start.6 = (bf16[38,3,128]{2,1,0:T(4,128)(2,1)S(1)}, bf16[38,3,128]{2,1,0:T(4,128)(2,1)S(1)}, u32[]{:S(2)}, u32[]{:S(2)}) collective-permute-start(bf16[38,3,128]{2,1,0:T(4,128)(2,1)S(1)} %get-tuple-element.36), channel_id=1, source_target_pairs={{0,8},{16,24},{32,40},{48,56},{64,72},{80,88},{96,104},{112,120},{... | collective-permute-start | bytes 87560 | tf_op jit(solution)/shard_map/ppermute | solution.py:248
  101.5 2.4 %shard_map.121.had = bf16[32,48,128]{2,1,0:T(8,128)(2,1)S(1)} custom-call(s32[2]{0:T(128)S(1)} %pad_add_fusion.flags, bf16[32,48,128]{2,1,0:T(8,128)(2,1)S(1)} %get-tuple-element.22.dz, bf16[3,48,128]{2,1,0:T(8,128)(2,1)S(1)} %collective-permute-done.4.lat_a, bf16[3,48,128]{2,1,0:T(8,128)(2,1)S(1)} %collective-permute-done.5.lat_b, ...), custom_call_target="tpu_custom_call" | custom-call | flops 100000000 | bytes 2097152 | tf_op jit(solution)/shard_map/pallas_call | solution.py:214
  103.9 0.4 collective-permute-done.6.lon_a
  104.3 2.4 %shard_map.122 = bf16[32,48,128]{2,1,0:T(8,128)(2,1)} custom-call(s32[2]{0:T(128)S(1)} %pad_add_fusion.flags, bf16[32,48,128]{2,1,0:T(8,128)(2,1)S(1)} %get-tuple-element.22.dz, bf16[3,48,128]{2,1,0:T(8,128)(2,1)S(1)} %collective-permute-done.4.lat_a, bf16[3,48,128]{2,1,0:T(8,128)(2,1)S(1)} %collective-permute-done.5.lat_b, ...), custom_call_target="tpu_custom_call" | custom-call | flops 50000000 | bytes 2097152 | tf_op jit(solution)/shard_map/pallas_call | solution.py:214
  106.7 0.8 shard_map.123
  107.5 0.6 reshape.34
  (30 shorter events, 0.4 us)
Async XLA Ops:
  0.6 0.7 copy-start.5
  2.3 15.7 %collective-permute-start.1 = (bf16[3,48,128]{2,1,0:T(8,128)(2,1)S(1)}, bf16[3,48,128]{2,1,0:T(8,128)(2,1)S(1)}, u32[]{:S(2)}, u32[]{:S(2)}) collective-permute-start(bf16[3,48,128]{2,1,0:T(8,128)(2,1)S(1)} %get-tuple-element.27), channel_id=1, source_target_pairs={{1,2},{3,4},{5,6},{2,1},{4,3},{6,5},{9,10},{11,12},{13,14},{10,9},... | collective-permute-start | bytes 110600 | tf_op jit(solution)/shard_map/ppermute | solution.py:247
  6.9 11.1 %collective-permute-start = (bf16[3,48,128]{2,1,0:T(8,128)(2,1)S(1)}, bf16[3,48,128]{2,1,0:T(8,128)(2,1)S(1)}, u32[]{:S(2)}, u32[]{:S(2)}) collective-permute-start(bf16[3,48,128]{2,1,0:T(8,128)(2,1)S(1)} %get-tuple-element.28), channel_id=1, source_target_pairs={{0,1},{2,3},{4,5},{6,7},{1,0},{3,2},{5,4},{7,6},{8,9},{10,11},{12,... | collective-permute-start | bytes 110600 | tf_op jit(solution)/shard_map/ppermute | solution.py:248
  16.9 1.1 %copy-start.4 = (f32[7,7,128]{2,1,0:T(8,128)S(1)}, f32[7,7,128]{2,1,0:T(8,128)}, u32[]{:S(2)}) copy-start(f32[7,7,128]{2,1,0:T(8,128)} %param.11) | copy-start | bytes 75268
  18.1 25.8 %collective-permute-start.3 = (bf16[38,3,128]{2,1,0:T(4,128)(2,1)S(1)}, bf16[38,3,128]{2,1,0:T(4,128)(2,1)S(1)}, u32[]{:S(2)}, u32[]{:S(2)}) collective-permute-start(bf16[38,3,128]{2,1,0:T(4,128)(2,1)S(1)} %get-tuple-element.37), channel_id=1, source_target_pairs={{8,16},{24,32},{40,48},{56,64},{72,80},{88,96},{104,112},{120,128}... | collective-permute-start | bytes 87560 | tf_op jit(solution)/shard_map/ppermute | solution.py:247
  32.4 11.6 %collective-permute-start.2 = (bf16[38,3,128]{2,1,0:T(4,128)(2,1)S(1)}, bf16[38,3,128]{2,1,0:T(4,128)(2,1)S(1)}, u32[]{:S(2)}, u32[]{:S(2)}) collective-permute-start(bf16[38,3,128]{2,1,0:T(4,128)(2,1)S(1)} %get-tuple-element.38), channel_id=1, source_target_pairs={{0,8},{16,24},{32,40},{48,56},{64,72},{80,88},{96,104},{112,120},{... | collective-permute-start | bytes 87560 | tf_op jit(solution)/shard_map/ppermute | solution.py:248
  34.3 0.8 copy-start
  34.3 0.9 copy-start.1
  34.6 0.7 copy-start.2
  34.6 0.7 copy-start.3
  49.9 16.9 %all-to-all-start = ((bf16[64,9,128]{2,1,0:T(8,128)(2,1)}), bf16[64,9,128]{2,1,0:T(8,128)(2,1)S(1)}, u32[]{:S(2)}, u32[]{:S(2)}) async-start(bf16[64,9,128]{2,1,0:T(8,128)(2,1)} %get-tuple-element.23), calls=%async_computation | async-start | bytes 524288 | tf_op jit(solution)/shard_map/all_to_all | solution.py:267
  54.7 8.5 %collective-permute-start.5 = (bf16[3,48,128]{2,1,0:T(8,128)(2,1)S(1)}, bf16[3,48,128]{2,1,0:T(8,128)(2,1)S(1)}, u32[]{:S(2)}, u32[]{:S(2)}) collective-permute-start(bf16[3,48,128]{2,1,0:T(8,128)(2,1)S(1)} %get-tuple-element.31), channel_id=1, source_target_pairs={{1,2},{3,4},{5,6},{2,1},{4,3},{6,5},{9,10},{11,12},{13,14},{10,9},... | collective-permute-start | bytes 110600 | tf_op jit(solution)/shard_map/ppermute | solution.py:247
  58.3 4.9 %collective-permute-start.4 = (bf16[3,48,128]{2,1,0:T(8,128)(2,1)S(1)}, bf16[3,48,128]{2,1,0:T(8,128)(2,1)S(1)}, u32[]{:S(2)}, u32[]{:S(2)}) collective-permute-start(bf16[3,48,128]{2,1,0:T(8,128)(2,1)S(1)} %get-tuple-element.32), channel_id=1, source_target_pairs={{0,1},{2,3},{4,5},{6,7},{1,0},{3,2},{5,4},{7,6},{8,9},{10,11},{12,... | collective-permute-start | bytes 110600 | tf_op jit(solution)/shard_map/ppermute | solution.py:248
  67.5 13.8 %all-to-all-start.1 = ((f32[12,9,128]{2,1,0:T(8,128)}), f32[12,9,128]{2,1,0:T(8,128)S(1)}, u32[]{:S(2)}, u32[]{:S(2)}) async-start(f32[12,9,128]{2,1,0:T(8,128)} %broadcast_in_dim.7), calls=%async_computation.1 | async-start | bytes 196608 | tf_op jit(solution)/shard_map/all_to_all | solution.py:271
  82.0 24.7 %all-to-all-start.2 = ((bf16[64,9,128]{2,1,0:T(8,128)(2,1)}), bf16[64,9,128]{2,1,0:T(8,128)(2,1)S(1)}, u32[]{:S(2)}, u32[]{:S(2)}) async-start(bf16[64,9,128]{2,1,0:T(8,128)(2,1)} %broadcast_in_dim.8), calls=%async_computation.2 | async-start | bytes 524288 | tf_op jit(solution)/shard_map/all_to_all | solution.py:273
  90.3 13.6 %collective-permute-start.7 = (bf16[38,3,128]{2,1,0:T(4,128)(2,1)S(1)}, bf16[38,3,128]{2,1,0:T(4,128)(2,1)S(1)}, u32[]{:S(2)}, u32[]{:S(2)}) collective-permute-start(bf16[38,3,128]{2,1,0:T(4,128)(2,1)S(1)} %get-tuple-element.35), channel_id=1, source_target_pairs={{8,16},{24,32},{40,48},{56,64},{72,80},{88,96},{104,112},{120,128}... | collective-permute-start | bytes 87560 | tf_op jit(solution)/shard_map/ppermute | solution.py:247
  99.6 4.8 %collective-permute-start.6 = (bf16[38,3,128]{2,1,0:T(4,128)(2,1)S(1)}, bf16[38,3,128]{2,1,0:T(4,128)(2,1)S(1)}, u32[]{:S(2)}, u32[]{:S(2)}) collective-permute-start(bf16[38,3,128]{2,1,0:T(4,128)(2,1)S(1)} %get-tuple-element.36), channel_id=1, source_target_pairs={{0,8},{16,24},{32,40},{48,56},{64,72},{80,88},{96,104},{112,120},{... | collective-permute-start | bytes 87560 | tf_op jit(solution)/shard_map/ppermute | solution.py:248

commit v4 on v3

--- a/solution.py
+++ b/solution.py
@@ -133,10 +133,10 @@
     params = (taps, gain, w_in, b_in, w_out)
 
     def block(index, carry):
-        main_rows(4, INSIDE, ((pad, 5, 32),), masked, gmask, ocean, params, advanced, dz_out, (acc_in, acc_out, acc_tap), index)
+        main_rows(16, INSIDE, ((pad, 5, 32),), masked, gmask, ocean, params, advanced, dz_out, (acc_in, acc_out, acc_tap), index)
         return carry
 
-    lax.fori_loop(0, ROWS // 4, block, 0)
+    lax.fori_loop(0, ROWS // 16, block, 0)
 
 
 def strips_kernel(
@@ -153,10 +153,10 @@
     params = (taps, gain, w_in, b_in, w_out)
 
     def block(index, carry):
-        main_rows(8, STRIPS, ((left, 5, 8), (right, 5, 8)), masked, gmask, ocean, params, advanced, dz_out, (acc_in, acc_out, acc_tap), index)
+        main_rows(32, STRIPS, ((left, 5, 8), (right, 5, 8)), masked, gmask, ocean, params, advanced, dz_out, (acc_in, acc_out, acc_tap), index)
         return carry
 
-    lax.fori_loop(0, ROWS // 8, block, 0)
+    lax.fori_loop(0, ROWS // 32, block, 0)
     lines[0:C, :] = acc_in[:, 0:C]
     lines[C : 2 * C, :] = acc_in[:, C:]
     lines[2 * C : 2 * C + FF, :] = acc_out[...].T
@@ -167,27 +167,23 @@
         terms[part] = lines[part * chunk : (part + 1) * chunk, :].astype(LINK)
 
 
-def back_inside_kernel(flags, dz, lat_a, lat_b, gmask, ocean, taps, field_grad, pad):
-    fill_rows(pad, dz, flags, lat_a, lat_b, 0, COLS, 0)
+def back_kernel(flags, dz, lon_a, lon_b, lat_a, lat_b, gmask, ocean, taps, field_grad, pad):
+    f32 = jnp.float32
+    even = flags[1] == 0
+    from_a, from_b = lon_a[...].astype(f32), lon_b[...].astype(f32)
+    pad[3 : 3 + ROWS, 8 : 8 + COLS, :] = dz[...].astype(f32)
+    pad[3 : 3 + ROWS, 5:8, :] = jnp.where(even, from_b, from_a)
+    pad[3 : 3 + ROWS, 8 + COLS : 11 + COLS, :] = jnp.where(even, from_a, from_b)
+    even = flags[0] == 0
+    from_a, from_b = lat_a[...].astype(f32), lat_b[...].astype(f32)
+    pad[0:3, 5 : 11 + COLS, :] = jnp.where(even, from_b, from_a)
+    pad[3 + ROWS : 6 + ROWS, 5 : 11 + COLS, :] = jnp.where(even, from_a, from_b)
 
     def block(index, carry):
-        back_rows(4, INSIDE, ((pad, 5, 32),), gmask, ocean, taps, field_grad, index)
+        back_rows(4, ((0, COLS),), ((pad, 5, COLS),), gmask, ocean, taps, field_grad, index)
         return carry
 
     lax.fori_loop(0, ROWS // 4, block, 0)
-
-
-def back_strips_kernel(
-    flags, dz, lat_a, lat_b, lon_a, lon_b, gmask, ocean, taps, had, field_grad, left, right
-):
-    fill_strips(left, right, dz, flags, lat_a, lat_b, lon_a, lon_b)
-    field_grad[:, 8:40, :] = had[:, 8:40, :]
-
-    def block(index, carry):
-        back_rows(8, STRIPS, ((left, 5, 8), (right, 5, 8)), gmask, ocean, taps, field_grad, index)
-        return carry
-
-    lax.fori_loop(0, ROWS // 8, block, 0)
 
 
 def back_rows(step, segs, pads, gmask, ocean, taps, field_grad, index):
@@ -228,6 +224,7 @@
 
 CELLS = kind(ROWS, COLS, C, dtype=jnp.bfloat16)
 WIDE = pltpu.VMEM((ROWS + 6, COLS, C), jnp.float32)
+PADDED = pltpu.VMEM((ROWS + 6, COLS + 16, C), jnp.float32)
 NARROW = pltpu.VMEM((ROWS + 6, 24, C), jnp.float32)
 SUMS = ((C, FF), (C, FF), (49, 8, C))
 
@@ -306,17 +303,16 @@
         170_000_000,
     )
     sums = grid_sum(terms)
-    lat = lat_halo(dz[:3], dz[ROWS - 3 :])
-    lon = lon_halo(dz[:, :3], dz[:, COLS - 3 :], *lat)
+    lon_a, lon_b = exchange(dz[:, :3], dz[:, COLS - 3 :], LON, group_size(LON), True)
+    even = flags[1] == 0
+    west, east = jnp.where(even, lon_b, lon_a), jnp.where(even, lon_a, lon_b)
+
+    def full(rows):
+        return jnp.concatenate([west[rows], dz[rows], east[rows]], axis=1)
+
+    lat = exchange(full(slice(0, 3)), full(slice(ROWS - 3, ROWS)), LAT, group_size(LAT), False)
     (field_grad,) = call(
-        back_inside_kernel, (flags, dz, *lat, gmask, ocean_b, taps), [CELLS], [WIDE], 100_000_000
-    )
-    (field_grad,) = call(
-        back_strips_kernel,
-        (flags, dz, *lat, *lon, gmask, ocean_b, taps, field_grad),
-        [CELLS],
-        [NARROW, NARROW],
-        50_000_000,
+        back_kernel, (flags, dz, lon_a, lon_b, *lat, gmask, ocean_b, taps), [CELLS], [PADDED], 100_000_000
     )
     cells = ROWS * COLS * group_size(LAT) * group_size(LON)
     kernel_grad, w_in_grad, w_out_grad = call(

time: 109 us -> 106 us (0.972)
  Pallas kernels: 20.1 us -> 14.8 us
  starting transfers between devices: 62.6 us -> 65.5 us
    pallas_call x5 -> x4, Pallas kernels: 20.1 us -> 14.8 us  [call(): pl.pallas_call(body, out_shape=outs, in_specs=[smem if a.dtype == jnp.int...]
    all_to_all x1, waiting for transfers between devices: 3.52 us -> 0.01 us  [grid_sum(): parts = lax.all_to_all(parts, OUTER, 0, 0, tiled=True)]
    ppermute x4, waiting for transfers between devices: 0.45 us -> 2.64 us  [exchange(): from_a = lax.ppermute(jnp.where(even, high, low), axes, pairs_a)]
    ppermute x4, starting transfers between devices: 31.7 us -> 33.5 us  [exchange(): from_b = lax.ppermute(jnp.where(even, low, high), axes, pairs_b)]
    all_to_all x1, starting transfers between devices: 8.14 us -> 9.44 us  [grid_sum(): return lax.all_to_all(spread, OUTER, 0, 0, tiled=True)]
  transfers between devices with their start and end apart: 11 -> 11, of which waited for: 4 -> 4; matrix products, arithmetic and copies ran while one was open for 3% -> 3% of each run, Pallas kernels for 12% -> 9%
where the time goes in v4:
time: 106 us; the launch traced here: 105 us
  starting transfers between devices  65.5 us (62%)
  waiting for transfers between devices  16.1 us (15%)
  Pallas kernels  14.8 us (14%)
  local copies, waits for them, and re-layouts  3.78 us (4%)
  other arithmetic  3.66 us (3%)
    ppermute x4, starting transfers between devices, exchange(): from_b = lax.ppermute(jnp.where(even, low, high), axes, pairs_b)  33.5 us
    pallas_call x4, Pallas kernels, call(): pl.pallas_call(body, out_shape=outs, in_specs=[smem if a.dtype == jnp.int...  14.8 us
    ppermute x4, starting transfers between devices, exchange(): from_a = lax.ppermute(jnp.where(even, high, low), axes, pairs_a)  14.3 us
    all_to_all x1, waiting for transfers between devices, grid_sum(): total = jnp.sum(lax.all_to_all(copies, INNER, 0, 0, tiled=True), axis=0)  10.4 us
    all_to_all x1, starting transfers between devices, grid_sum(): return lax.all_to_all(spread, OUTER, 0, 0, tiled=True)  9.44 us
    all_to_all x1, starting transfers between devices, grid_sum(): parts = lax.all_to_all(parts, OUTER, 0, 0, tiled=True)  4.84 us
    all_to_all x1, starting transfers between devices, grid_sum(): total = jnp.sum(lax.all_to_all(copies, INNER, 0, 0, tiled=True), axis=0)  3.51 us
    ppermute x4, waiting for transfers between devices, exchange(): from_b = lax.ppermute(jnp.where(even, low, high), axes, pairs_b)  3.1 us
  transfers between devices with their start and end apart: 11, of which 4 were waited for; matrix products, arithmetic and copies ran while one was open for 3% of the time, Pallas kernels for 9%

profile of v4, /device:TPU:1, one launch (start us, length us, event | category | flops | bytes accessed | tf_op | source)
XLA Modules:
  0.0 104.8 jit_solution(8869207747222342886)
XLA Ops:
  0.7 0.7 copy-done.5
  1.4 0.9 broadcast_select_fusion.6
  2.3 4.6 %collective-permute-start.1 = (bf16[3,48,128]{2,1,0:T(8,128)(2,1)S(1)}, bf16[3,48,128]{2,1,0:T(8,128)(2,1)S(1)}, u32[]{:S(2)}, u32[]{:S(2)}) collective-permute-start(bf16[3,48,128]{2,1,0:T(8,128)(2,1)S(1)} %get-tuple-element.27), channel_id=1, source_target_pairs={{1,2},{3,4},{5,6},{2,1},{4,3},{6,5},{9,10},{11,12},{13,14},{10,9},... | collective-permute-start | bytes 110600 | tf_op jit(solution)/shard_map/ppermute | solution.py:244
  6.9 8.5 %collective-permute-start = (bf16[3,48,128]{2,1,0:T(8,128)(2,1)S(1)}, bf16[3,48,128]{2,1,0:T(8,128)(2,1)S(1)}, u32[]{:S(2)}, u32[]{:S(2)}) collective-permute-start(bf16[3,48,128]{2,1,0:T(8,128)(2,1)S(1)} %get-tuple-element.28), channel_id=1, source_target_pairs={{0,1},{2,3},{4,5},{6,7},{1,0},{3,2},{5,4},{7,6},{8,9},{10,11},{12,... | collective-permute-start | bytes 110600 | tf_op jit(solution)/shard_map/ppermute | solution.py:245
  15.4 0.1 fusion.5
  15.5 1.4 %broadcast_multiply_fusion = (bf16[32,48,128]{2,1,0:T(8,128)(2,1)S(1)}, bf16[32,48,128]{2,1,0:T(8,128)(2,1)S(1)}) fusion(bf16[32,48,128]{2,1,0:T(8,128)(2,1)} %param.10, bf16[32,48]{1,0:T(8,128)(2,1)S(1)} %convert_element_type.17, bf16[32,48,128]{2,1,0:T(8,128)(2,1)} %param.8), kind=kLoop, calls=%fused_computation.1 | loop fusion | flops 393216 | bytes 1575936 | tf_op jit(solution)/shard_map/mul | solution.py:288
  16.9 1.0 slice_multiply_fusion.3
  17.9 0.1 pad_add_fusion.flags
  18.1 14.3 %collective-permute-start.3 = (bf16[38,3,128]{2,1,0:T(4,128)(2,1)S(1)}, bf16[38,3,128]{2,1,0:T(4,128)(2,1)S(1)}, u32[]{:S(2)}, u32[]{:S(2)}) collective-permute-start(bf16[38,3,128]{2,1,0:T(4,128)(2,1)S(1)} %get-tuple-element.37), channel_id=1, source_target_pairs={{8,16},{24,32},{40,48},{56,64},{72,80},{88,96},{104,112},{120,128}... | collective-permute-start | bytes 87560 | tf_op jit(solution)/shard_map/ppermute | solution.py:244
  32.4 1.9 %collective-permute-start.2 = (bf16[38,3,128]{2,1,0:T(4,128)(2,1)S(1)}, bf16[38,3,128]{2,1,0:T(4,128)(2,1)S(1)}, u32[]{:S(2)}, u32[]{:S(2)}) collective-permute-start(bf16[38,3,128]{2,1,0:T(4,128)(2,1)S(1)} %get-tuple-element.38), channel_id=1, source_target_pairs={{0,8},{16,24},{32,40},{48,56},{64,72},{80,88},{96,104},{112,120},{... | collective-permute-start | bytes 87560 | tf_op jit(solution)/shard_map/ppermute | solution.py:245
  34.3 0.3 broadcast_in_dim.6.ocean
  34.6 0.5 copy-done
  35.2 0.1 copy-done.2
  35.3 5.4 %shard_map.119 = (bf16[32,48,128]{2,1,0:T(8,128)(2,1)S(1)}, bf16[32,48,128]{2,1,0:T(8,128)(2,1)S(1)}, f32[128,256]{1,0:T(8,128)S(1)}, f32[128,256]{1,0:T(8,128)S(1)}, f32[49,8,128]{2,1,0:T(8,128)S(1)}) custom-call(s32[2]{0:T(128)S(1)} %pad_add_fusion.flags, bf16[32,48,128]{2,1,0:T(8,128)(2,1)S(1)} %get-tuple-element.52.masked, ...), custom_call_target="tpu_custom_call" | custom-call | flops 350000000 | bytes 2097152 | tf_op jit(solution)/shard_map/pallas_call | solution.py:210
  40.8 4.6 %shard_map.120 = (bf16[32,48,128]{2,1,0:T(8,128)(2,1)}, bf16[32,48,128]{2,1,0:T(8,128)(2,1)S(1)}, bf16[64,9,128]{2,1,0:T(8,128)(2,1)}) custom-call(s32[2]{0:T(128)S(1)} %pad_add_fusion.flags, bf16[32,48,128]{2,1,0:T(8,128)(2,1)S(1)} %get-tuple-element.52.masked, bf16[3,48,128]{2,1,0:T(8,128)(2,1)S(1)} %collective-permute-done.lat_a, ...), custom_call_target="tpu_custom_call" | custom-call | flops 170000000 | bytes 2097152 | tf_op jit(solution)/shard_map/pallas_call | solution.py:210
  45.4 4.8 %all-to-all-start = ((bf16[64,9,128]{2,1,0:T(8,128)(2,1)}), bf16[64,9,128]{2,1,0:T(8,128)(2,1)S(1)}, u32[]{:S(2)}, u32[]{:S(2)}) async-start(bf16[64,9,128]{2,1,0:T(8,128)(2,1)} %get-tuple-element.23), calls=%async_computation | async-start | bytes 524288 | tf_op jit(solution)/shard_map/all_to_all | solution.py:264
  50.3 11.0 %collective-permute-start.5 = (bf16[32,3,128]{2,1,0:T(4,128)(2,1)S(1)}, bf16[32,3,128]{2,1,0:T(4,128)(2,1)S(1)}, u32[]{:S(2)}, u32[]{:S(2)}) collective-permute-start(bf16[32,3,128]{2,1,0:T(4,128)(2,1)S(1)} %get-tuple-element.31), channel_id=1, source_target_pairs={{8,16},{24,32},{40,48},{56,64},{72,80},{88,96},{104,112},{120,128}... | collective-permute-start | bytes 73736 | tf_op jit(solution)/shard_map/ppermute | solution.py:244
  61.3 1.9 %collective-permute-start.4 = (bf16[32,3,128]{2,1,0:T(4,128)(2,1)S(1)}, bf16[32,3,128]{2,1,0:T(4,128)(2,1)S(1)}, u32[]{:S(2)}, u32[]{:S(2)}) collective-permute-start(bf16[32,3,128]{2,1,0:T(4,128)(2,1)S(1)} %get-tuple-element.32), channel_id=1, source_target_pairs={{0,8},{16,24},{32,40},{48,56},{64,72},{80,88},{96,104},{112,120},{... | collective-permute-start | bytes 73736 | tf_op jit(solution)/shard_map/ppermute | solution.py:245
  63.3 0.1 collective-permute-done.5.lon_b
  63.4 2.6 %collective-permute-done.4.lon_a = bf16[32,3,128]{2,1,0:T(4,128)(2,1)S(1)} collective-permute-done((bf16[32,3,128]{2,1,0:T(4,128)(2,1)S(1)}, bf16[32,3,128]{2,1,0:T(4,128)(2,1)S(1)}, u32[]{:S(2)}, u32[]{:S(2)}) %collective-permute-start.4) | collective-permute-done | bytes 24608 | tf_op jit(solution)/shard_map/ppermute | solution.py:245
  66.0 0.1 convert_reduce_fusion
  66.1 0.7 broadcast_in_dim.7
  66.8 3.5 %all-to-all-start.1 = ((f32[12,9,128]{2,1,0:T(8,128)}), f32[12,9,128]{2,1,0:T(8,128)S(1)}, u32[]{:S(2)}, u32[]{:S(2)}) async-start(f32[12,9,128]{2,1,0:T(8,128)} %broadcast_in_dim.7), calls=%async_computation.1 | async-start | bytes 196608 | tf_op jit(solution)/shard_map/all_to_all | solution.py:268
  70.3 10.4 %all-to-all-done.1 = f32[12,9,128]{2,1,0:T(8,128)S(1)} async-done(((f32[12,9,128]{2,1,0:T(8,128)}), f32[12,9,128]{2,1,0:T(8,128)S(1)}, u32[]{:S(2)}, u32[]{:S(2)}) %all-to-all-start.1) | async-done | bytes 55328 | tf_op jit(solution)/shard_map/all_to_all | solution.py:268
  80.7 0.7 broadcast_in_dim.8
  81.4 9.4 %all-to-all-start.2 = ((bf16[64,9,128]{2,1,0:T(8,128)(2,1)}), bf16[64,9,128]{2,1,0:T(8,128)(2,1)S(1)}, u32[]{:S(2)}, u32[]{:S(2)}) async-start(bf16[64,9,128]{2,1,0:T(8,128)(2,1)} %broadcast_in_dim.8), calls=%async_computation.2 | async-start | bytes 524288 | tf_op jit(solution)/shard_map/all_to_all | solution.py:270
  90.9 3.5 %collective-permute-start.7 = (bf16[3,54,128]{2,1,0:T(8,128)(2,1)S(1)}, bf16[3,54,128]{2,1,0:T(8,128)(2,1)S(1)}, u32[]{:S(2)}, u32[]{:S(2)}) collective-permute-start(bf16[3,54,128]{2,1,0:T(8,128)(2,1)S(1)} %get-tuple-element.35), channel_id=1, source_target_pairs={{1,2},{3,4},{5,6},{2,1},{4,3},{6,5},{9,10},{11,12},{13,14},{10,9},... | collective-permute-start | bytes 124424 | tf_op jit(solution)/shard_map/ppermute | solution.py:244
  94.5 1.9 %collective-permute-start.6 = (bf16[3,54,128]{2,1,0:T(8,128)(2,1)S(1)}, bf16[3,54,128]{2,1,0:T(8,128)(2,1)S(1)}, u32[]{:S(2)}, u32[]{:S(2)}) collective-permute-start(bf16[3,54,128]{2,1,0:T(8,128)(2,1)S(1)} %get-tuple-element.36), channel_id=1, source_target_pairs={{0,1},{2,3},{4,5},{6,7},{1,0},{3,2},{5,4},{7,6},{8,9},{10,11},{12,... | collective-permute-start | bytes 124424 | tf_op jit(solution)/shard_map/ppermute | solution.py:245
  96.4 3.0 %collective-permute-done.7.lat_b = bf16[3,54,128]{2,1,0:T(8,128)(2,1)S(1)} collective-permute-done((bf16[3,54,128]{2,1,0:T(8,128)(2,1)S(1)}, bf16[3,54,128]{2,1,0:T(8,128)(2,1)S(1)}, u32[]{:S(2)}, u32[]{:S(2)}) %collective-permute-start.7) | collective-permute-done | bytes 41504 | tf_op jit(solution)/shard_map/ppermute | solution.py:244
  99.4 4.0 %shard_map.121 = bf16[32,48,128]{2,1,0:T(8,128)(2,1)} custom-call(s32[2]{0:T(128)S(1)} %pad_add_fusion.flags, bf16[32,48,128]{2,1,0:T(8,128)(2,1)S(1)} %get-tuple-element.22.dz, bf16[32,3,128]{2,1,0:T(4,128)(2,1)S(1)} %collective-permute-done.4.lon_a, bf16[32,3,128]{2,1,0:T(4,128)(2,1)S(1)} %collective-permute-done.5.lon_b, ...), custom_call_target="tpu_custom_call" | custom-call | flops 100000000 | bytes 2097152 | tf_op jit(solution)/shard_map/pallas_call | solution.py:210
  103.5 0.8 shard_map.122
  104.2 0.6 reshape.34
  (29 shorter events, 0.3 us)
Async XLA Ops:
  0.6 0.7 copy-start.5
  2.3 15.7 %collective-permute-start.1 = (bf16[3,48,128]{2,1,0:T(8,128)(2,1)S(1)}, bf16[3,48,128]{2,1,0:T(8,128)(2,1)S(1)}, u32[]{:S(2)}, u32[]{:S(2)}) collective-permute-start(bf16[3,48,128]{2,1,0:T(8,128)(2,1)S(1)} %get-tuple-element.27), channel_id=1, source_target_pairs={{1,2},{3,4},{5,6},{2,1},{4,3},{6,5},{9,10},{11,12},{13,14},{10,9},... | collective-permute-start | bytes 110600 | tf_op jit(solution)/shard_map/ppermute | solution.py:244
  6.9 11.1 %collective-permute-start = (bf16[3,48,128]{2,1,0:T(8,128)(2,1)S(1)}, bf16[3,48,128]{2,1,0:T(8,128)(2,1)S(1)}, u32[]{:S(2)}, u32[]{:S(2)}) collective-permute-start(bf16[3,48,128]{2,1,0:T(8,128)(2,1)S(1)} %get-tuple-element.28), channel_id=1, source_target_pairs={{0,1},{2,3},{4,5},{6,7},{1,0},{3,2},{5,4},{7,6},{8,9},{10,11},{12,... | collective-permute-start | bytes 110600 | tf_op jit(solution)/shard_map/ppermute | solution.py:245
  16.9 1.1 %copy-start.4 = (f32[7,7,128]{2,1,0:T(8,128)S(1)}, f32[7,7,128]{2,1,0:T(8,128)}, u32[]{:S(2)}) copy-start(f32[7,7,128]{2,1,0:T(8,128)} %param.11) | copy-start | bytes 75268
  18.1 22.7 %collective-permute-start.3 = (bf16[38,3,128]{2,1,0:T(4,128)(2,1)S(1)}, bf16[38,3,128]{2,1,0:T(4,128)(2,1)S(1)}, u32[]{:S(2)}, u32[]{:S(2)}) collective-permute-start(bf16[38,3,128]{2,1,0:T(4,128)(2,1)S(1)} %get-tuple-element.37), channel_id=1, source_target_pairs={{8,16},{24,32},{40,48},{56,64},{72,80},{88,96},{104,112},{120,128}... | collective-permute-start | bytes 87560 | tf_op jit(solution)/shard_map/ppermute | solution.py:244
  32.4 8.4 %collective-permute-start.2 = (bf16[38,3,128]{2,1,0:T(4,128)(2,1)S(1)}, bf16[38,3,128]{2,1,0:T(4,128)(2,1)S(1)}, u32[]{:S(2)}, u32[]{:S(2)}) collective-permute-start(bf16[38,3,128]{2,1,0:T(4,128)(2,1)S(1)} %get-tuple-element.38), channel_id=1, source_target_pairs={{0,8},{16,24},{32,40},{48,56},{64,72},{80,88},{96,104},{112,120},{... | collective-permute-start | bytes 87560 | tf_op jit(solution)/shard_map/ppermute | solution.py:245
  34.3 0.8 copy-start
  34.3 0.9 copy-start.1
  34.6 0.7 copy-start.2
  34.6 0.7 copy-start.3
  45.4 20.6 %all-to-all-start = ((bf16[64,9,128]{2,1,0:T(8,128)(2,1)}), bf16[64,9,128]{2,1,0:T(8,128)(2,1)S(1)}, u32[]{:S(2)}, u32[]{:S(2)}) async-start(bf16[64,9,128]{2,1,0:T(8,128)(2,1)} %get-tuple-element.23), calls=%async_computation | async-start | bytes 524288 | tf_op jit(solution)/shard_map/all_to_all | solution.py:264
  50.3 13.1 %collective-permute-start.5 = (bf16[32,3,128]{2,1,0:T(4,128)(2,1)S(1)}, bf16[32,3,128]{2,1,0:T(4,128)(2,1)S(1)}, u32[]{:S(2)}, u32[]{:S(2)}) collective-permute-start(bf16[32,3,128]{2,1,0:T(4,128)(2,1)S(1)} %get-tuple-element.31), channel_id=1, source_target_pairs={{8,16},{24,32},{40,48},{56,64},{72,80},{88,96},{104,112},{120,128}... | collective-permute-start | bytes 73736 | tf_op jit(solution)/shard_map/ppermute | solution.py:244
  61.3 4.7 %collective-permute-start.4 = (bf16[32,3,128]{2,1,0:T(4,128)(2,1)S(1)}, bf16[32,3,128]{2,1,0:T(4,128)(2,1)S(1)}, u32[]{:S(2)}, u32[]{:S(2)}) collective-permute-start(bf16[32,3,128]{2,1,0:T(4,128)(2,1)S(1)} %get-tuple-element.32), channel_id=1, source_target_pairs={{0,8},{16,24},{32,40},{48,56},{64,72},{80,88},{96,104},{112,120},{... | collective-permute-start | bytes 73736 | tf_op jit(solution)/shard_map/ppermute | solution.py:245
  66.8 13.9 %all-to-all-start.1 = ((f32[12,9,128]{2,1,0:T(8,128)}), f32[12,9,128]{2,1,0:T(8,128)S(1)}, u32[]{:S(2)}, u32[]{:S(2)}) async-start(f32[12,9,128]{2,1,0:T(8,128)} %broadcast_in_dim.7), calls=%async_computation.1 | async-start | bytes 196608 | tf_op jit(solution)/shard_map/all_to_all | solution.py:268
  81.4 22.0 %all-to-all-start.2 = ((bf16[64,9,128]{2,1,0:T(8,128)(2,1)}), bf16[64,9,128]{2,1,0:T(8,128)(2,1)S(1)}, u32[]{:S(2)}, u32[]{:S(2)}) async-start(bf16[64,9,128]{2,1,0:T(8,128)(2,1)} %broadcast_in_dim.8), calls=%async_computation.2 | async-start | bytes 524288 | tf_op jit(solution)/shard_map/all_to_all | solution.py:270
  90.9 8.5 %collective-permute-start.7 = (bf16[3,54,128]{2,1,0:T(8,128)(2,1)S(1)}, bf16[3,54,128]{2,1,0:T(8,128)(2,1)S(1)}, u32[]{:S(2)}, u32[]{:S(2)}) collective-permute-start(bf16[3,54,128]{2,1,0:T(8,128)(2,1)S(1)} %get-tuple-element.35), channel_id=1, source_target_pairs={{1,2},{3,4},{5,6},{2,1},{4,3},{6,5},{9,10},{11,12},{13,14},{10,9},... | collective-permute-start | bytes 124424 | tf_op jit(solution)/shard_map/ppermute | solution.py:244
  94.5 4.9 %collective-permute-start.6 = (bf16[3,54,128]{2,1,0:T(8,128)(2,1)S(1)}, bf16[3,54,128]{2,1,0:T(8,128)(2,1)S(1)}, u32[]{:S(2)}, u32[]{:S(2)}) collective-permute-start(bf16[3,54,128]{2,1,0:T(8,128)(2,1)S(1)} %get-tuple-element.36), channel_id=1, source_target_pairs={{0,1},{2,3},{4,5},{6,7},{1,0},{3,2},{5,4},{7,6},{8,9},{10,11},{12,... | collective-permute-start | bytes 124424 | tf_op jit(solution)/shard_map/ppermute | solution.py:245

commit v5 on v4

--- a/solution.py
+++ b/solution.py
@@ -201,7 +201,8 @@
     w_in_grad[:, 0:C] = lines[0:C, :]
     w_in_grad[:, C:] = lines[C : 2 * C, :]
     w_out_grad[...] = lines[2 * C : 2 * C + FF, :]
-    kernel_grad[...] = lines[512:561, :]
+    for row in range(7):
+        kernel_grad[row] = lines[512 + 7 * row : 519 + 7 * row, :]
 
 
 def call(body, args, outs, scratch, flops):
@@ -236,13 +237,16 @@
     return size
 
 
+def swap(values, axes, count, first, wraps):
+    starts = [i for i in range(first, count, 2) if wraps or i + 1 < count]
+    pairs = [(i, (i + 1) % count) for i in starts] + [((i + 1) % count, i) for i in starts]
+    return lax.ppermute(values, axes, pairs)
+
+
 def exchange(low, high, axes, count, wraps):
     even = lax.axis_index(axes[-1]) % 2 == 0
-    joins = [i for i in range(1, count, 2) if wraps or i + 1 < count]
-    pairs_b = [(i, (i + 1) % count) for i in joins] + [((i + 1) % count, i) for i in joins]
-    pairs_a = [(i, i + 1) for i in range(0, count, 2)] + [(i + 1, i) for i in range(0, count, 2)]
-    from_b = lax.ppermute(jnp.where(even, low, high), axes, pairs_b)
-    from_a = lax.ppermute(jnp.where(even, high, low), axes, pairs_a)
+    from_b = swap(jnp.where(even, low, high), axes, count, 1, wraps)
+    from_a = swap(jnp.where(even, high, low), axes, count, 0, wraps)
     return from_a, from_b
 
 
@@ -259,14 +263,17 @@
     return exchange(head, tail, LON, group_size(LON), True)
 
 
-def grid_sum(parts):
-    size, chunk, _ = parts.shape
-    parts = lax.all_to_all(parts, OUTER, 0, 0, tiled=True)
-    own = jnp.sum(parts.astype(jnp.float32), axis=0)
-    count = group_size(INNER)
-    copies = jnp.broadcast_to(own[None], (count, chunk, C))
-    total = jnp.sum(lax.all_to_all(copies, INNER, 0, 0, tiled=True), axis=0)
-    spread = jnp.broadcast_to(total.astype(LINK)[None], (size, chunk, C))
+def scatter_sum(parts):
+    return jnp.sum(lax.all_to_all(parts, OUTER, 0, 0, tiled=True).astype(jnp.float32), axis=0)
+
+
+def inner_sum(own):
+    copies = jnp.broadcast_to(own[None], (group_size(INNER), *own.shape))
+    return jnp.sum(lax.all_to_all(copies, INNER, 0, 0, tiled=True), axis=0).astype(LINK)
+
+
+def hand_out(total):
+    spread = jnp.broadcast_to(total[None], (group_size(OUTER), *total.shape))
     return lax.all_to_all(spread, OUTER, 0, 0, tiled=True)
 
 
@@ -279,13 +286,11 @@
         return fields[rows, cols] * ocean[rows, cols].astype(jnp.bfloat16)[..., None]
 
     every = slice(None)
-    top, bottom = edge(slice(0, 3), every), edge(slice(ROWS - 3, ROWS), every)
-    head, tail = edge(every, slice(0, 3)), edge(every, slice(COLS - 3, COLS))
-    lat = lat_halo(top, bottom)
-    lon = lon_halo(head, tail, *lat)
+    lat = lat_halo(edge(slice(0, 3), every), edge(slice(ROWS - 3, ROWS), every))
     ocean_b = jnp.broadcast_to(ocean.astype(jnp.bfloat16)[..., None], fields.shape)
     masked = fields * ocean_b
     gmask = cotangent * ocean_b
+    lon = lon_halo(masked[:, :3], masked[:, COLS - 3 :], *lat)
     scratch = [pltpu.VMEM(shape, jnp.float32) for shape in SUMS]
     inside = call(
         inside_kernel,
@@ -302,15 +307,20 @@
         [NARROW, NARROW, *scratch, pltpu.VMEM((TERM_ROWS, C), jnp.float32)],
         170_000_000,
     )
-    sums = grid_sum(terms)
-    lon_a, lon_b = exchange(dz[:, :3], dz[:, COLS - 3 :], LON, group_size(LON), True)
+    own = scatter_sum(terms)
     even = flags[1] == 0
+    low, high = dz[:, :3], dz[:, COLS - 3 :]
+    lon_b = swap(jnp.where(even, low, high), LON, group_size(LON), 1, True)
+    near, own = lax.optimization_barrier((jnp.where(even, high, low), own))
+    lon_a = swap(near, LON, group_size(LON), 0, True)
     west, east = jnp.where(even, lon_b, lon_a), jnp.where(even, lon_a, lon_b)
 
     def full(rows):
         return jnp.concatenate([west[rows], dz[rows], east[rows]], axis=1)
 
     lat = exchange(full(slice(0, 3)), full(slice(ROWS - 3, ROWS)), LAT, group_size(LAT), False)
+    total, *lat = lax.optimization_barrier((inner_sum(own), *lat))
+    sums = hand_out(total)
     (field_grad,) = call(
         back_kernel, (flags, dz, lon_a, lon_b, *lat, gmask, ocean_b, taps), [CELLS], [PADDED], 100_000_000
     )
@@ -318,11 +328,11 @@
     kernel_grad, w_in_grad, w_out_grad = call(
         functools.partial(final_kernel, factor=cells**-0.5),
         (sums,),
-        [kind(49, C), kind(C, FF), kind(FF, C)],
+        [kind(7, 7, C), kind(C, FF), kind(FF, C)],
         [pltpu.VMEM((TERM_ROWS, C), jnp.float32)],
         1_000_000,
     )
-    return (advanced, field_grad, kernel_grad.reshape(7, 7, C), w_in_grad, w_out_grad)
+    return (advanced, field_grad, kernel_grad, w_in_grad, w_out_grad)
 
 
 def solution(mesh):

time: 106 us -> 102 us (0.962)
  waiting for transfers between devices: 16.1 us -> 13.6 us
    ppermute x8, waiting for transfers between devices: 5.74 us -> 0.02 us  [swap(): return lax.ppermute(values, axes, pairs)]
    all_to_all x3, waiting for transfers between devices: 10.4 us -> 13.5 us  [the longest x1 7.96 us: hand_out(): return lax.all_to_all(spread, OUTER, 0, 0, tiled=True)]
    ppermute x8, starting transfers between devices: 47.7 us -> 49.2 us  [swap(): return lax.ppermute(values, axes, pairs)]
    all_to_all x3, starting transfers between devices: 17.8 us -> 16.5 us  [the longest x1 8.18 us: hand_out(): return lax.all_to_all(spread, OUTER, 0, 0, tiled=True)]
  transfers between devices with their start and end apart: 11 -> 11, of which waited for: 4 -> 3; matrix products, arithmetic and copies ran while one was open for 3% -> 3% of each run, Pallas kernels for 9% -> 9%
where the time goes in v5:
time: 102 us; the launch traced here: 101 us
  starting transfers between devices  65.7 us (64%)
  Pallas kernels  14.8 us (15%)
  waiting for transfers between devices  13.6 us (13%)
  local copies, waits for them, and re-layouts  3.73 us (4%)
  other arithmetic  2.65 us (3%)
    ppermute x8, starting transfers between devices, swap(): return lax.ppermute(values, axes, pairs)  49.2 us
    pallas_call x4, Pallas kernels, call(): pl.pallas_call(body, out_shape=outs, in_specs=[smem if a.dtype == jnp.int...  14.8 us
    all_to_all x1, starting transfers between devices, hand_out(): return lax.all_to_all(spread, OUTER, 0, 0, tiled=True)  8.18 us
    all_to_all x1, waiting for transfers between devices, hand_out(): return lax.all_to_all(spread, OUTER, 0, 0, tiled=True)  7.96 us
    all_to_all x1, starting transfers between devices, scatter_sum(): lax.all_to_all(parts, OUTER, 0, 0, tiled=True).astype(jnp.float32)  4.83 us
    all_to_all x1, waiting for transfers between devices, inner_sum(): lax.all_to_all(copies, INNER, 0, 0, tiled=True)  4.3 us
    all_to_all x1, starting transfers between devices, inner_sum(): lax.all_to_all(copies, INNER, 0, 0, tiled=True)  3.51 us
  transfers between devices with their start and end apart: 11, of which 3 were waited for; matrix products, arithmetic and copies ran while one was open for 3% of the time, Pallas kernels for 9%

profile of v5, /device:TPU:1, one launch (start us, length us, event | category | flops | bytes accessed | tf_op | source)
XLA Modules:
  0.0 101.4 jit_solution(15573549011635106976)
XLA Ops:
  0.7 0.7 copy-done.5
  1.4 0.9 broadcast_select_fusion.6
  2.3 4.6 %collective-permute-start.1 = (bf16[3,48,128]{2,1,0:T(8,128)(2,1)S(1)}, bf16[3,48,128]{2,1,0:T(8,128)(2,1)S(1)}, u32[]{:S(2)}, u32[]{:S(2)}) collective-permute-start(bf16[3,48,128]{2,1,0:T(8,128)(2,1)S(1)} %get-tuple-element.37), channel_id=1, source_target_pairs={{1,2},{3,4},{5,6},{2,1},{4,3},{6,5},{9,10},{11,12},{13,14},{10,9},... | collective-permute-start | bytes 110600 | tf_op jit(solution)/shard_map/ppermute | solution.py:243
  6.9 8.5 %collective-permute-start = (bf16[3,48,128]{2,1,0:T(8,128)(2,1)S(1)}, bf16[3,48,128]{2,1,0:T(8,128)(2,1)S(1)}, u32[]{:S(2)}, u32[]{:S(2)}) collective-permute-start(bf16[3,48,128]{2,1,0:T(8,128)(2,1)S(1)} %get-tuple-element.38), channel_id=1, source_target_pairs={{0,1},{2,3},{4,5},{6,7},{1,0},{3,2},{5,4},{7,6},{8,9},{10,11},{12,... | collective-permute-start | bytes 110600 | tf_op jit(solution)/shard_map/ppermute | solution.py:243
  15.4 1.4 %broadcast_multiply_fusion = (bf16[32,48,128]{2,1,0:T(8,128)(2,1)S(1)}, bf16[32,48,128]{2,1,0:T(8,128)(2,1)S(1)}) fusion(bf16[32,48,128]{2,1,0:T(8,128)(2,1)} %param.10, bf16[32,48]{1,0:T(8,128)(2,1)S(1)} %convert_element_type.11, bf16[32,48,128]{2,1,0:T(8,128)(2,1)} %param.8), kind=kLoop, calls=%fused_computation.1 | loop fusion | flops 393216 | bytes 1575936 | tf_op jit(solution)/shard_map/mul | solution.py:292
  16.8 0.1 pad_add_fusion.flags
  16.9 0.6 copy-done.4
  17.6 0.1 broadcast_select_fusion.2
  17.6 14.3 %collective-permute-start.3 = (bf16[38,3,128]{2,1,0:T(4,128)(2,1)S(1)}, bf16[38,3,128]{2,1,0:T(4,128)(2,1)S(1)}, u32[]{:S(2)}, u32[]{:S(2)}) collective-permute-start(bf16[38,3,128]{2,1,0:T(4,128)(2,1)S(1)} %get-tuple-element.47), channel_id=1, source_target_pairs={{8,16},{24,32},{40,48},{56,64},{72,80},{88,96},{104,112},{120,128}... | collective-permute-start | bytes 87560 | tf_op jit(solution)/shard_map/ppermute | solution.py:243
  31.9 1.9 %collective-permute-start.2 = (bf16[38,3,128]{2,1,0:T(4,128)(2,1)S(1)}, bf16[38,3,128]{2,1,0:T(4,128)(2,1)S(1)}, u32[]{:S(2)}, u32[]{:S(2)}) collective-permute-start(bf16[38,3,128]{2,1,0:T(4,128)(2,1)S(1)} %get-tuple-element.48), channel_id=1, source_target_pairs={{0,8},{16,24},{32,40},{48,56},{64,72},{80,88},{96,104},{112,120},{... | collective-permute-start | bytes 87560 | tf_op jit(solution)/shard_map/ppermute | solution.py:243
  33.9 0.0 copy-start
  33.9 0.3 broadcast_in_dim.6.ocean
  34.2 0.5 copy-done
  34.7 0.0 copy-done.1
  34.7 0.1 copy-done.2
  34.9 5.4 %shard_map.119 = (bf16[32,48,128]{2,1,0:T(8,128)(2,1)S(1)}, bf16[32,48,128]{2,1,0:T(8,128)(2,1)S(1)}, f32[128,256]{1,0:T(8,128)S(1)}, f32[128,256]{1,0:T(8,128)S(1)}, f32[49,8,128]{2,1,0:T(8,128)S(1)}) custom-call(s32[2]{0:T(128)S(1)} %pad_add_fusion.flags, bf16[32,48,128]{2,1,0:T(8,128)(2,1)S(1)} %get-tuple-element.62.masked, ...), custom_call_target="tpu_custom_call" | custom-call | flops 350000000 | bytes 2097152 | tf_op jit(solution)/shard_map/pallas_call | solution.py:211
  40.3 4.6 %shard_map.120 = (bf16[32,48,128]{2,1,0:T(8,128)(2,1)}, bf16[32,48,128]{2,1,0:T(8,128)(2,1)S(1)}, bf16[64,9,128]{2,1,0:T(8,128)(2,1)}) custom-call(s32[2]{0:T(128)S(1)} %pad_add_fusion.flags, bf16[32,48,128]{2,1,0:T(8,128)(2,1)S(1)} %get-tuple-element.62.masked, bf16[3,48,128]{2,1,0:T(8,128)(2,1)S(1)} %collective-permute-done.lat_a, ...), custom_call_target="tpu_custom_call" | custom-call | flops 170000000 | bytes 2097152 | tf_op jit(solution)/shard_map/pallas_call | solution.py:211
  44.9 4.8 %all-to-all-start = ((bf16[64,9,128]{2,1,0:T(8,128)(2,1)}), bf16[64,9,128]{2,1,0:T(8,128)(2,1)S(1)}, u32[]{:S(2)}, u32[]{:S(2)}) async-start(bf16[64,9,128]{2,1,0:T(8,128)(2,1)} %get-tuple-element.28), calls=%async_computation | async-start | bytes 524288 | tf_op jit(solution)/shard_map/all_to_all | solution.py:267
  49.8 11.0 %collective-permute-start.5 = (bf16[32,3,128]{2,1,0:T(4,128)(2,1)S(1)}, bf16[32,3,128]{2,1,0:T(4,128)(2,1)S(1)}, u32[]{:S(2)}, u32[]{:S(2)}) collective-permute-start(bf16[32,3,128]{2,1,0:T(4,128)(2,1)S(1)} %get-tuple-element.41), channel_id=1, source_target_pairs={{8,16},{24,32},{40,48},{56,64},{72,80},{88,96},{104,112},{120,128}... | collective-permute-start | bytes 73736 | tf_op jit(solution)/shard_map/ppermute | solution.py:243
  60.9 1.3 %all-to-all-done = bf16[64,9,128]{2,1,0:T(8,128)(2,1)S(1)} async-done(((bf16[64,9,128]{2,1,0:T(8,128)(2,1)}), bf16[64,9,128]{2,1,0:T(8,128)(2,1)S(1)}, u32[]{:S(2)}, u32[]{:S(2)}) %all-to-all-start) | async-done | bytes 147488 | tf_op jit(solution)/shard_map/all_to_all | solution.py:267
  62.2 0.1 convert_reduce_fusion
  62.2 3.3 %collective-permute-start.4 = (bf16[32,3,128]{2,1,0:T(4,128)(2,1)S(1)}, bf16[32,3,128]{2,1,0:T(4,128)(2,1)S(1)}, u32[]{:S(2)}, u32[]{:S(2)}) collective-permute-start(bf16[32,3,128]{2,1,0:T(4,128)(2,1)S(1)} %get-tuple-element.29), channel_id=1, source_target_pairs={{0,8},{16,24},{32,40},{48,56},{64,72},{80,88},{96,104},{112,120},{... | collective-permute-start | bytes 73736 | tf_op jit(solution)/shard_map/ppermute | solution.py:243
  65.5 0.6 broadcast_in_dim.7
  66.2 3.5 %all-to-all-start.1 = ((f32[12,9,128]{2,1,0:T(8,128)}), f32[12,9,128]{2,1,0:T(8,128)S(1)}, u32[]{:S(2)}, u32[]{:S(2)}) async-start(f32[12,9,128]{2,1,0:T(8,128)} %broadcast_in_dim.7), calls=%async_computation.1 | async-start | bytes 196608 | tf_op jit(solution)/shard_map/all_to_all | solution.py:272
  69.9 3.7 %collective-permute-start.7 = (bf16[3,54,128]{2,1,0:T(8,128)(2,1)S(1)}, bf16[3,54,128]{2,1,0:T(8,128)(2,1)S(1)}, u32[]{:S(2)}, u32[]{:S(2)}) collective-permute-start(bf16[3,54,128]{2,1,0:T(8,128)(2,1)S(1)} %get-tuple-element.45), channel_id=1, source_target_pairs={{1,2},{3,4},{5,6},{2,1},{4,3},{6,5},{9,10},{11,12},{13,14},{10,9},... | collective-permute-start | bytes 124424 | tf_op jit(solution)/shard_map/ppermute | solution.py:243
  73.5 1.9 %collective-permute-start.6 = (bf16[3,54,128]{2,1,0:T(8,128)(2,1)S(1)}, bf16[3,54,128]{2,1,0:T(8,128)(2,1)S(1)}, u32[]{:S(2)}, u32[]{:S(2)}) collective-permute-start(bf16[3,54,128]{2,1,0:T(8,128)(2,1)S(1)} %get-tuple-element.46), channel_id=1, source_target_pairs={{0,1},{2,3},{4,5},{6,7},{1,0},{3,2},{5,4},{7,6},{8,9},{10,11},{12,... | collective-permute-start | bytes 124424 | tf_op jit(solution)/shard_map/ppermute | solution.py:243
  75.4 4.3 %all-to-all-done.1 = f32[12,9,128]{2,1,0:T(8,128)S(1)} async-done(((f32[12,9,128]{2,1,0:T(8,128)}), f32[12,9,128]{2,1,0:T(8,128)S(1)}, u32[]{:S(2)}, u32[]{:S(2)}) %all-to-all-start.1) | async-done | bytes 55328 | tf_op jit(solution)/shard_map/all_to_all | solution.py:272
  79.8 0.7 broadcast_in_dim.8
  80.5 8.2 %all-to-all-start.2 = ((bf16[64,9,128]{2,1,0:T(8,128)(2,1)}), bf16[64,9,128]{2,1,0:T(8,128)(2,1)S(1)}, u32[]{:S(2)}, u32[]{:S(2)}) async-start(bf16[64,9,128]{2,1,0:T(8,128)(2,1)} %broadcast_in_dim.8), calls=%async_computation.2 | async-start | bytes 524288 | tf_op jit(solution)/shard_map/all_to_all | solution.py:277
  88.7 4.0 %shard_map.121 = bf16[32,48,128]{2,1,0:T(8,128)(2,1)} custom-call(s32[2]{0:T(128)S(1)} %pad_add_fusion.flags, bf16[32,48,128]{2,1,0:T(8,128)(2,1)S(1)} %get-tuple-element.27.dz, bf16[32,3,128]{2,1,0:T(4,128)(2,1)S(1)} %collective-permute-done.4.lon_a, bf16[32,3,128]{2,1,0:T(4,128)(2,1)S(1)} %collective-permute-done.5.lon_b, ...), custom_call_target="tpu_custom_call" | custom-call | flops 100000000 | bytes 2097152 | tf_op jit(solution)/shard_map/pallas_call | solution.py:211
  92.7 8.0 %all-to-all-done.2.parts = bf16[64,9,128]{2,1,0:T(8,128)(2,1)S(1)} async-done(((bf16[64,9,128]{2,1,0:T(8,128)(2,1)}), bf16[64,9,128]{2,1,0:T(8,128)(2,1)S(1)}, u32[]{:S(2)}, u32[]{:S(2)}) %all-to-all-start.2) | async-done | bytes 147488 | tf_op jit(solution)/shard_map/all_to_all | solution.py:277
  100.7 0.7 shard_map.122
  (27 shorter events, 0.3 us)
Async XLA Ops:
  0.6 0.7 copy-start.5
  2.3 15.3 %collective-permute-start.1 = (bf16[3,48,128]{2,1,0:T(8,128)(2,1)S(1)}, bf16[3,48,128]{2,1,0:T(8,128)(2,1)S(1)}, u32[]{:S(2)}, u32[]{:S(2)}) collective-permute-start(bf16[3,48,128]{2,1,0:T(8,128)(2,1)S(1)} %get-tuple-element.37), channel_id=1, source_target_pairs={{1,2},{3,4},{5,6},{2,1},{4,3},{6,5},{9,10},{11,12},{13,14},{10,9},... | collective-permute-start | bytes 110600 | tf_op jit(solution)/shard_map/ppermute | solution.py:243
  6.9 10.7 %collective-permute-start = (bf16[3,48,128]{2,1,0:T(8,128)(2,1)S(1)}, bf16[3,48,128]{2,1,0:T(8,128)(2,1)S(1)}, u32[]{:S(2)}, u32[]{:S(2)}) collective-permute-start(bf16[3,48,128]{2,1,0:T(8,128)(2,1)S(1)} %get-tuple-element.38), channel_id=1, source_target_pairs={{0,1},{2,3},{4,5},{6,7},{1,0},{3,2},{5,4},{7,6},{8,9},{10,11},{12,... | collective-permute-start | bytes 110600 | tf_op jit(solution)/shard_map/ppermute | solution.py:243
  16.8 0.8 copy-start.4
  17.6 22.7 %collective-permute-start.3 = (bf16[38,3,128]{2,1,0:T(4,128)(2,1)S(1)}, bf16[38,3,128]{2,1,0:T(4,128)(2,1)S(1)}, u32[]{:S(2)}, u32[]{:S(2)}) collective-permute-start(bf16[38,3,128]{2,1,0:T(4,128)(2,1)S(1)} %get-tuple-element.47), channel_id=1, source_target_pairs={{8,16},{24,32},{40,48},{56,64},{72,80},{88,96},{104,112},{120,128}... | collective-permute-start | bytes 87560 | tf_op jit(solution)/shard_map/ppermute | solution.py:243
  31.9 8.4 %collective-permute-start.2 = (bf16[38,3,128]{2,1,0:T(4,128)(2,1)S(1)}, bf16[38,3,128]{2,1,0:T(4,128)(2,1)S(1)}, u32[]{:S(2)}, u32[]{:S(2)}) collective-permute-start(bf16[38,3,128]{2,1,0:T(4,128)(2,1)S(1)} %get-tuple-element.48), channel_id=1, source_target_pairs={{0,8},{16,24},{32,40},{48,56},{64,72},{80,88},{96,104},{112,120},{... | collective-permute-start | bytes 87560 | tf_op jit(solution)/shard_map/ppermute | solution.py:243
  33.9 0.8 copy-start
  33.9 0.9 copy-start.1
  34.2 0.7 copy-start.2
  34.2 0.7 copy-start.3
  44.9 17.2 %all-to-all-start = ((bf16[64,9,128]{2,1,0:T(8,128)(2,1)}), bf16[64,9,128]{2,1,0:T(8,128)(2,1)S(1)}, u32[]{:S(2)}, u32[]{:S(2)}) async-start(bf16[64,9,128]{2,1,0:T(8,128)(2,1)} %get-tuple-element.28), calls=%async_computation | async-start | bytes 524288 | tf_op jit(solution)/shard_map/all_to_all | solution.py:267
  49.8 19.9 %collective-permute-start.5 = (bf16[32,3,128]{2,1,0:T(4,128)(2,1)S(1)}, bf16[32,3,128]{2,1,0:T(4,128)(2,1)S(1)}, u32[]{:S(2)}, u32[]{:S(2)}) collective-permute-start(bf16[32,3,128]{2,1,0:T(4,128)(2,1)S(1)} %get-tuple-element.41), channel_id=1, source_target_pairs={{8,16},{24,32},{40,48},{56,64},{72,80},{88,96},{104,112},{120,128}... | collective-permute-start | bytes 73736 | tf_op jit(solution)/shard_map/ppermute | solution.py:243
  62.2 7.5 %collective-permute-start.4 = (bf16[32,3,128]{2,1,0:T(4,128)(2,1)S(1)}, bf16[32,3,128]{2,1,0:T(4,128)(2,1)S(1)}, u32[]{:S(2)}, u32[]{:S(2)}) collective-permute-start(bf16[32,3,128]{2,1,0:T(4,128)(2,1)S(1)} %get-tuple-element.29), channel_id=1, source_target_pairs={{0,8},{16,24},{32,40},{48,56},{64,72},{80,88},{96,104},{112,120},{... | collective-permute-start | bytes 73736 | tf_op jit(solution)/shard_map/ppermute | solution.py:243
  66.2 13.5 %all-to-all-start.1 = ((f32[12,9,128]{2,1,0:T(8,128)}), f32[12,9,128]{2,1,0:T(8,128)S(1)}, u32[]{:S(2)}, u32[]{:S(2)}) async-start(f32[12,9,128]{2,1,0:T(8,128)} %broadcast_in_dim.7), calls=%async_computation.1 | async-start | bytes 196608 | tf_op jit(solution)/shard_map/all_to_all | solution.py:272
  69.9 9.9 %collective-permute-start.7 = (bf16[3,54,128]{2,1,0:T(8,128)(2,1)S(1)}, bf16[3,54,128]{2,1,0:T(8,128)(2,1)S(1)}, u32[]{:S(2)}, u32[]{:S(2)}) collective-permute-start(bf16[3,54,128]{2,1,0:T(8,128)(2,1)S(1)} %get-tuple-element.45), channel_id=1, source_target_pairs={{1,2},{3,4},{5,6},{2,1},{4,3},{6,5},{9,10},{11,12},{13,14},{10,9},... | collective-permute-start | bytes 124424 | tf_op jit(solution)/shard_map/ppermute | solution.py:243
  73.5 6.3 %collective-permute-start.6 = (bf16[3,54,128]{2,1,0:T(8,128)(2,1)S(1)}, bf16[3,54,128]{2,1,0:T(8,128)(2,1)S(1)}, u32[]{:S(2)}, u32[]{:S(2)}) collective-permute-start(bf16[3,54,128]{2,1,0:T(8,128)(2,1)S(1)} %get-tuple-element.46), channel_id=1, source_target_pairs={{0,1},{2,3},{4,5},{6,7},{1,0},{3,2},{5,4},{7,6},{8,9},{10,11},{12,... | collective-permute-start | bytes 124424 | tf_op jit(solution)/shard_map/ppermute | solution.py:243
  80.5 20.2 %all-to-all-start.2 = ((bf16[64,9,128]{2,1,0:T(8,128)(2,1)}), bf16[64,9,128]{2,1,0:T(8,128)(2,1)S(1)}, u32[]{:S(2)}, u32[]{:S(2)}) async-start(bf16[64,9,128]{2,1,0:T(8,128)(2,1)} %broadcast_in_dim.8), calls=%async_computation.2 | async-start | bytes 524288 | tf_op jit(solution)/shard_map/all_to_all | solution.py:277

commit v6 on v5

--- a/solution.py
+++ b/solution.py
@@ -22,6 +22,8 @@
 
 INSIDE = ((8, 32),)
 STRIPS = ((0, 8), (40, 8))
+INSIDE_OUT = ((0, 32),)
+STRIPS_OUT = ((0, 8), (8, 8))
 
 
 def fill_rows(pad, own, flags, halo_a, halo_b, first, last, at):
@@ -73,7 +75,7 @@
             at += w
 
 
-def main_rows(step, segs, pads, masked, gmask, ocean, params, advanced, dz_out, sums, index):
+def main_rows(step, segs, outs, pads, gmask, params, hidden_out, dz_out, sums, index):
     f32, bf16 = jnp.float32, jnp.bfloat16
     taps, gain, w_in, b_in, w_out = params
     acc_in, acc_out, acc_tap = sums
@@ -88,7 +90,7 @@
     preact = jnp.dot(normed, w_in[...], preferred_element_type=f32) + b_in[...]
     cdf = 0.5 * (1.0 + lax.erf(preact * 0.7071067811865476))
     hidden = (preact * cdf).astype(bf16)
-    out = jnp.dot(hidden, w_out[...], preferred_element_type=f32)
+    hidden_out[pl.ds(index * hidden.shape[0], hidden.shape[0]), :] = hidden
     d_hidden = lax.dot_general(grad, w_out[...], (((1,), (1,)), ((), ())), preferred_element_type=f32)
     slopes = cdf + preact * jnp.exp(-0.5 * preact * preact) * 0.3989422804014327
     d_pre = (d_hidden * slopes).astype(bf16)
@@ -102,10 +104,7 @@
         - jnp.mean(scaled, axis=-1, keepdims=True)
         - unit * jnp.mean(scaled * unit, axis=-1, keepdims=True)
     )
-    write_cells(dz_out, first, step, segs, dz)
-    own = read_cells(masked, first, step, segs)
-    keep = read_cells(ocean, first, step, segs)
-    write_cells(advanced, first, step, segs, own + keep * out)
+    write_cells(dz_out, first, step, outs, dz)
     grads = dz.astype(bf16).astype(f32)
     per_row = sum(w for _, w in segs)
     for tap in range(7):
@@ -124,54 +123,72 @@
 
 
 def inside_kernel(
-    flags, masked, lat_a, lat_b, gmask, ocean, taps, gain, w_in, b_in, w_out,
-    advanced, dz_out, acc_in, acc_out, acc_tap, pad,
+    flags, masked, lat_b, lat_a, gmask, taps, gain, w_in, b_in, w_out,
+    hidden, dz_out, acc_in, acc_out, acc_tap, pad,
 ):
     fill_rows(pad, masked, flags, lat_a, lat_b, 0, COLS, 0)
     for acc in (acc_in, acc_out, acc_tap):
         acc[...] = jnp.zeros_like(acc)
     params = (taps, gain, w_in, b_in, w_out)
+    sums = (acc_in, acc_out, acc_tap)
 
     def block(index, carry):
-        main_rows(16, INSIDE, ((pad, 5, 32),), masked, gmask, ocean, params, advanced, dz_out, (acc_in, acc_out, acc_tap), index)
+        main_rows(16, INSIDE, INSIDE_OUT, ((pad, 5, 32),), gmask, params, hidden, dz_out, sums, index)
         return carry
 
     lax.fori_loop(0, ROWS // 16, block, 0)
 
 
 def strips_kernel(
-    flags, masked, lat_a, lat_b, lon_a, lon_b, gmask, ocean, taps, gain, w_in, b_in, w_out,
-    had_advanced, had_dz, had_in, had_out, had_tap,
-    advanced, dz_out, terms, left, right, acc_in, acc_out, acc_tap, lines,
+    flags, masked, lat_b, lat_a, lon_b, lon_a, gmask, taps, gain, w_in, b_in, w_out,
+    had_in, had_out, had_tap,
+    hidden, dz_out, terms, left, right, acc_in, acc_out, acc_tap,
 ):
     fill_strips(left, right, masked, flags, lat_a, lat_b, lon_a, lon_b)
-    advanced[:, 8:40, :] = had_advanced[:, 8:40, :]
-    dz_out[:, 8:40, :] = had_dz[:, 8:40, :]
     acc_in[...] = had_in[...]
     acc_out[...] = had_out[...]
     acc_tap[...] = had_tap[...]
     params = (taps, gain, w_in, b_in, w_out)
+    pads = ((left, 5, 8), (right, 5, 8))
+    main_rows(ROWS, STRIPS, STRIPS_OUT, pads, gmask, params, hidden, dz_out, (acc_in, acc_out, acc_tap), 0)
+    half = C // 8
+    turned = acc_out[...].T
+    tap_sums = jnp.sum(acc_tap[...], axis=1)
+    for part in range(half):
+        rows = slice(8 * part, 8 * part + 8)
+        terms[part, 0:8, :] = acc_in[rows, 0:C].astype(LINK)
+        terms[half + part, 0:8, :] = acc_in[rows, C:].astype(LINK)
+    for part in range(2 * half):
+        terms[2 * half + part, 0:8, :] = turned[8 * part : 8 * part + 8].astype(LINK)
+    for part in range(terms.shape[0]):
+        row = tap_sums[part : part + 1] if part < 49 else jnp.zeros((1, C), jnp.float32)
+        terms[part, 8:9, :] = row.astype(LINK)
+
+
+def advance_kernel(hidden_in, hidden_st, masked, ocean, w_out, advanced):
+    f32 = jnp.float32
 
     def block(index, carry):
-        main_rows(32, STRIPS, ((left, 5, 8), (right, 5, 8)), masked, gmask, ocean, params, advanced, dz_out, (acc_in, acc_out, acc_tap), index)
+        first = index * 8
+        for hidden, segs, outs in ((hidden_in, INSIDE, INSIDE_OUT), (hidden_st, STRIPS, STRIPS_OUT)):
+            width = sum(w for _, w in outs)
+            size = 8 * width
+            out = jnp.dot(hidden[pl.ds(index * size, size), :], w_out[...], preferred_element_type=f32)
+            own = read_cells(masked, first, 8, segs)
+            keep = read_cells(ocean, first, 8, segs)
+            write_cells(advanced, first, 8, segs, own + keep * out)
         return carry
 
-    lax.fori_loop(0, ROWS // 32, block, 0)
-    lines[0:C, :] = acc_in[:, 0:C]
-    lines[C : 2 * C, :] = acc_in[:, C:]
-    lines[2 * C : 2 * C + FF, :] = acc_out[...].T
-    lines[512:561, :] = jnp.sum(acc_tap[...], axis=1)
-    lines[561:576, :] = jnp.zeros((15, C), jnp.float32)
-    chunk = terms.shape[1]
-    for part in range(terms.shape[0]):
-        terms[part] = lines[part * chunk : (part + 1) * chunk, :].astype(LINK)
-
-
-def back_kernel(flags, dz, lon_a, lon_b, lat_a, lat_b, gmask, ocean, taps, field_grad, pad):
+    lax.fori_loop(0, ROWS // 8, block, 0)
+
+
+def back_kernel(flags, dz_in, dz_st, lon_b, lon_a, lat_b, lat_a, gmask, ocean, taps, field_grad, pad):
     f32 = jnp.float32
     even = flags[1] == 0
     from_a, from_b = lon_a[...].astype(f32), lon_b[...].astype(f32)
-    pad[3 : 3 + ROWS, 8 : 8 + COLS, :] = dz[...].astype(f32)
+    pad[3 : 3 + ROWS, 8:16, :] = dz_st[:, 0:8, :].astype(f32)
+    pad[3 : 3 + ROWS, 16:48, :] = dz_in[...].astype(f32)
+    pad[3 : 3 + ROWS, 48:56, :] = dz_st[:, 8:16, :].astype(f32)
     pad[3 : 3 + ROWS, 5:8, :] = jnp.where(even, from_b, from_a)
     pad[3 : 3 + ROWS, 8 + COLS : 11 + COLS, :] = jnp.where(even, from_a, from_b)
     even = flags[0] == 0
@@ -194,15 +211,18 @@
     write_cells(field_grad, first, step, segs, own + keep * back)
 
 
-def final_kernel(parts, kernel_grad, w_in_grad, w_out_grad, lines, *, factor):
-    chunk = parts.shape[1]
+def final_kernel(parts, kernel_grad, w_in_grad, w_out_grad, *, factor):
+    half = C // 8
     for part in range(parts.shape[0]):
-        lines[part * chunk : (part + 1) * chunk, :] = parts[part].astype(jnp.float32) * factor
-    w_in_grad[:, 0:C] = lines[0:C, :]
-    w_in_grad[:, C:] = lines[C : 2 * C, :]
-    w_out_grad[...] = lines[2 * C : 2 * C + FF, :]
-    for row in range(7):
-        kernel_grad[row] = lines[512 + 7 * row : 519 + 7 * row, :]
+        rows = parts[part, 0:8, :].astype(jnp.float32) * factor
+        if part < half:
+            w_in_grad[8 * part : 8 * part + 8, 0:C] = rows
+        elif part < 2 * half:
+            w_in_grad[8 * (part - half) : 8 * (part - half) + 8, C:] = rows
+        else:
+            w_out_grad[8 * (part - 2 * half) : 8 * (part - 2 * half) + 8, :] = rows
+    for part in range(49):
+        kernel_grad[part // 7, part % 7 : part % 7 + 1, :] = parts[part, 8:9, :].astype(jnp.float32) * factor
 
 
 def call(body, args, outs, scratch, flops):
@@ -247,14 +267,14 @@
     even = lax.axis_index(axes[-1]) % 2 == 0
     from_b = swap(jnp.where(even, low, high), axes, count, 1, wraps)
     from_a = swap(jnp.where(even, high, low), axes, count, 0, wraps)
-    return from_a, from_b
+    return from_b, from_a
 
 
 def lat_halo(top, bottom):
     return exchange(top, bottom, LAT, group_size(LAT), False)
 
 
-def lon_halo(head, tail, lat_a, lat_b):
+def lon_halo(head, tail, lat_b, lat_a):
     even = lax.axis_index(LAT[-1]) % 2 == 0
     north = jnp.where(even, lat_b, lat_a)
     south = jnp.where(even, lat_a, lat_b)
@@ -267,8 +287,11 @@
     return jnp.sum(lax.all_to_all(parts, OUTER, 0, 0, tiled=True).astype(jnp.float32), axis=0)
 
 
-def inner_sum(own):
-    copies = jnp.broadcast_to(own[None], (group_size(INNER), *own.shape))
+def inner_copies(own):
+    return jnp.broadcast_to(own[None], (group_size(INNER), *own.shape))
+
+
+def inner_sum(copies):
     return jnp.sum(lax.all_to_all(copies, INNER, 0, 0, tiled=True), axis=0).astype(LINK)
 
 
@@ -292,44 +315,54 @@
     gmask = cotangent * ocean_b
     lon = lon_halo(masked[:, :3], masked[:, COLS - 3 :], *lat)
     scratch = [pltpu.VMEM(shape, jnp.float32) for shape in SUMS]
-    inside = call(
+    hidden_in, dz_in, *sums = call(
         inside_kernel,
-        (flags, masked, *lat, gmask, ocean_b, *params),
-        [CELLS, CELLS, *(kind(*shape) for shape in SUMS)],
+        (flags, masked, *lat, gmask, *params),
+        [
+            kind(ROWS * 32, FF, dtype=jnp.bfloat16),
+            kind(ROWS, 32, C, dtype=jnp.bfloat16),
+            *(kind(*shape) for shape in SUMS),
+        ],
         [WIDE],
         350_000_000,
     )
     parts = group_size(OUTER)
-    advanced, dz, terms = call(
+    hidden_st, dz_st, terms = call(
         strips_kernel,
-        (flags, masked, *lat, *lon, gmask, ocean_b, *params, *inside),
-        [CELLS, CELLS, kind(parts, TERM_ROWS // parts, C, dtype=LINK)],
-        [NARROW, NARROW, *scratch, pltpu.VMEM((TERM_ROWS, C), jnp.float32)],
+        (flags, masked, *lat, *lon, gmask, *params, *sums),
+        [
+            kind(ROWS * 16, FF, dtype=jnp.bfloat16),
+            kind(ROWS, 16, C, dtype=jnp.bfloat16),
+            kind(parts, TERM_ROWS // parts, C, dtype=LINK),
+        ],
+        [NARROW, NARROW, *scratch],
         170_000_000,
     )
-    own = scatter_sum(terms)
+    copies = inner_copies(scatter_sum(terms))
     even = flags[1] == 0
-    low, high = dz[:, :3], dz[:, COLS - 3 :]
+    low, high = dz_st[:, :3], dz_st[:, 13:]
     lon_b = swap(jnp.where(even, low, high), LON, group_size(LON), 1, True)
-    near, own = lax.optimization_barrier((jnp.where(even, high, low), own))
+    (advanced,) = call(
+        advance_kernel, (hidden_in, hidden_st, masked, ocean_b, w_out), [CELLS], [], 100_000_000
+    )
+    near, copies = lax.optimization_barrier((jnp.where(even, high, low), copies))
     lon_a = swap(near, LON, group_size(LON), 0, True)
     west, east = jnp.where(even, lon_b, lon_a), jnp.where(even, lon_a, lon_b)
 
     def full(rows):
-        return jnp.concatenate([west[rows], dz[rows], east[rows]], axis=1)
+        return jnp.concatenate([west[rows], dz_st[rows, :8], dz_in[rows], dz_st[rows, 8:], east[rows]], axis=1)
 
     lat = exchange(full(slice(0, 3)), full(slice(ROWS - 3, ROWS)), LAT, group_size(LAT), False)
-    total, *lat = lax.optimization_barrier((inner_sum(own), *lat))
-    sums = hand_out(total)
+    sums = hand_out(inner_sum(copies))
     (field_grad,) = call(
-        back_kernel, (flags, dz, lon_a, lon_b, *lat, gmask, ocean_b, taps), [CELLS], [PADDED], 100_000_000
+        back_kernel, (flags, dz_in, dz_st, lon_b, lon_a, *lat, gmask, ocean_b, taps), [CELLS], [PADDED], 100_000_000
     )
     cells = ROWS * COLS * group_size(LAT) * group_size(LON)
     kernel_grad, w_in_grad, w_out_grad = call(
         functools.partial(final_kernel, factor=cells**-0.5),
         (sums,),
         [kind(7, 7, C), kind(C, FF), kind(FF, C)],
-        [pltpu.VMEM((TERM_ROWS, C), jnp.float32)],
+        [],
         1_000_000,
     )
     return (advanced, field_grad, kernel_grad, w_in_grad, w_out_grad)

time: 102 us -> 103 us (level)
  waiting for transfers between devices: 13.6 us -> 11.6 us
  Pallas kernels: 14.8 us -> 16.7 us
    all_to_all x1, waiting for transfers between devices: 7.96 us -> 0.01 us  [hand_out(): return lax.all_to_all(spread, OUTER, 0, 0, tiled=True)]
    all_to_all x1, waiting for transfers between devices: 4.3 us -> 9.95 us  [inner_sum(): lax.all_to_all(copies, INNER, 0, 0, tiled=True)]
    pallas_call x4 -> x5, Pallas kernels: 14.8 us -> 16.7 us  [call(): pl.pallas_call(body, out_shape=outs, in_specs=[smem if a.dtype == jnp.int...]
  transfers between devices with their start and end apart: 11 -> 11, of which waited for: 3 -> 3; matrix products, arithmetic and copies ran while one was open for 3% -> 3% of each run, Pallas kernels for 9% -> 11%
where the time goes in v6:
time: 103 us; the launch traced here: 102 us
  starting transfers between devices  65.6 us (64%)
  Pallas kernels  16.7 us (16%)
  waiting for transfers between devices  11.6 us (11%)
  local copies, waits for them, and re-layouts  4.51 us (4%)
  other arithmetic  2.63 us (3%)
    ppermute x8, starting transfers between devices, swap(): return lax.ppermute(values, axes, pairs)  49.1 us
    pallas_call x5, Pallas kernels, call(): pl.pallas_call(body, out_shape=outs, in_specs=[smem if a.dtype == jnp.int...  16.7 us
    all_to_all x1, waiting for transfers between devices, inner_sum(): lax.all_to_all(copies, INNER, 0, 0, tiled=True)  9.95 us
    all_to_all x1, starting transfers between devices, hand_out(): return lax.all_to_all(spread, OUTER, 0, 0, tiled=True)  8.18 us
    all_to_all x1, starting transfers between devices, scatter_sum(): lax.all_to_all(parts, OUTER, 0, 0, tiled=True).astype(jnp.float32)  4.83 us
    all_to_all x1, starting transfers between devices, inner_sum(): lax.all_to_all(copies, INNER, 0, 0, tiled=True)  3.52 us
  transfers between devices with their start and end apart: 11, of which 3 were waited for; matrix products, arithmetic and copies ran while one was open for 3% of the time, Pallas kernels for 11%

profile of v6, /device:TPU:1, one launch (start us, length us, event | category | flops | bytes accessed | tf_op | source)
XLA Modules:
  0.0 102.1 jit_solution(8268082130351368270)
XLA Ops:
  0.7 0.7 copy-done.5
  1.4 0.9 broadcast_select_fusion.6
  2.3 4.6 %collective-permute-start = (bf16[3,48,128]{2,1,0:T(8,128)(2,1)S(1)}, bf16[3,48,128]{2,1,0:T(8,128)(2,1)S(1)}, u32[]{:S(2)}, u32[]{:S(2)}) collective-permute-start(bf16[3,48,128]{2,1,0:T(8,128)(2,1)S(1)} %get-tuple-element.32), channel_id=1, source_target_pairs={{1,2},{3,4},{5,6},{2,1},{4,3},{6,5},{9,10},{11,12},{13,14},{10,9},... | collective-permute-start | bytes 110600 | tf_op jit(solution)/shard_map/ppermute | solution.py:263
  6.9 8.5 %collective-permute-start.1 = (bf16[3,48,128]{2,1,0:T(8,128)(2,1)S(1)}, bf16[3,48,128]{2,1,0:T(8,128)(2,1)S(1)}, u32[]{:S(2)}, u32[]{:S(2)}) collective-permute-start(bf16[3,48,128]{2,1,0:T(8,128)(2,1)S(1)} %get-tuple-element.31), channel_id=1, source_target_pairs={{0,1},{2,3},{4,5},{6,7},{1,0},{3,2},{5,4},{7,6},{8,9},{10,11},{12,... | collective-permute-start | bytes 110600 | tf_op jit(solution)/shard_map/ppermute | solution.py:263
  15.4 1.4 %broadcast_multiply_fusion = (bf16[32,48,128]{2,1,0:T(8,128)(2,1)S(1)}, bf16[32,48,128]{2,1,0:T(8,128)(2,1)S(1)}) fusion(bf16[32,48,128]{2,1,0:T(8,128)(2,1)} %param.10, bf16[32,48]{1,0:T(8,128)(2,1)S(1)} %convert_element_type.15, bf16[32,48,128]{2,1,0:T(8,128)(2,1)} %param.8), kind=kLoop, calls=%fused_computation.1 | loop fusion | flops 393216 | bytes 1575936 | tf_op jit(solution)/shard_map/mul | solution.py:315
  16.8 0.1 pad_add_fusion.flags
  16.9 0.6 copy-done.4
  17.6 0.1 broadcast_select_fusion.2
  17.7 14.3 %collective-permute-start.2 = (bf16[38,3,128]{2,1,0:T(4,128)(2,1)S(1)}, bf16[38,3,128]{2,1,0:T(4,128)(2,1)S(1)}, u32[]{:S(2)}, u32[]{:S(2)}) collective-permute-start(bf16[38,3,128]{2,1,0:T(4,128)(2,1)S(1)} %get-tuple-element.46), channel_id=1, source_target_pairs={{8,16},{24,32},{40,48},{56,64},{72,80},{88,96},{104,112},{120,128}... | collective-permute-start | bytes 87560 | tf_op jit(solution)/shard_map/ppermute | solution.py:263
  32.0 1.9 %collective-permute-start.3 = (bf16[38,3,128]{2,1,0:T(4,128)(2,1)S(1)}, bf16[38,3,128]{2,1,0:T(4,128)(2,1)S(1)}, u32[]{:S(2)}, u32[]{:S(2)}) collective-permute-start(bf16[38,3,128]{2,1,0:T(4,128)(2,1)S(1)} %get-tuple-element.45), channel_id=1, source_target_pairs={{0,8},{16,24},{32,40},{48,56},{64,72},{80,88},{96,104},{112,120},{... | collective-permute-start | bytes 87560 | tf_op jit(solution)/shard_map/ppermute | solution.py:263
  33.9 0.6 copy-done.2
  34.6 5.7 %shard_map.119 = (bf16[1024,256]{1,0:T(8,128)(2,1)S(1)}, bf16[32,32,128]{2,1,0:T(8,128)(2,1)S(1)}, f32[128,256]{1,0:T(8,128)S(1)}, f32[128,256]{1,0:T(8,128)S(1)}, f32[49,8,128]{2,1,0:T(8,128)S(1)}) custom-call(s32[2]{0:T(128)S(1)} %pad_add_fusion.flags, bf16[32,48,128]{2,1,0:T(8,128)(2,1)S(1)} %get-tuple-element.60.masked, ...), custom_call_target="tpu_custom_call" | custom-call | flops 350000000 | bytes 2097152 | tf_op jit(solution)/shard_map/pallas_call | solution.py:231
  40.3 4.6 %shard_map.120 = (bf16[512,256]{1,0:T(8,128)(2,1)S(1)}, bf16[32,16,128]{2,1,0:T(8,128)(2,1)S(1)}, bf16[64,9,128]{2,1,0:T(8,128)(2,1)}) custom-call(s32[2]{0:T(128)S(1)} %pad_add_fusion.flags, bf16[32,48,128]{2,1,0:T(8,128)(2,1)S(1)} %get-tuple-element.60.masked, bf16[3,48,128]{2,1,0:T(8,128)(2,1)S(1)} %collective-permute-done.lat_b, ...), custom_call_target="tpu_custom_call" | custom-call | flops 170000000 | bytes 2097152 | tf_op jit(solution)/shard_map/pallas_call | solution.py:231
  44.9 4.8 %all-to-all-start = ((bf16[64,9,128]{2,1,0:T(8,128)(2,1)}), bf16[64,9,128]{2,1,0:T(8,128)(2,1)S(1)}, u32[]{:S(2)}, u32[]{:S(2)}) async-start(bf16[64,9,128]{2,1,0:T(8,128)(2,1)} %get-tuple-element.25), calls=%async_computation | async-start | bytes 524288 | tf_op jit(solution)/shard_map/all_to_all | solution.py:287
  49.8 11.1 %collective-permute-start.4 = (bf16[32,3,128]{2,1,0:T(4,128)(2,1)S(1)}, bf16[32,3,128]{2,1,0:T(4,128)(2,1)S(1)}, u32[]{:S(2)}, u32[]{:S(2)}) collective-permute-start(bf16[32,3,128]{2,1,0:T(4,128)(2,1)S(1)} %get-tuple-element.42), channel_id=1, source_target_pairs={{8,16},{24,32},{40,48},{56,64},{72,80},{88,96},{104,112},{120,128}... | collective-permute-start | bytes 73736 | tf_op jit(solution)/shard_map/ppermute | solution.py:263
  60.9 1.3 %all-to-all-done = bf16[64,9,128]{2,1,0:T(8,128)(2,1)S(1)} async-done(((bf16[64,9,128]{2,1,0:T(8,128)(2,1)}), bf16[64,9,128]{2,1,0:T(8,128)(2,1)S(1)}, u32[]{:S(2)}, u32[]{:S(2)}) %all-to-all-start) | async-done | bytes 147488 | tf_op jit(solution)/shard_map/all_to_all | solution.py:287
  62.2 0.1 convert_reduce_fusion
  62.3 0.7 broadcast_in_dim.7
  62.9 3.3 %collective-permute-start.5 = (bf16[32,3,128]{2,1,0:T(4,128)(2,1)S(1)}, bf16[32,3,128]{2,1,0:T(4,128)(2,1)S(1)}, u32[]{:S(2)}, u32[]{:S(2)}) collective-permute-start(bf16[32,3,128]{2,1,0:T(4,128)(2,1)S(1)} %get-tuple-element.26), channel_id=1, source_target_pairs={{0,8},{16,24},{32,40},{48,56},{64,72},{80,88},{96,104},{112,120},{... | collective-permute-start | bytes 73736 | tf_op jit(solution)/shard_map/ppermute | solution.py:263
  66.2 3.5 %all-to-all-start.1 = ((f32[12,9,128]{2,1,0:T(8,128)}), f32[12,9,128]{2,1,0:T(8,128)S(1)}, u32[]{:S(2)}, u32[]{:S(2)}) async-start(f32[12,9,128]{2,1,0:T(8,128)} %broadcast_in_dim.7), calls=%async_computation.1 | async-start | bytes 196608 | tf_op jit(solution)/shard_map/all_to_all | solution.py:295
  69.8 10.0 %all-to-all-done.1 = f32[12,9,128]{2,1,0:T(8,128)S(1)} async-done(((f32[12,9,128]{2,1,0:T(8,128)}), f32[12,9,128]{2,1,0:T(8,128)S(1)}, u32[]{:S(2)}, u32[]{:S(2)}) %all-to-all-start.1) | async-done | bytes 55328 | tf_op jit(solution)/shard_map/all_to_all | solution.py:295
  79.8 0.7 broadcast_in_dim.8
  80.5 8.2 %all-to-all-start.2 = ((bf16[64,9,128]{2,1,0:T(8,128)(2,1)}), bf16[64,9,128]{2,1,0:T(8,128)(2,1)S(1)}, u32[]{:S(2)}, u32[]{:S(2)}) async-start(bf16[64,9,128]{2,1,0:T(8,128)(2,1)} %broadcast_in_dim.8), calls=%async_computation.2 | async-start | bytes 524288 | tf_op jit(solution)/shard_map/all_to_all | solution.py:300
  88.7 0.4 concatenate.14
  89.1 0.4 concatenate.15
  89.5 3.5 %collective-permute-start.6 = (bf16[3,54,128]{2,1,0:T(8,128)(2,1)S(1)}, bf16[3,54,128]{2,1,0:T(8,128)(2,1)S(1)}, u32[]{:S(2)}, u32[]{:S(2)}) collective-permute-start(bf16[3,54,128]{2,1,0:T(8,128)(2,1)S(1)} %get-tuple-element.44), channel_id=1, source_target_pairs={{1,2},{3,4},{5,6},{2,1},{4,3},{6,5},{9,10},{11,12},{13,14},{10,9},... | collective-permute-start | bytes 124424 | tf_op jit(solution)/shard_map/ppermute | solution.py:263
  93.1 1.9 %collective-permute-start.7 = (bf16[3,54,128]{2,1,0:T(8,128)(2,1)S(1)}, bf16[3,54,128]{2,1,0:T(8,128)(2,1)S(1)}, u32[]{:S(2)}, u32[]{:S(2)}) collective-permute-start(bf16[3,54,128]{2,1,0:T(8,128)(2,1)S(1)} %get-tuple-element.43), channel_id=1, source_target_pairs={{0,1},{2,3},{4,5},{6,7},{1,0},{3,2},{5,4},{7,6},{8,9},{10,11},{12,... | collective-permute-start | bytes 124424 | tf_op jit(solution)/shard_map/ppermute | solution.py:263
  95.0 0.3 broadcast_in_dim.6.ocean
  95.3 1.5 %shard_map.121 = bf16[32,48,128]{2,1,0:T(8,128)(2,1)} custom-call(bf16[1024,256]{1,0:T(8,128)(2,1)S(1)} %get-tuple-element.18.hidden_in, bf16[512,256]{1,0:T(8,128)(2,1)S(1)} %get-tuple-element.22.hidden_st, bf16[32,48,128]{2,1,0:T(8,128)(2,1)S(1)} %get-tuple-element.60.masked, bf16[32,48,128]{2,1,0:T(8,128)(2,1)S(1)} %broadcast_in_dim.6.ocean, ...), custom_call_target="tpu_custom_call" | custom-call | flops 100000000 | bytes 2097152 | tf_op jit(solution)/shard_map/pallas_call | solution.py:231
  96.8 0.4 collective-permute-done.6.lat_b
  97.3 4.1 %shard_map.122 = bf16[32,48,128]{2,1,0:T(8,128)(2,1)} custom-call(s32[2]{0:T(128)S(1)} %pad_add_fusion.flags, bf16[32,32,128]{2,1,0:T(8,128)(2,1)S(1)} %get-tuple-element.23.dz_in, bf16[32,16,128]{2,1,0:T(8,128)(2,1)S(1)} %get-tuple-element.24.dz_st, bf16[32,3,128]{2,1,0:T(4,128)(2,1)S(1)} %collective-permute-done.4.lon_b, ...), custom_call_target="tpu_custom_call" | custom-call | flops 100000000 | bytes 2097152 | tf_op jit(solution)/shard_map/pallas_call | solution.py:231
  101.3 0.8 shard_map.123
  (31 shorter events, 0.3 us)
Async XLA Ops:
  0.6 0.7 copy-start.5
  2.3 15.3 %collective-permute-start = (bf16[3,48,128]{2,1,0:T(8,128)(2,1)S(1)}, bf16[3,48,128]{2,1,0:T(8,128)(2,1)S(1)}, u32[]{:S(2)}, u32[]{:S(2)}) collective-permute-start(bf16[3,48,128]{2,1,0:T(8,128)(2,1)S(1)} %get-tuple-element.32), channel_id=1, source_target_pairs={{1,2},{3,4},{5,6},{2,1},{4,3},{6,5},{9,10},{11,12},{13,14},{10,9},... | collective-permute-start | bytes 110600 | tf_op jit(solution)/shard_map/ppermute | solution.py:263
  6.9 10.7 %collective-permute-start.1 = (bf16[3,48,128]{2,1,0:T(8,128)(2,1)S(1)}, bf16[3,48,128]{2,1,0:T(8,128)(2,1)S(1)}, u32[]{:S(2)}, u32[]{:S(2)}) collective-permute-start(bf16[3,48,128]{2,1,0:T(8,128)(2,1)S(1)} %get-tuple-element.31), channel_id=1, source_target_pairs={{0,1},{2,3},{4,5},{6,7},{1,0},{3,2},{5,4},{7,6},{8,9},{10,11},{12,... | collective-permute-start | bytes 110600 | tf_op jit(solution)/shard_map/ppermute | solution.py:263
  16.8 0.8 copy-start.4
  17.6 16.4 %copy-start = (bf16[256,128]{1,0:T(8,128)(2,1)S(1)}, bf16[256,128]{1,0:T(8,128)(2,1)}, u32[]{:S(2)}) copy-start(bf16[256,128]{1,0:T(8,128)(2,1)} %w_out.5) | copy-start | bytes 196612
  17.6 16.4 %copy-start.1 = (bf16[128,256]{1,0:T(8,128)(2,1)S(1)}, bf16[128,256]{1,0:T(8,128)(2,1)}, u32[]{:S(2)}) copy-start(bf16[128,256]{1,0:T(8,128)(2,1)} %w_in.3) | copy-start | bytes 196612
  17.7 22.6 %collective-permute-start.2 = (bf16[38,3,128]{2,1,0:T(4,128)(2,1)S(1)}, bf16[38,3,128]{2,1,0:T(4,128)(2,1)S(1)}, u32[]{:S(2)}, u32[]{:S(2)}) collective-permute-start(bf16[38,3,128]{2,1,0:T(4,128)(2,1)S(1)} %get-tuple-element.46), channel_id=1, source_target_pairs={{8,16},{24,32},{40,48},{56,64},{72,80},{88,96},{104,112},{120,128}... | collective-permute-start | bytes 87560 | tf_op jit(solution)/shard_map/ppermute | solution.py:263
  32.0 8.4 %collective-permute-start.3 = (bf16[38,3,128]{2,1,0:T(4,128)(2,1)S(1)}, bf16[38,3,128]{2,1,0:T(4,128)(2,1)S(1)}, u32[]{:S(2)}, u32[]{:S(2)}) collective-permute-start(bf16[38,3,128]{2,1,0:T(4,128)(2,1)S(1)} %get-tuple-element.45), channel_id=1, source_target_pairs={{0,8},{16,24},{32,40},{48,56},{64,72},{80,88},{96,104},{112,120},{... | collective-permute-start | bytes 87560 | tf_op jit(solution)/shard_map/ppermute | solution.py:263
  33.9 0.7 copy-start.2
  33.9 0.7 copy-start.3
  44.9 17.2 %all-to-all-start = ((bf16[64,9,128]{2,1,0:T(8,128)(2,1)}), bf16[64,9,128]{2,1,0:T(8,128)(2,1)S(1)}, u32[]{:S(2)}, u32[]{:S(2)}) async-start(bf16[64,9,128]{2,1,0:T(8,128)(2,1)} %get-tuple-element.25), calls=%async_computation | async-start | bytes 524288 | tf_op jit(solution)/shard_map/all_to_all | solution.py:287
  49.8 19.9 %collective-permute-start.4 = (bf16[32,3,128]{2,1,0:T(4,128)(2,1)S(1)}, bf16[32,3,128]{2,1,0:T(4,128)(2,1)S(1)}, u32[]{:S(2)}, u32[]{:S(2)}) collective-permute-start(bf16[32,3,128]{2,1,0:T(4,128)(2,1)S(1)} %get-tuple-element.42), channel_id=1, source_target_pairs={{8,16},{24,32},{40,48},{56,64},{72,80},{88,96},{104,112},{120,128}... | collective-permute-start | bytes 73736 | tf_op jit(solution)/shard_map/ppermute | solution.py:263
  62.9 6.8 %collective-permute-start.5 = (bf16[32,3,128]{2,1,0:T(4,128)(2,1)S(1)}, bf16[32,3,128]{2,1,0:T(4,128)(2,1)S(1)}, u32[]{:S(2)}, u32[]{:S(2)}) collective-permute-start(bf16[32,3,128]{2,1,0:T(4,128)(2,1)S(1)} %get-tuple-element.26), channel_id=1, source_target_pairs={{0,8},{16,24},{32,40},{48,56},{64,72},{80,88},{96,104},{112,120},{... | collective-permute-start | bytes 73736 | tf_op jit(solution)/shard_map/ppermute | solution.py:263
  66.2 13.6 %all-to-all-start.1 = ((f32[12,9,128]{2,1,0:T(8,128)}), f32[12,9,128]{2,1,0:T(8,128)S(1)}, u32[]{:S(2)}, u32[]{:S(2)}) async-start(f32[12,9,128]{2,1,0:T(8,128)} %broadcast_in_dim.7), calls=%async_computation.1 | async-start | bytes 196608 | tf_op jit(solution)/shard_map/all_to_all | solution.py:295
  80.5 20.8 %all-to-all-start.2 = ((bf16[64,9,128]{2,1,0:T(8,128)(2,1)}), bf16[64,9,128]{2,1,0:T(8,128)(2,1)S(1)}, u32[]{:S(2)}, u32[]{:S(2)}) async-start(bf16[64,9,128]{2,1,0:T(8,128)(2,1)} %broadcast_in_dim.8), calls=%async_computation.2 | async-start | bytes 524288 | tf_op jit(solution)/shard_map/all_to_all | solution.py:300
  89.5 7.7 %collective-permute-start.6 = (bf16[3,54,128]{2,1,0:T(8,128)(2,1)S(1)}, bf16[3,54,128]{2,1,0:T(8,128)(2,1)S(1)}, u32[]{:S(2)}, u32[]{:S(2)}) collective-permute-start(bf16[3,54,128]{2,1,0:T(8,128)(2,1)S(1)} %get-tuple-element.44), channel_id=1, source_target_pairs={{1,2},{3,4},{5,6},{2,1},{4,3},{6,5},{9,10},{11,12},{13,14},{10,9},... | collective-permute-start | bytes 124424 | tf_op jit(solution)/shard_map/ppermute | solution.py:263
  93.1 4.2 %collective-permute-start.7 = (bf16[3,54,128]{2,1,0:T(8,128)(2,1)S(1)}, bf16[3,54,128]{2,1,0:T(8,128)(2,1)S(1)}, u32[]{:S(2)}, u32[]{:S(2)}) collective-permute-start(bf16[3,54,128]{2,1,0:T(8,128)(2,1)S(1)} %get-tuple-element.43), channel_id=1, source_target_pairs={{0,1},{2,3},{4,5},{6,7},{1,0},{3,2},{5,4},{7,6},{8,9},{10,11},{12,... | collective-permute-start | bytes 124424 | tf_op jit(solution)/shard_map/ppermute | solution.py:263

commit v7 on v6

--- a/solution.py
+++ b/solution.py
@@ -345,15 +345,18 @@
     (advanced,) = call(
         advance_kernel, (hidden_in, hidden_st, masked, ocean_b, w_out), [CELLS], [], 100_000_000
     )
-    near, copies = lax.optimization_barrier((jnp.where(even, high, low), copies))
+    near = jnp.where(even, high, low)
     lon_a = swap(near, LON, group_size(LON), 0, True)
+    lon_a, lon_b, dz_in, advanced, total = lax.optimization_barrier(
+        (lon_a, lon_b, dz_in, advanced, inner_sum(copies))
+    )
     west, east = jnp.where(even, lon_b, lon_a), jnp.where(even, lon_a, lon_b)
 
     def full(rows):
         return jnp.concatenate([west[rows], dz_st[rows, :8], dz_in[rows], dz_st[rows, 8:], east[rows]], axis=1)
 
     lat = exchange(full(slice(0, 3)), full(slice(ROWS - 3, ROWS)), LAT, group_size(LAT), False)
-    sums = hand_out(inner_sum(copies))
+    sums = hand_out(total)
     (field_grad,) = call(
         back_kernel, (flags, dz_in, dz_st, lon_b, lon_a, *lat, gmask, ocean_b, taps), [CELLS], [PADDED], 100_000_000
     )

time: 103 us -> 99.4 us (0.965)
  starting transfers between devices: 65.6 us -> 63.1 us
    ppermute x8, waiting for transfers between devices: 0.43 us -> 2.25 us  [swap(): return lax.ppermute(values, axes, pairs)]
    all_to_all x1, waiting for transfers between devices: 9.95 us -> 8.56 us  [inner_sum(): lax.all_to_all(copies, INNER, 0, 0, tiled=True)]
    ppermute x8, starting transfers between devices: 49.1 us -> 47.8 us  [swap(): return lax.ppermute(values, axes, pairs)]
    all_to_all x1, waiting for transfers between devices: 1.26 us -> 0.01 us  [scatter_sum(): lax.all_to_all(parts, OUTER, 0, 0, tiled=True).astype(jnp.float32)]
    all_to_all x1, starting transfers between devices: 8.18 us -> 6.97 us  [hand_out(): return lax.all_to_all(spread, OUTER, 0, 0, tiled=True)]
  transfers between devices with their start and end apart: 11 -> 11, of which waited for: 3 -> 2; matrix products, arithmetic and copies ran while one was open for 3% -> 3% of each run, Pallas kernels for 11% -> 11%
where the time goes in v7:
time: 99.4 us; the launch traced here: 98.7 us
  starting transfers between devices  63.1 us (63%)
  Pallas kernels  16.7 us (17%)
  waiting for transfers between devices  10.8 us (11%)
  local copies, waits for them, and re-layouts  4.51 us (5%)
  other arithmetic  2.63 us (3%)
    ppermute x8, starting transfers between devices, swap(): return lax.ppermute(values, axes, pairs)  47.8 us
    pallas_call x5, Pallas kernels, call(): pl.pallas_call(body, out_shape=outs, in_specs=[smem if a.dtype == jnp.int...  16.7 us
    all_to_all x1, waiting for transfers between devices, inner_sum(): lax.all_to_all(copies, INNER, 0, 0, tiled=True)  8.56 us
    all_to_all x1, starting transfers between devices, hand_out(): return lax.all_to_all(spread, OUTER, 0, 0, tiled=True)  6.97 us
    all_to_all x1, starting transfers between devices, scatter_sum(): lax.all_to_all(parts, OUTER, 0, 0, tiled=True).astype(jnp.float32)  4.83 us
    all_to_all x1, starting transfers between devices, inner_sum(): lax.all_to_all(copies, INNER, 0, 0, tiled=True)  3.51 us
    ppermute x8, waiting for transfers between devices, swap(): return lax.ppermute(values, axes, pairs)  2.25 us
  transfers between devices with their start and end apart: 11, of which 2 were waited for; matrix products, arithmetic and copies ran while one was open for 3% of the time, Pallas kernels for 11%

profile of v7, /device:TPU:1, one launch (start us, length us, event | category | flops | bytes accessed | tf_op | source)
XLA Modules:
  0.0 98.7 jit_solution(336805663974701091)
XLA Ops:
  0.7 0.7 copy-done.5
  1.4 0.9 broadcast_select_fusion.6
  2.3 4.6 %collective-permute-start = (bf16[3,48,128]{2,1,0:T(8,128)(2,1)S(1)}, bf16[3,48,128]{2,1,0:T(8,128)(2,1)S(1)}, u32[]{:S(2)}, u32[]{:S(2)}) collective-permute-start(bf16[3,48,128]{2,1,0:T(8,128)(2,1)S(1)} %get-tuple-element.38), channel_id=1, source_target_pairs={{1,2},{3,4},{5,6},{2,1},{4,3},{6,5},{9,10},{11,12},{13,14},{10,9},... | collective-permute-start | bytes 110600 | tf_op jit(solution)/shard_map/ppermute | solution.py:263
  6.9 8.5 %collective-permute-start.1 = (bf16[3,48,128]{2,1,0:T(8,128)(2,1)S(1)}, bf16[3,48,128]{2,1,0:T(8,128)(2,1)S(1)}, u32[]{:S(2)}, u32[]{:S(2)}) collective-permute-start(bf16[3,48,128]{2,1,0:T(8,128)(2,1)S(1)} %get-tuple-element.37), channel_id=1, source_target_pairs={{0,1},{2,3},{4,5},{6,7},{1,0},{3,2},{5,4},{7,6},{8,9},{10,11},{12,... | collective-permute-start | bytes 110600 | tf_op jit(solution)/shard_map/ppermute | solution.py:263
  15.4 1.4 %broadcast_multiply_fusion = (bf16[32,48,128]{2,1,0:T(8,128)(2,1)S(1)}, bf16[32,48,128]{2,1,0:T(8,128)(2,1)S(1)}) fusion(bf16[32,48,128]{2,1,0:T(8,128)(2,1)} %param.10, bf16[32,48]{1,0:T(8,128)(2,1)S(1)} %convert_element_type.11, bf16[32,48,128]{2,1,0:T(8,128)(2,1)} %param.8), kind=kLoop, calls=%fused_computation.1 | loop fusion | flops 393216 | bytes 1575936 | tf_op jit(solution)/shard_map/mul | solution.py:315
  16.8 0.1 pad_add_fusion.flags
  16.9 0.6 copy-done.4
  17.6 0.0 copy-start.1
  17.6 0.1 broadcast_select_fusion.2
  17.7 14.3 %collective-permute-start.2 = (bf16[38,3,128]{2,1,0:T(4,128)(2,1)S(1)}, bf16[38,3,128]{2,1,0:T(4,128)(2,1)S(1)}, u32[]{:S(2)}, u32[]{:S(2)}) collective-permute-start(bf16[38,3,128]{2,1,0:T(4,128)(2,1)S(1)} %get-tuple-element.52), channel_id=1, source_target_pairs={{8,16},{24,32},{40,48},{56,64},{72,80},{88,96},{104,112},{120,128}... | collective-permute-start | bytes 87560 | tf_op jit(solution)/shard_map/ppermute | solution.py:263
  32.0 1.9 %collective-permute-start.3 = (bf16[38,3,128]{2,1,0:T(4,128)(2,1)S(1)}, bf16[38,3,128]{2,1,0:T(4,128)(2,1)S(1)}, u32[]{:S(2)}, u32[]{:S(2)}) collective-permute-start(bf16[38,3,128]{2,1,0:T(4,128)(2,1)S(1)} %get-tuple-element.51), channel_id=1, source_target_pairs={{0,8},{16,24},{32,40},{48,56},{64,72},{80,88},{96,104},{112,120},{... | collective-permute-start | bytes 87560 | tf_op jit(solution)/shard_map/ppermute | solution.py:263
  33.9 0.6 copy-done.2
  34.6 5.7 %shard_map.119 = (bf16[1024,256]{1,0:T(8,128)(2,1)S(1)}, bf16[32,32,128]{2,1,0:T(8,128)(2,1)S(1)}, f32[128,256]{1,0:T(8,128)S(1)}, f32[128,256]{1,0:T(8,128)S(1)}, f32[49,8,128]{2,1,0:T(8,128)S(1)}) custom-call(s32[2]{0:T(128)S(1)} %pad_add_fusion.flags, bf16[32,48,128]{2,1,0:T(8,128)(2,1)S(1)} %get-tuple-element.66.masked, ...), custom_call_target="tpu_custom_call" | custom-call | flops 350000000 | bytes 2097152 | tf_op jit(solution)/shard_map/pallas_call | solution.py:231
  40.3 4.6 %shard_map.120 = (bf16[512,256]{1,0:T(8,128)(2,1)S(1)}, bf16[32,16,128]{2,1,0:T(8,128)(2,1)S(1)}, bf16[64,9,128]{2,1,0:T(8,128)(2,1)}) custom-call(s32[2]{0:T(128)S(1)} %pad_add_fusion.flags, bf16[32,48,128]{2,1,0:T(8,128)(2,1)S(1)} %get-tuple-element.66.masked, bf16[3,48,128]{2,1,0:T(8,128)(2,1)S(1)} %collective-permute-done.lat_b, ...), custom_call_target="tpu_custom_call" | custom-call | flops 170000000 | bytes 2097152 | tf_op jit(solution)/shard_map/pallas_call | solution.py:231
  44.9 4.8 %all-to-all-start = ((bf16[64,9,128]{2,1,0:T(8,128)(2,1)}), bf16[64,9,128]{2,1,0:T(8,128)(2,1)S(1)}, u32[]{:S(2)}, u32[]{:S(2)}) async-start(bf16[64,9,128]{2,1,0:T(8,128)(2,1)} %get-tuple-element.28), calls=%async_computation | async-start | bytes 524288 | tf_op jit(solution)/shard_map/all_to_all | solution.py:287
  49.8 3.6 %collective-permute-start.4 = (bf16[32,3,128]{2,1,0:T(4,128)(2,1)S(1)}, bf16[32,3,128]{2,1,0:T(4,128)(2,1)S(1)}, u32[]{:S(2)}, u32[]{:S(2)}) collective-permute-start(bf16[32,3,128]{2,1,0:T(4,128)(2,1)S(1)} %get-tuple-element.48), channel_id=1, source_target_pairs={{0,8},{16,24},{32,40},{48,56},{64,72},{80,88},{96,104},{112,120},{... | collective-permute-start | bytes 73736 | tf_op jit(solution)/shard_map/ppermute | solution.py:263
  53.4 9.4 %collective-permute-start.5 = (bf16[32,3,128]{2,1,0:T(4,128)(2,1)S(1)}, bf16[32,3,128]{2,1,0:T(4,128)(2,1)S(1)}, u32[]{:S(2)}, u32[]{:S(2)}) collective-permute-start(bf16[32,3,128]{2,1,0:T(4,128)(2,1)S(1)} %get-tuple-element.47), channel_id=1, source_target_pairs={{8,16},{24,32},{40,48},{56,64},{72,80},{88,96},{104,112},{120,128}... | collective-permute-start | bytes 73736 | tf_op jit(solution)/shard_map/ppermute | solution.py:263
  62.8 0.1 convert_reduce_fusion
  62.9 0.7 broadcast_in_dim.7
  63.6 3.5 %all-to-all-start.1 = ((f32[12,9,128]{2,1,0:T(8,128)}), f32[12,9,128]{2,1,0:T(8,128)S(1)}, u32[]{:S(2)}, u32[]{:S(2)}) async-start(f32[12,9,128]{2,1,0:T(8,128)} %broadcast_in_dim.7), calls=%async_computation.1 | async-start | bytes 196608 | tf_op jit(solution)/shard_map/all_to_all | solution.py:295
  67.1 0.3 broadcast_in_dim.6.ocean
  67.4 1.5 %shard_map.121 = bf16[32,48,128]{2,1,0:T(8,128)(2,1)} custom-call(bf16[1024,256]{1,0:T(8,128)(2,1)S(1)} %get-tuple-element.26.hidden_in, bf16[512,256]{1,0:T(8,128)(2,1)S(1)} %get-tuple-element.27.hidden_st, bf16[32,48,128]{2,1,0:T(8,128)(2,1)S(1)} %get-tuple-element.66.masked, bf16[32,48,128]{2,1,0:T(8,128)(2,1)S(1)} %broadcast_in_dim.6.ocean, ...), custom_call_target="tpu_custom_call" | custom-call | flops 100000000 | bytes 2097152 | tf_op jit(solution)/shard_map/pallas_call | solution.py:231
  68.9 8.6 %all-to-all-done.1 = f32[12,9,128]{2,1,0:T(8,128)S(1)} async-done(((f32[12,9,128]{2,1,0:T(8,128)}), f32[12,9,128]{2,1,0:T(8,128)S(1)}, u32[]{:S(2)}, u32[]{:S(2)}) %all-to-all-start.1) | async-done | bytes 55328 | tf_op jit(solution)/shard_map/all_to_all | solution.py:295
  77.6 0.7 broadcast_in_dim.8
  78.3 7.0 %all-to-all-start.2 = ((bf16[64,9,128]{2,1,0:T(8,128)(2,1)}), bf16[64,9,128]{2,1,0:T(8,128)(2,1)S(1)}, u32[]{:S(2)}, u32[]{:S(2)}) async-start(bf16[64,9,128]{2,1,0:T(8,128)(2,1)} %broadcast_in_dim.8), calls=%async_computation.2 | async-start | bytes 524288 | tf_op jit(solution)/shard_map/all_to_all | solution.py:300
  85.3 0.4 concatenate.14
  85.7 0.4 concatenate.15
  86.1 3.5 %collective-permute-start.6 = (bf16[3,54,128]{2,1,0:T(8,128)(2,1)S(1)}, bf16[3,54,128]{2,1,0:T(8,128)(2,1)S(1)}, u32[]{:S(2)}, u32[]{:S(2)}) collective-permute-start(bf16[3,54,128]{2,1,0:T(8,128)(2,1)S(1)} %get-tuple-element.50), channel_id=1, source_target_pairs={{1,2},{3,4},{5,6},{2,1},{4,3},{6,5},{9,10},{11,12},{13,14},{10,9},... | collective-permute-start | bytes 124424 | tf_op jit(solution)/shard_map/ppermute | solution.py:263
  89.7 1.9 %collective-permute-start.7 = (bf16[3,54,128]{2,1,0:T(8,128)(2,1)S(1)}, bf16[3,54,128]{2,1,0:T(8,128)(2,1)S(1)}, u32[]{:S(2)}, u32[]{:S(2)}) collective-permute-start(bf16[3,54,128]{2,1,0:T(8,128)(2,1)S(1)} %get-tuple-element.49), channel_id=1, source_target_pairs={{0,1},{2,3},{4,5},{6,7},{1,0},{3,2},{5,4},{7,6},{8,9},{10,11},{12,... | collective-permute-start | bytes 124424 | tf_op jit(solution)/shard_map/ppermute | solution.py:263
  91.6 2.2 %collective-permute-done.6.lat_b = bf16[3,54,128]{2,1,0:T(8,128)(2,1)S(1)} collective-permute-done((bf16[3,54,128]{2,1,0:T(8,128)(2,1)S(1)}, bf16[3,54,128]{2,1,0:T(8,128)(2,1)S(1)}, u32[]{:S(2)}, u32[]{:S(2)}) %collective-permute-start.6) | collective-permute-done | bytes 41504 | tf_op jit(solution)/shard_map/ppermute | solution.py:263
  93.9 4.0 %shard_map.122 = bf16[32,48,128]{2,1,0:T(8,128)(2,1)} custom-call(s32[2]{0:T(128)S(1)} %pad_add_fusion.flags, bf16[32,32,128]{2,1,0:T(8,128)(2,1)S(1)} %get-tuple-element.30.dz_in, bf16[32,16,128]{2,1,0:T(8,128)(2,1)S(1)} %get-tuple-element.24.dz_st, bf16[32,3,128]{2,1,0:T(4,128)(2,1)S(1)} %collective-permute-done.5.lon_b, ...), custom_call_target="tpu_custom_call" | custom-call | flops 100000000 | bytes 2097152 | tf_op jit(solution)/shard_map/pallas_call | solution.py:231
  97.9 0.8 shard_map.123
  (31 shorter events, 0.3 us)
Async XLA Ops:
  0.6 0.7 copy-start.5
  2.3 15.3 %collective-permute-start = (bf16[3,48,128]{2,1,0:T(8,128)(2,1)S(1)}, bf16[3,48,128]{2,1,0:T(8,128)(2,1)S(1)}, u32[]{:S(2)}, u32[]{:S(2)}) collective-permute-start(bf16[3,48,128]{2,1,0:T(8,128)(2,1)S(1)} %get-tuple-element.38), channel_id=1, source_target_pairs={{1,2},{3,4},{5,6},{2,1},{4,3},{6,5},{9,10},{11,12},{13,14},{10,9},... | collective-permute-start | bytes 110600 | tf_op jit(solution)/shard_map/ppermute | solution.py:263
  6.9 10.7 %collective-permute-start.1 = (bf16[3,48,128]{2,1,0:T(8,128)(2,1)S(1)}, bf16[3,48,128]{2,1,0:T(8,128)(2,1)S(1)}, u32[]{:S(2)}, u32[]{:S(2)}) collective-permute-start(bf16[3,48,128]{2,1,0:T(8,128)(2,1)S(1)} %get-tuple-element.37), channel_id=1, source_target_pairs={{0,1},{2,3},{4,5},{6,7},{1,0},{3,2},{5,4},{7,6},{8,9},{10,11},{12,... | collective-permute-start | bytes 110600 | tf_op jit(solution)/shard_map/ppermute | solution.py:263
  16.8 0.8 copy-start.4
  17.6 16.4 %copy-start = (bf16[256,128]{1,0:T(8,128)(2,1)S(1)}, bf16[256,128]{1,0:T(8,128)(2,1)}, u32[]{:S(2)}) copy-start(bf16[256,128]{1,0:T(8,128)(2,1)} %w_out.5) | copy-start | bytes 196612
  17.6 16.4 %copy-start.1 = (bf16[128,256]{1,0:T(8,128)(2,1)S(1)}, bf16[128,256]{1,0:T(8,128)(2,1)}, u32[]{:S(2)}) copy-start(bf16[128,256]{1,0:T(8,128)(2,1)} %w_in.3) | copy-start | bytes 196612
  17.7 22.6 %collective-permute-start.2 = (bf16[38,3,128]{2,1,0:T(4,128)(2,1)S(1)}, bf16[38,3,128]{2,1,0:T(4,128)(2,1)S(1)}, u32[]{:S(2)}, u32[]{:S(2)}) collective-permute-start(bf16[38,3,128]{2,1,0:T(4,128)(2,1)S(1)} %get-tuple-element.52), channel_id=1, source_target_pairs={{8,16},{24,32},{40,48},{56,64},{72,80},{88,96},{104,112},{120,128}... | collective-permute-start | bytes 87560 | tf_op jit(solution)/shard_map/ppermute | solution.py:263
  32.0 8.3 %collective-permute-start.3 = (bf16[38,3,128]{2,1,0:T(4,128)(2,1)S(1)}, bf16[38,3,128]{2,1,0:T(4,128)(2,1)S(1)}, u32[]{:S(2)}, u32[]{:S(2)}) collective-permute-start(bf16[38,3,128]{2,1,0:T(4,128)(2,1)S(1)} %get-tuple-element.51), channel_id=1, source_target_pairs={{0,8},{16,24},{32,40},{48,56},{64,72},{80,88},{96,104},{112,120},{... | collective-permute-start | bytes 87560 | tf_op jit(solution)/shard_map/ppermute | solution.py:263
  33.9 0.7 copy-start.2
  33.9 0.7 copy-start.3
  44.9 17.9 %all-to-all-start = ((bf16[64,9,128]{2,1,0:T(8,128)(2,1)}), bf16[64,9,128]{2,1,0:T(8,128)(2,1)S(1)}, u32[]{:S(2)}, u32[]{:S(2)}) async-start(bf16[64,9,128]{2,1,0:T(8,128)(2,1)} %get-tuple-element.28), calls=%async_computation | async-start | bytes 524288 | tf_op jit(solution)/shard_map/all_to_all | solution.py:287
  49.8 27.7 %collective-permute-start.4 = (bf16[32,3,128]{2,1,0:T(4,128)(2,1)S(1)}, bf16[32,3,128]{2,1,0:T(4,128)(2,1)S(1)}, u32[]{:S(2)}, u32[]{:S(2)}) collective-permute-start(bf16[32,3,128]{2,1,0:T(4,128)(2,1)S(1)} %get-tuple-element.48), channel_id=1, source_target_pairs={{0,8},{16,24},{32,40},{48,56},{64,72},{80,88},{96,104},{112,120},{... | collective-permute-start | bytes 73736 | tf_op jit(solution)/shard_map/ppermute | solution.py:263
  53.4 24.1 %collective-permute-start.5 = (bf16[32,3,128]{2,1,0:T(4,128)(2,1)S(1)}, bf16[32,3,128]{2,1,0:T(4,128)(2,1)S(1)}, u32[]{:S(2)}, u32[]{:S(2)}) collective-permute-start(bf16[32,3,128]{2,1,0:T(4,128)(2,1)S(1)} %get-tuple-element.47), channel_id=1, source_target_pairs={{8,16},{24,32},{40,48},{56,64},{72,80},{88,96},{104,112},{120,128}... | collective-permute-start | bytes 73736 | tf_op jit(solution)/shard_map/ppermute | solution.py:263
  63.6 13.9 %all-to-all-start.1 = ((f32[12,9,128]{2,1,0:T(8,128)}), f32[12,9,128]{2,1,0:T(8,128)S(1)}, u32[]{:S(2)}, u32[]{:S(2)}) async-start(f32[12,9,128]{2,1,0:T(8,128)} %broadcast_in_dim.7), calls=%async_computation.1 | async-start | bytes 196608 | tf_op jit(solution)/shard_map/all_to_all | solution.py:295
  78.3 19.6 %all-to-all-start.2 = ((bf16[64,9,128]{2,1,0:T(8,128)(2,1)}), bf16[64,9,128]{2,1,0:T(8,128)(2,1)S(1)}, u32[]{:S(2)}, u32[]{:S(2)}) async-start(bf16[64,9,128]{2,1,0:T(8,128)(2,1)} %broadcast_in_dim.8), calls=%async_computation.2 | async-start | bytes 524288 | tf_op jit(solution)/shard_map/all_to_all | solution.py:300
  86.1 7.7 %collective-permute-start.6 = (bf16[3,54,128]{2,1,0:T(8,128)(2,1)S(1)}, bf16[3,54,128]{2,1,0:T(8,128)(2,1)S(1)}, u32[]{:S(2)}, u32[]{:S(2)}) collective-permute-start(bf16[3,54,128]{2,1,0:T(8,128)(2,1)S(1)} %get-tuple-element.50), channel_id=1, source_target_pairs={{1,2},{3,4},{5,6},{2,1},{4,3},{6,5},{9,10},{11,12},{13,14},{10,9},... | collective-permute-start | bytes 124424 | tf_op jit(solution)/shard_map/ppermute | solution.py:263
  89.7 4.2 %collective-permute-start.7 = (bf16[3,54,128]{2,1,0:T(8,128)(2,1)S(1)}, bf16[3,54,128]{2,1,0:T(8,128)(2,1)S(1)}, u32[]{:S(2)}, u32[]{:S(2)}) collective-permute-start(bf16[3,54,128]{2,1,0:T(8,128)(2,1)S(1)} %get-tuple-element.49), channel_id=1, source_target_pairs={{0,1},{2,3},{4,5},{6,7},{1,0},{3,2},{5,4},{7,6},{8,9},{10,11},{12,... | collective-permute-start | bytes 124424 | tf_op jit(solution)/shard_map/ppermute | solution.py:263

commit v8 on v7

--- a/solution.py
+++ b/solution.py
@@ -55,9 +55,8 @@
                 for out in range(step):
                     tap = row - out
                     if 0 <= tap < 7:
-                        at = tap * 7 + col
-                        at = 48 - at if flip else at
-                        sums[out][seg] = sums[out][seg] + cells * taps[at : at + 1, :]
+                        a, b = (6 - tap, 6 - col) if flip else (tap, col)
+                        sums[out][seg] = sums[out][seg] + cells * taps[a, b : b + 1, :]
     return jnp.concatenate([part for line in sums for part in line], axis=0)
 
 
@@ -77,7 +76,9 @@
 
 def main_rows(step, segs, outs, pads, gmask, params, hidden_out, dz_out, sums, index):
     f32, bf16 = jnp.float32, jnp.bfloat16
-    taps, gain, w_in, b_in, w_out = params
+    taps, vectors, w_in, w_out = params
+    gain = vectors[0:1, :]
+    b_in = jnp.concatenate([vectors[1:2, :], vectors[2:3, :]], axis=1)
     acc_in, acc_out, acc_tap = sums
     first = index * step
     z = conv_rows(pads, taps, first, step, False)
@@ -86,8 +87,8 @@
     centre = z - average
     inverse = lax.rsqrt(jnp.mean(centre * centre, axis=-1, keepdims=True) + 1e-06)
     unit = centre * inverse
-    normed = (unit * gain[...]).astype(bf16)
-    preact = jnp.dot(normed, w_in[...], preferred_element_type=f32) + b_in[...]
+    normed = (unit * gain).astype(bf16)
+    preact = jnp.dot(normed, w_in[...], preferred_element_type=f32) + b_in
     cdf = 0.5 * (1.0 + lax.erf(preact * 0.7071067811865476))
     hidden = (preact * cdf).astype(bf16)
     hidden_out[pl.ds(index * hidden.shape[0], hidden.shape[0]), :] = hidden
@@ -98,7 +99,7 @@
     acc_out[...] += lax.dot_general(grad, hidden, contract, preferred_element_type=f32)
     acc_in[...] += lax.dot_general(normed, d_pre, contract, preferred_element_type=f32)
     d_norm = lax.dot_general(d_pre, w_in[...], (((1,), (1,)), ((), ())), preferred_element_type=f32)
-    scaled = d_norm * gain[...]
+    scaled = d_norm * gain
     dz = inverse * (
         scaled
         - jnp.mean(scaled, axis=-1, keepdims=True)
@@ -123,13 +124,13 @@
 
 
 def inside_kernel(
-    flags, masked, lat_b, lat_a, gmask, taps, gain, w_in, b_in, w_out,
+    flags, masked, lat_b, lat_a, gmask, taps, vectors, w_in, w_out,
     hidden, dz_out, acc_in, acc_out, acc_tap, pad,
 ):
     fill_rows(pad, masked, flags, lat_a, lat_b, 0, COLS, 0)
     for acc in (acc_in, acc_out, acc_tap):
         acc[...] = jnp.zeros_like(acc)
-    params = (taps, gain, w_in, b_in, w_out)
+    params = (taps, vectors, w_in, w_out)
     sums = (acc_in, acc_out, acc_tap)
 
     def block(index, carry):
@@ -140,7 +141,7 @@
 
 
 def strips_kernel(
-    flags, masked, lat_b, lat_a, lon_b, lon_a, gmask, taps, gain, w_in, b_in, w_out,
+    flags, masked, lat_b, lat_a, lon_b, lon_a, gmask, taps, vectors, w_in, w_out,
     had_in, had_out, had_tap,
     hidden, dz_out, terms, left, right, acc_in, acc_out, acc_tap,
 ):
@@ -148,7 +149,7 @@
     acc_in[...] = had_in[...]
     acc_out[...] = had_out[...]
     acc_tap[...] = had_tap[...]
-    params = (taps, gain, w_in, b_in, w_out)
+    params = (taps, vectors, w_in, w_out)
     pads = ((left, 5, 8), (right, 5, 8))
     main_rows(ROWS, STRIPS, STRIPS_OUT, pads, gmask, params, hidden, dz_out, (acc_in, acc_out, acc_tap), 0)
     half = C // 8
@@ -288,11 +289,12 @@
 
 
 def inner_copies(own):
-    return jnp.broadcast_to(own[None], (group_size(INNER), *own.shape))
+    return jnp.broadcast_to(own.astype(LINK)[None], (group_size(INNER), *own.shape))
 
 
 def inner_sum(copies):
-    return jnp.sum(lax.all_to_all(copies, INNER, 0, 0, tiled=True), axis=0).astype(LINK)
+    parts = lax.all_to_all(copies, INNER, 0, 0, tiled=True).astype(jnp.float32)
+    return jnp.sum(parts, axis=0).astype(LINK)
 
 
 def hand_out(total):
@@ -302,8 +304,8 @@
 
 def shards(fields, ocean, cotangent, kernel, ln_gain, w_in, b_in, w_out):
     flags = jnp.stack([lax.axis_index(LAT[-1]) % 2, lax.axis_index(LON[-1]) % 2]).astype(jnp.int32)
-    taps = kernel.reshape(49, C)
-    params = (taps, ln_gain.reshape(1, C), w_in, b_in.reshape(1, FF), w_out)
+    vectors = jnp.concatenate([ln_gain.reshape(1, C), b_in.reshape(2, C)])
+    params = (kernel, vectors, w_in, w_out)
 
     def edge(rows, cols):
         return fields[rows, cols] * ocean[rows, cols].astype(jnp.bfloat16)[..., None]
@@ -358,7 +360,7 @@
     lat = exchange(full(slice(0, 3)), full(slice(ROWS - 3, ROWS)), LAT, group_size(LAT), False)
     sums = hand_out(total)
     (field_grad,) = call(
-        back_kernel, (flags, dz_in, dz_st, lon_b, lon_a, *lat, gmask, ocean_b, taps), [CELLS], [PADDED], 100_000_000
+        back_kernel, (flags, dz_in, dz_st, lon_b, lon_a, *lat, gmask, ocean_b, kernel), [CELLS], [PADDED], 100_000_000
     )
     cells = ROWS * COLS * group_size(LAT) * group_size(LON)
     kernel_grad, w_in_grad, w_out_grad = call(

time: 99.4 us -> 97.7 us (0.983)
  transfers between devices with their start and end apart: 11 -> 11, of which waited for: 2 -> 2; matrix products, arithmetic and copies ran while one was open for 3% -> 3% of each run, Pallas kernels for 11% -> 12%
where the time goes in v8:
time: 97.7 us; the launch traced here: 97 us
  starting transfers between devices  62.8 us (64%)
  Pallas kernels  16.7 us (17%)
  waiting for transfers between devices  10 us (10%)
  local copies, waits for them, and re-layouts  3.89 us (4%)
  other arithmetic  2.64 us (3%)
  between operations  0.98 us (1%)
    ppermute x8, starting transfers between devices, swap(): return lax.ppermute(values, axes, pairs)  48.4 us
    pallas_call x5, Pallas kernels, call(): pl.pallas_call(body, out_shape=outs, in_specs=[smem if a.dtype == jnp.int...  16.7 us
    all_to_all x1, waiting for transfers between devices, inner_sum(): parts = lax.all_to_all(copies, INNER, 0, 0, tiled=True).astype(jnp.float32)  7.76 us
    all_to_all x1, starting transfers between devices, hand_out(): return lax.all_to_all(spread, OUTER, 0, 0, tiled=True)  6.07 us
    all_to_all x1, starting transfers between devices, scatter_sum(): lax.all_to_all(parts, OUTER, 0, 0, tiled=True).astype(jnp.float32)  4.83 us
    all_to_all x1, starting transfers between devices, inner_sum(): parts = lax.all_to_all(copies, INNER, 0, 0, tiled=True).astype(jnp.float32)  3.5 us
    ppermute x8, waiting for transfers between devices, swap(): return lax.ppermute(values, axes, pairs)  2.25 us
  transfers between devices with their start and end apart: 11, of which 2 were waited for; matrix products, arithmetic and copies ran while one was open for 3% of the time, Pallas kernels for 12%

profile of v8, /device:TPU:1, one launch (start us, length us, event | category | flops | bytes accessed | tf_op | source)
XLA Modules:
  0.0 97.0 jit_solution(16592310970281597807)
XLA Ops:
  0.7 0.7 copy-done.3
  1.4 0.9 broadcast_select_fusion.6
  2.3 4.6 %collective-permute-start = (bf16[3,48,128]{2,1,0:T(8,128)(2,1)S(1)}, bf16[3,48,128]{2,1,0:T(8,128)(2,1)S(1)}, u32[]{:S(2)}, u32[]{:S(2)}) collective-permute-start(bf16[3,48,128]{2,1,0:T(8,128)(2,1)S(1)} %get-tuple-element.38), channel_id=1, source_target_pairs={{1,2},{3,4},{5,6},{2,1},{4,3},{6,5},{9,10},{11,12},{13,14},{10,9},... | collective-permute-start | bytes 110600 | tf_op jit(solution)/shard_map/ppermute | solution.py:264
  6.9 8.5 %collective-permute-start.1 = (bf16[3,48,128]{2,1,0:T(8,128)(2,1)S(1)}, bf16[3,48,128]{2,1,0:T(8,128)(2,1)S(1)}, u32[]{:S(2)}, u32[]{:S(2)}) collective-permute-start(bf16[3,48,128]{2,1,0:T(8,128)(2,1)S(1)} %get-tuple-element.37), channel_id=1, source_target_pairs={{0,1},{2,3},{4,5},{6,7},{1,0},{3,2},{5,4},{7,6},{8,9},{10,11},{12,... | collective-permute-start | bytes 110600 | tf_op jit(solution)/shard_map/ppermute | solution.py:264
  15.4 1.4 %broadcast_multiply_fusion = (bf16[32,48,128]{2,1,0:T(8,128)(2,1)S(1)}, bf16[32,48,128]{2,1,0:T(8,128)(2,1)S(1)}) fusion(bf16[32,48,128]{2,1,0:T(8,128)(2,1)} %param.10, bf16[32,48]{1,0:T(8,128)(2,1)S(1)} %convert_element_type.2, bf16[32,48,128]{2,1,0:T(8,128)(2,1)} %param.8), kind=kLoop, calls=%fused_computation | loop fusion | flops 393216 | bytes 1575936 | tf_op jit(solution)/shard_map/mul | solution.py:317
  16.8 0.0 copy-start.4
  16.8 0.0 copy-start.5
  16.8 0.7 copy-done.4
  17.5 0.1 pad_add_fusion.flags
  17.7 0.1 broadcast_select_fusion.2
  17.7 14.3 %collective-permute-start.2 = (bf16[38,3,128]{2,1,0:T(4,128)(2,1)S(1)}, bf16[38,3,128]{2,1,0:T(4,128)(2,1)S(1)}, u32[]{:S(2)}, u32[]{:S(2)}) collective-permute-start(bf16[38,3,128]{2,1,0:T(4,128)(2,1)S(1)} %get-tuple-element.52), channel_id=1, source_target_pairs={{8,16},{24,32},{40,48},{56,64},{72,80},{88,96},{104,112},{120,128}... | collective-permute-start | bytes 87560 | tf_op jit(solution)/shard_map/ppermute | solution.py:264
  32.0 1.9 %collective-permute-start.3 = (bf16[38,3,128]{2,1,0:T(4,128)(2,1)S(1)}, bf16[38,3,128]{2,1,0:T(4,128)(2,1)S(1)}, u32[]{:S(2)}, u32[]{:S(2)}) collective-permute-start(bf16[38,3,128]{2,1,0:T(4,128)(2,1)S(1)} %get-tuple-element.51), channel_id=1, source_target_pairs={{0,8},{16,24},{32,40},{48,56},{64,72},{80,88},{96,104},{112,120},{... | collective-permute-start | bytes 87560 | tf_op jit(solution)/shard_map/ppermute | solution.py:264
  34.0 5.7 %shard_map.119 = (bf16[1024,256]{1,0:T(8,128)(2,1)S(1)}, bf16[32,32,128]{2,1,0:T(8,128)(2,1)S(1)}, f32[128,256]{1,0:T(8,128)S(1)}, f32[128,256]{1,0:T(8,128)S(1)}, f32[49,8,128]{2,1,0:T(8,128)S(1)}) custom-call(s32[2]{0:T(128)S(1)} %pad_add_fusion.flags, bf16[32,48,128]{2,1,0:T(8,128)(2,1)S(1)} %get-tuple-element.66.masked, ...), custom_call_target="tpu_custom_call" | custom-call | flops 350000000 | bytes 2097152 | tf_op jit(solution)/shard_map/pallas_call | solution.py:232
  39.8 4.6 %shard_map.120 = (bf16[512,256]{1,0:T(8,128)(2,1)S(1)}, bf16[32,16,128]{2,1,0:T(8,128)(2,1)S(1)}, bf16[64,9,128]{2,1,0:T(8,128)(2,1)}) custom-call(s32[2]{0:T(128)S(1)} %pad_add_fusion.flags, bf16[32,48,128]{2,1,0:T(8,128)(2,1)S(1)} %get-tuple-element.66.masked, bf16[3,48,128]{2,1,0:T(8,128)(2,1)S(1)} %collective-permute-done.lat_b, ...), custom_call_target="tpu_custom_call" | custom-call | flops 170000000 | bytes 2097152 | tf_op jit(solution)/shard_map/pallas_call | solution.py:232
  44.4 4.8 %all-to-all-start = ((bf16[64,9,128]{2,1,0:T(8,128)(2,1)}), bf16[64,9,128]{2,1,0:T(8,128)(2,1)S(1)}, u32[]{:S(2)}, u32[]{:S(2)}) async-start(bf16[64,9,128]{2,1,0:T(8,128)(2,1)} %get-tuple-element.28), calls=%async_computation | async-start | bytes 524288 | tf_op jit(solution)/shard_map/all_to_all | solution.py:288
  49.3 3.6 %collective-permute-start.4 = (bf16[32,3,128]{2,1,0:T(4,128)(2,1)S(1)}, bf16[32,3,128]{2,1,0:T(4,128)(2,1)S(1)}, u32[]{:S(2)}, u32[]{:S(2)}) collective-permute-start(bf16[32,3,128]{2,1,0:T(4,128)(2,1)S(1)} %get-tuple-element.48), channel_id=1, source_target_pairs={{0,8},{16,24},{32,40},{48,56},{64,72},{80,88},{96,104},{112,120},{... | collective-permute-start | bytes 73736 | tf_op jit(solution)/shard_map/ppermute | solution.py:264
  52.9 10.0 %collective-permute-start.5 = (bf16[32,3,128]{2,1,0:T(4,128)(2,1)S(1)}, bf16[32,3,128]{2,1,0:T(4,128)(2,1)S(1)}, u32[]{:S(2)}, u32[]{:S(2)}) collective-permute-start(bf16[32,3,128]{2,1,0:T(4,128)(2,1)S(1)} %get-tuple-element.47), channel_id=1, source_target_pairs={{8,16},{24,32},{40,48},{56,64},{72,80},{88,96},{104,112},{120,128}... | collective-permute-start | bytes 73736 | tf_op jit(solution)/shard_map/ppermute | solution.py:264
  62.9 0.1 reduce_sum.24
  63.0 0.6 broadcast_in_dim.7
  63.6 3.5 %all-to-all-start.1 = ((bf16[12,9,128]{2,1,0:T(8,128)(2,1)}), bf16[12,9,128]{2,1,0:T(8,128)(2,1)S(1)}, u32[]{:S(2)}, u32[]{:S(2)}) async-start(bf16[12,9,128]{2,1,0:T(8,128)(2,1)} %broadcast_in_dim.7), calls=%async_computation.1 | async-start | bytes 98304 | tf_op jit(solution)/shard_map/all_to_all | solution.py:296
  67.2 0.3 broadcast_in_dim.6.ocean
  67.4 1.5 %shard_map.121 = bf16[32,48,128]{2,1,0:T(8,128)(2,1)} custom-call(bf16[1024,256]{1,0:T(8,128)(2,1)S(1)} %get-tuple-element.26.hidden_in, bf16[512,256]{1,0:T(8,128)(2,1)S(1)} %get-tuple-element.27.hidden_st, bf16[32,48,128]{2,1,0:T(8,128)(2,1)S(1)} %get-tuple-element.66.masked, bf16[32,48,128]{2,1,0:T(8,128)(2,1)S(1)} %broadcast_in_dim.6.ocean, ...), custom_call_target="tpu_custom_call" | custom-call | flops 100000000 | bytes 2097152 | tf_op jit(solution)/shard_map/pallas_call | solution.py:232
  69.0 7.8 %all-to-all-done.1 = bf16[12,9,128]{2,1,0:T(8,128)(2,1)S(1)} async-done(((bf16[12,9,128]{2,1,0:T(8,128)(2,1)}), bf16[12,9,128]{2,1,0:T(8,128)(2,1)S(1)}, u32[]{:S(2)}, u32[]{:S(2)}) %all-to-all-start.1) | async-done | bytes 27680 | tf_op jit(solution)/shard_map/all_to_all | solution.py:296
  76.8 0.7 broadcast_in_dim.8
  77.6 6.1 %all-to-all-start.2 = ((bf16[64,9,128]{2,1,0:T(8,128)(2,1)}), bf16[64,9,128]{2,1,0:T(8,128)(2,1)S(1)}, u32[]{:S(2)}, u32[]{:S(2)}) async-start(bf16[64,9,128]{2,1,0:T(8,128)(2,1)} %broadcast_in_dim.8), calls=%async_computation.2 | async-start | bytes 524288 | tf_op jit(solution)/shard_map/all_to_all | solution.py:302
  83.7 0.4 concatenate.18
  84.1 0.4 concatenate.19
  84.5 3.5 %collective-permute-start.6 = (bf16[3,54,128]{2,1,0:T(8,128)(2,1)S(1)}, bf16[3,54,128]{2,1,0:T(8,128)(2,1)S(1)}, u32[]{:S(2)}, u32[]{:S(2)}) collective-permute-start(bf16[3,54,128]{2,1,0:T(8,128)(2,1)S(1)} %get-tuple-element.50), channel_id=1, source_target_pairs={{1,2},{3,4},{5,6},{2,1},{4,3},{6,5},{9,10},{11,12},{13,14},{10,9},... | collective-permute-start | bytes 124424 | tf_op jit(solution)/shard_map/ppermute | solution.py:264
  88.0 1.9 %collective-permute-start.7 = (bf16[3,54,128]{2,1,0:T(8,128)(2,1)S(1)}, bf16[3,54,128]{2,1,0:T(8,128)(2,1)S(1)}, u32[]{:S(2)}, u32[]{:S(2)}) collective-permute-start(bf16[3,54,128]{2,1,0:T(8,128)(2,1)S(1)} %get-tuple-element.49), channel_id=1, source_target_pairs={{0,1},{2,3},{4,5},{6,7},{1,0},{3,2},{5,4},{7,6},{8,9},{10,11},{12,... | collective-permute-start | bytes 124424 | tf_op jit(solution)/shard_map/ppermute | solution.py:264
  90.0 2.2 %collective-permute-done.6.lat_b = bf16[3,54,128]{2,1,0:T(8,128)(2,1)S(1)} collective-permute-done((bf16[3,54,128]{2,1,0:T(8,128)(2,1)S(1)}, bf16[3,54,128]{2,1,0:T(8,128)(2,1)S(1)}, u32[]{:S(2)}, u32[]{:S(2)}) %collective-permute-start.6) | collective-permute-done | bytes 41504 | tf_op jit(solution)/shard_map/ppermute | solution.py:264
  92.2 4.0 %shard_map.122 = bf16[32,48,128]{2,1,0:T(8,128)(2,1)} custom-call(s32[2]{0:T(128)S(1)} %pad_add_fusion.flags, bf16[32,32,128]{2,1,0:T(8,128)(2,1)S(1)} %get-tuple-element.30.dz_in, bf16[32,16,128]{2,1,0:T(8,128)(2,1)S(1)} %get-tuple-element.24.dz_st, bf16[32,3,128]{2,1,0:T(4,128)(2,1)S(1)} %collective-permute-done.5.lon_b, ...), custom_call_target="tpu_custom_call" | custom-call | flops 100000000 | bytes 2097152 | tf_op jit(solution)/shard_map/pallas_call | solution.py:232
  96.3 0.8 shard_map.123
  (31 shorter events, 0.3 us)
Async XLA Ops:
  0.6 0.7 copy-start.3
  2.3 15.3 %collective-permute-start = (bf16[3,48,128]{2,1,0:T(8,128)(2,1)S(1)}, bf16[3,48,128]{2,1,0:T(8,128)(2,1)S(1)}, u32[]{:S(2)}, u32[]{:S(2)}) collective-permute-start(bf16[3,48,128]{2,1,0:T(8,128)(2,1)S(1)} %get-tuple-element.38), channel_id=1, source_target_pairs={{1,2},{3,4},{5,6},{2,1},{4,3},{6,5},{9,10},{11,12},{13,14},{10,9},... | collective-permute-start | bytes 110600 | tf_op jit(solution)/shard_map/ppermute | solution.py:264
  6.9 10.7 %collective-permute-start.1 = (bf16[3,48,128]{2,1,0:T(8,128)(2,1)S(1)}, bf16[3,48,128]{2,1,0:T(8,128)(2,1)S(1)}, u32[]{:S(2)}, u32[]{:S(2)}) collective-permute-start(bf16[3,48,128]{2,1,0:T(8,128)(2,1)S(1)} %get-tuple-element.37), channel_id=1, source_target_pairs={{0,1},{2,3},{4,5},{6,7},{1,0},{3,2},{5,4},{7,6},{8,9},{10,11},{12,... | collective-permute-start | bytes 110600 | tf_op jit(solution)/shard_map/ppermute | solution.py:264
  16.8 0.7 copy-start.4
  16.8 0.7 copy-start.5
  17.6 16.3 %copy-start = (bf16[256,128]{1,0:T(8,128)(2,1)S(1)}, bf16[256,128]{1,0:T(8,128)(2,1)}, u32[]{:S(2)}) copy-start(bf16[256,128]{1,0:T(8,128)(2,1)} %w_out.5) | copy-start | bytes 196612
  17.6 16.3 %copy-start.1 = (f32[7,7,128]{2,1,0:T(8,128)S(1)}, f32[7,7,128]{2,1,0:T(8,128)}, u32[]{:S(2)}) copy-start(f32[7,7,128]{2,1,0:T(8,128)} %taps.5) | copy-start | bytes 75268
  17.6 16.3 %copy-start.2 = (bf16[128,256]{1,0:T(8,128)(2,1)S(1)}, bf16[128,256]{1,0:T(8,128)(2,1)}, u32[]{:S(2)}) copy-start(bf16[128,256]{1,0:T(8,128)(2,1)} %w_in.3) | copy-start | bytes 196612
  17.7 22.0 %collective-permute-start.2 = (bf16[38,3,128]{2,1,0:T(4,128)(2,1)S(1)}, bf16[38,3,128]{2,1,0:T(4,128)(2,1)S(1)}, u32[]{:S(2)}, u32[]{:S(2)}) collective-permute-start(bf16[38,3,128]{2,1,0:T(4,128)(2,1)S(1)} %get-tuple-element.52), channel_id=1, source_target_pairs={{8,16},{24,32},{40,48},{56,64},{72,80},{88,96},{104,112},{120,128}... | collective-permute-start | bytes 87560 | tf_op jit(solution)/shard_map/ppermute | solution.py:264
  32.0 7.7 %collective-permute-start.3 = (bf16[38,3,128]{2,1,0:T(4,128)(2,1)S(1)}, bf16[38,3,128]{2,1,0:T(4,128)(2,1)S(1)}, u32[]{:S(2)}, u32[]{:S(2)}) collective-permute-start(bf16[38,3,128]{2,1,0:T(4,128)(2,1)S(1)} %get-tuple-element.51), channel_id=1, source_target_pairs={{0,8},{16,24},{32,40},{48,56},{64,72},{80,88},{96,104},{112,120},{... | collective-permute-start | bytes 87560 | tf_op jit(solution)/shard_map/ppermute | solution.py:264
  44.4 18.5 %all-to-all-start = ((bf16[64,9,128]{2,1,0:T(8,128)(2,1)}), bf16[64,9,128]{2,1,0:T(8,128)(2,1)S(1)}, u32[]{:S(2)}, u32[]{:S(2)}) async-start(bf16[64,9,128]{2,1,0:T(8,128)(2,1)} %get-tuple-element.28), calls=%async_computation | async-start | bytes 524288 | tf_op jit(solution)/shard_map/all_to_all | solution.py:288
  49.3 27.5 %collective-permute-start.4 = (bf16[32,3,128]{2,1,0:T(4,128)(2,1)S(1)}, bf16[32,3,128]{2,1,0:T(4,128)(2,1)S(1)}, u32[]{:S(2)}, u32[]{:S(2)}) collective-permute-start(bf16[32,3,128]{2,1,0:T(4,128)(2,1)S(1)} %get-tuple-element.48), channel_id=1, source_target_pairs={{0,8},{16,24},{32,40},{48,56},{64,72},{80,88},{96,104},{112,120},{... | collective-permute-start | bytes 73736 | tf_op jit(solution)/shard_map/ppermute | solution.py:264
  52.9 23.9 %collective-permute-start.5 = (bf16[32,3,128]{2,1,0:T(4,128)(2,1)S(1)}, bf16[32,3,128]{2,1,0:T(4,128)(2,1)S(1)}, u32[]{:S(2)}, u32[]{:S(2)}) collective-permute-start(bf16[32,3,128]{2,1,0:T(4,128)(2,1)S(1)} %get-tuple-element.47), channel_id=1, source_target_pairs={{8,16},{24,32},{40,48},{56,64},{72,80},{88,96},{104,112},{120,128}... | collective-permute-start | bytes 73736 | tf_op jit(solution)/shard_map/ppermute | solution.py:264
  63.6 13.1 %all-to-all-start.1 = ((bf16[12,9,128]{2,1,0:T(8,128)(2,1)}), bf16[12,9,128]{2,1,0:T(8,128)(2,1)S(1)}, u32[]{:S(2)}, u32[]{:S(2)}) async-start(bf16[12,9,128]{2,1,0:T(8,128)(2,1)} %broadcast_in_dim.7), calls=%async_computation.1 | async-start | bytes 98304 | tf_op jit(solution)/shard_map/all_to_all | solution.py:296
  77.6 18.7 %all-to-all-start.2 = ((bf16[64,9,128]{2,1,0:T(8,128)(2,1)}), bf16[64,9,128]{2,1,0:T(8,128)(2,1)S(1)}, u32[]{:S(2)}, u32[]{:S(2)}) async-start(bf16[64,9,128]{2,1,0:T(8,128)(2,1)} %broadcast_in_dim.8), calls=%async_computation.2 | async-start | bytes 524288 | tf_op jit(solution)/shard_map/all_to_all | solution.py:302
  84.5 7.7 %collective-permute-start.6 = (bf16[3,54,128]{2,1,0:T(8,128)(2,1)S(1)}, bf16[3,54,128]{2,1,0:T(8,128)(2,1)S(1)}, u32[]{:S(2)}, u32[]{:S(2)}) collective-permute-start(bf16[3,54,128]{2,1,0:T(8,128)(2,1)S(1)} %get-tuple-element.50), channel_id=1, source_target_pairs={{1,2},{3,4},{5,6},{2,1},{4,3},{6,5},{9,10},{11,12},{13,14},{10,9},... | collective-permute-start | bytes 124424 | tf_op jit(solution)/shard_map/ppermute | solution.py:264
  88.0 4.2 %collective-permute-start.7 = (bf16[3,54,128]{2,1,0:T(8,128)(2,1)S(1)}, bf16[3,54,128]{2,1,0:T(8,128)(2,1)S(1)}, u32[]{:S(2)}, u32[]{:S(2)}) collective-permute-start(bf16[3,54,128]{2,1,0:T(8,128)(2,1)S(1)} %get-tuple-element.49), channel_id=1, source_target_pairs={{0,1},{2,3},{4,5},{6,7},{1,0},{3,2},{5,4},{7,6},{8,9},{10,11},{12,... | collective-permute-start | bytes 124424 | tf_op jit(solution)/shard_map/ppermute | solution.py:264

commit v9 on v8

--- a/solution.py
+++ b/solution.py
@@ -17,7 +17,6 @@
 COLS = 48
 C = 128
 FF = 256
-TERM_ROWS = 576
 
 
 INSIDE = ((8, 32),)
@@ -143,7 +142,7 @@
 def strips_kernel(
     flags, masked, lat_b, lat_a, lon_b, lon_a, gmask, taps, vectors, w_in, w_out,
     had_in, had_out, had_tap,
-    hidden, dz_out, terms, left, right, acc_in, acc_out, acc_tap,
+    hidden, dz_out, terms, left, right, acc_in, acc_out, acc_tap, turned,
 ):
     fill_strips(left, right, masked, flags, lat_a, lat_b, lon_a, lon_b)
     acc_in[...] = had_in[...]
@@ -153,17 +152,18 @@
     pads = ((left, 5, 8), (right, 5, 8))
     main_rows(ROWS, STRIPS, STRIPS_OUT, pads, gmask, params, hidden, dz_out, (acc_in, acc_out, acc_tap), 0)
     half = C // 8
-    turned = acc_out[...].T
+    turned[...] = acc_out[...].T
     tap_sums = jnp.sum(acc_tap[...], axis=1)
-    for part in range(half):
-        rows = slice(8 * part, 8 * part + 8)
-        terms[part, 0:8, :] = acc_in[rows, 0:C].astype(LINK)
-        terms[half + part, 0:8, :] = acc_in[rows, C:].astype(LINK)
-    for part in range(2 * half):
-        terms[2 * half + part, 0:8, :] = turned[8 * part : 8 * part + 8].astype(LINK)
-    for part in range(terms.shape[0]):
+    for part in range(4 * half):
+        if part < 2 * half:
+            first, lanes, source = 8 * (part % half), slice(C * (part // half), C * (part // half) + C), acc_in
+        else:
+            first, lanes, source = 8 * (part - 2 * half), slice(0, C), turned
         row = tap_sums[part : part + 1] if part < 49 else jnp.zeros((1, C), jnp.float32)
-        terms[part, 8:9, :] = row.astype(LINK)
+        terms[part, 0] = source[first : first + 3, lanes].astype(LINK)
+        terms[part, 1] = source[first + 3 : first + 6, lanes].astype(LINK)
+        terms[part, 2, 0:2, :] = source[first + 6 : first + 8, lanes].astype(LINK)
+        terms[part, 2, 2:3, :] = row.astype(LINK)
 
 
 def advance_kernel(hidden_in, hidden_st, masked, ocean, w_out, advanced):
@@ -214,16 +214,16 @@
 
 def final_kernel(parts, kernel_grad, w_in_grad, w_out_grad, *, factor):
     half = C // 8
-    for part in range(parts.shape[0]):
-        rows = parts[part, 0:8, :].astype(jnp.float32) * factor
-        if part < half:
-            w_in_grad[8 * part : 8 * part + 8, 0:C] = rows
-        elif part < 2 * half:
-            w_in_grad[8 * (part - half) : 8 * (part - half) + 8, C:] = rows
+    for part in range(4 * half):
+        if part < 2 * half:
+            first, lanes, target = 8 * (part % half), slice(C * (part // half), C * (part // half) + C), w_in_grad
         else:
-            w_out_grad[8 * (part - 2 * half) : 8 * (part - 2 * half) + 8, :] = rows
+            first, lanes, target = 8 * (part - 2 * half), slice(0, C), w_out_grad
+        target[first : first + 3, lanes] = parts[part, 0].astype(jnp.float32) * factor
+        target[first + 3 : first + 6, lanes] = parts[part, 1].astype(jnp.float32) * factor
+        target[first + 6 : first + 8, lanes] = parts[part, 2, 0:2, :].astype(jnp.float32) * factor
     for part in range(49):
-        kernel_grad[part // 7, part % 7 : part % 7 + 1, :] = parts[part, 8:9, :].astype(jnp.float32) * factor
+        kernel_grad[part // 7, part % 7 : part % 7 + 1, :] = parts[part, 2, 2:3, :].astype(jnp.float32) * factor
 
 
 def call(body, args, outs, scratch, flops):
@@ -335,9 +335,9 @@
         [
             kind(ROWS * 16, FF, dtype=jnp.bfloat16),
             kind(ROWS, 16, C, dtype=jnp.bfloat16),
-            kind(parts, TERM_ROWS // parts, C, dtype=LINK),
+            kind(parts, 3, 3, C, dtype=LINK),
         ],
-        [NARROW, NARROW, *scratch],
+        [NARROW, NARROW, *scratch, pltpu.VMEM((FF, C), jnp.float32)],
         170_000_000,
     )
     copies = inner_copies(scatter_sum(terms))
@@ -349,8 +349,8 @@
     )
     near = jnp.where(even, high, low)
     lon_a = swap(near, LON, group_size(LON), 0, True)
-    lon_a, lon_b, dz_in, advanced, total = lax.optimization_barrier(
-        (lon_a, lon_b, dz_in, advanced, inner_sum(copies))
+    lon_b, lon_a, dz_in, advanced, total = lax.optimization_barrier(
+        (lon_b, lon_a, dz_in, advanced, inner_sum(copies))
     )
     west, east = jnp.where(even, lon_b, lon_a), jnp.where(even, lon_a, lon_b)
 

time: 97.7 us -> 96.5 us (0.988)
  waiting for transfers between devices: 10 us -> 8.77 us
    ppermute x8, waiting for transfers between devices: 2.25 us -> 1.2 us  [swap(): return lax.ppermute(values, axes, pairs)]
  transfers between devices with their start and end apart: 11 -> 11, of which waited for: 2 -> 3; matrix products, arithmetic and copies ran while one was open for 3% -> 4% of each run, Pallas kernels for 12% -> 12%
where the time goes in v9:
time: 96.5 us; the launch traced here: 95.8 us
  starting transfers between devices  62.6 us (65%)
  Pallas kernels  16.9 us (18%)
  waiting for transfers between devices  8.77 us (9%)
  local copies, waits for them, and re-layouts  3.89 us (4%)
  other arithmetic  2.69 us (3%)
  between operations  0.98 us (1%)
    ppermute x8, starting transfers between devices, swap(): return lax.ppermute(values, axes, pairs)  48.4 us
    pallas_call x5, Pallas kernels, call(): pl.pallas_call(body, out_shape=outs, in_specs=[smem if a.dtype == jnp.int...  16.9 us
    all_to_all x1, waiting for transfers between devices, inner_sum(): parts = lax.all_to_all(copies, INNER, 0, 0, tiled=True).astype(jnp.float32)  7.56 us
    all_to_all x1, starting transfers between devices, hand_out(): return lax.all_to_all(spread, OUTER, 0, 0, tiled=True)  5.84 us
    all_to_all x1, starting transfers between devices, scatter_sum(): lax.all_to_all(parts, OUTER, 0, 0, tiled=True).astype(jnp.float32)  4.84 us
    all_to_all x1, starting transfers between devices, inner_sum(): parts = lax.all_to_all(copies, INNER, 0, 0, tiled=True).astype(jnp.float32)  3.5 us
  transfers between devices with their start and end apart: 11, of which 3 were waited for; matrix products, arithmetic and copies ran while one was open for 4% of the time, Pallas kernels for 12%

profile of v9, /device:TPU:1, one launch (start us, length us, event | category | flops | bytes accessed | tf_op | source)
XLA Modules:
  0.0 95.8 jit_solution(11730185299901662384)
XLA Ops:
  0.7 0.7 copy-done.3
  1.4 0.9 broadcast_select_fusion.6
  2.3 4.6 %collective-permute-start = (bf16[3,48,128]{2,1,0:T(8,128)(2,1)S(1)}, bf16[3,48,128]{2,1,0:T(8,128)(2,1)S(1)}, u32[]{:S(2)}, u32[]{:S(2)}) collective-permute-start(bf16[3,48,128]{2,1,0:T(8,128)(2,1)S(1)} %get-tuple-element.38), channel_id=1, source_target_pairs={{1,2},{3,4},{5,6},{2,1},{4,3},{6,5},{9,10},{11,12},{13,14},{10,9},... | collective-permute-start | bytes 110600 | tf_op jit(solution)/shard_map/ppermute | solution.py:264
  6.9 8.5 %collective-permute-start.1 = (bf16[3,48,128]{2,1,0:T(8,128)(2,1)S(1)}, bf16[3,48,128]{2,1,0:T(8,128)(2,1)S(1)}, u32[]{:S(2)}, u32[]{:S(2)}) collective-permute-start(bf16[3,48,128]{2,1,0:T(8,128)(2,1)S(1)} %get-tuple-element.37), channel_id=1, source_target_pairs={{0,1},{2,3},{4,5},{6,7},{1,0},{3,2},{5,4},{7,6},{8,9},{10,11},{12,... | collective-permute-start | bytes 110600 | tf_op jit(solution)/shard_map/ppermute | solution.py:264
  15.4 1.4 %broadcast_multiply_fusion = (bf16[32,48,128]{2,1,0:T(8,128)(2,1)S(1)}, bf16[32,48,128]{2,1,0:T(8,128)(2,1)S(1)}) fusion(bf16[32,48,128]{2,1,0:T(8,128)(2,1)} %param.10, bf16[32,48]{1,0:T(8,128)(2,1)S(1)} %convert_element_type.2, bf16[32,48,128]{2,1,0:T(8,128)(2,1)} %param.8), kind=kLoop, calls=%fused_computation | loop fusion | flops 393216 | bytes 1575936 | tf_op jit(solution)/shard_map/mul | solution.py:317
  16.8 0.0 copy-start.4
  16.8 0.7 copy-done.4
  17.5 0.1 pad_add_fusion.flags
  17.7 0.1 broadcast_select_fusion.2
  17.7 14.3 %collective-permute-start.2 = (bf16[38,3,128]{2,1,0:T(4,128)(2,1)S(1)}, bf16[38,3,128]{2,1,0:T(4,128)(2,1)S(1)}, u32[]{:S(2)}, u32[]{:S(2)}) collective-permute-start(bf16[38,3,128]{2,1,0:T(4,128)(2,1)S(1)} %get-tuple-element.52), channel_id=1, source_target_pairs={{8,16},{24,32},{40,48},{56,64},{72,80},{88,96},{104,112},{120,128}... | collective-permute-start | bytes 87560 | tf_op jit(solution)/shard_map/ppermute | solution.py:264
  32.0 1.9 %collective-permute-start.3 = (bf16[38,3,128]{2,1,0:T(4,128)(2,1)S(1)}, bf16[38,3,128]{2,1,0:T(4,128)(2,1)S(1)}, u32[]{:S(2)}, u32[]{:S(2)}) collective-permute-start(bf16[38,3,128]{2,1,0:T(4,128)(2,1)S(1)} %get-tuple-element.51), channel_id=1, source_target_pairs={{0,8},{16,24},{32,40},{48,56},{64,72},{80,88},{96,104},{112,120},{... | collective-permute-start | bytes 87560 | tf_op jit(solution)/shard_map/ppermute | solution.py:264
  34.0 5.7 %shard_map.119 = (bf16[1024,256]{1,0:T(8,128)(2,1)S(1)}, bf16[32,32,128]{2,1,0:T(8,128)(2,1)S(1)}, f32[128,256]{1,0:T(8,128)S(1)}, f32[128,256]{1,0:T(8,128)S(1)}, f32[49,8,128]{2,1,0:T(8,128)S(1)}) custom-call(s32[2]{0:T(128)S(1)} %pad_add_fusion.flags, bf16[32,48,128]{2,1,0:T(8,128)(2,1)S(1)} %get-tuple-element.66.masked, ...), custom_call_target="tpu_custom_call" | custom-call | flops 350000000 | bytes 2097152 | tf_op jit(solution)/shard_map/pallas_call | solution.py:232
  39.8 4.7 %shard_map.120 = (bf16[512,256]{1,0:T(8,128)(2,1)S(1)}, bf16[32,16,128]{2,1,0:T(8,128)(2,1)S(1)}, bf16[64,3,3,128]{3,2,1,0:T(4,128)(2,1)}) custom-call(s32[2]{0:T(128)S(1)} %pad_add_fusion.flags, bf16[32,48,128]{2,1,0:T(8,128)(2,1)S(1)} %get-tuple-element.66.masked, bf16[3,48,128]{2,1,0:T(8,128)(2,1)S(1)} %collective-permute-done.lat_b, ...), custom_call_target="tpu_custom_call" | custom-call | flops 170000000 | bytes 2097152 | tf_op jit(solution)/shard_map/pallas_call | solution.py:232
  44.5 4.8 %all-to-all-start = ((bf16[64,3,3,128]{3,2,1,0:T(4,128)(2,1)}), bf16[64,3,3,128]{3,2,1,0:T(4,128)(2,1)S(1)}, u32[]{:S(2)}, u32[]{:S(2)}) async-start(bf16[64,3,3,128]{3,2,1,0:T(4,128)(2,1)} %get-tuple-element.28), calls=%async_computation | async-start | bytes 393216 | tf_op jit(solution)/shard_map/all_to_all | solution.py:288
  49.4 11.7 %collective-permute-start.4 = (bf16[32,3,128]{2,1,0:T(4,128)(2,1)S(1)}, bf16[32,3,128]{2,1,0:T(4,128)(2,1)S(1)}, u32[]{:S(2)}, u32[]{:S(2)}) collective-permute-start(bf16[32,3,128]{2,1,0:T(4,128)(2,1)S(1)} %get-tuple-element.48), channel_id=1, source_target_pairs={{8,16},{24,32},{40,48},{56,64},{72,80},{88,96},{104,112},{120,128}... | collective-permute-start | bytes 73736 | tf_op jit(solution)/shard_map/ppermute | solution.py:264
  61.1 1.9 %collective-permute-start.5 = (bf16[32,3,128]{2,1,0:T(4,128)(2,1)S(1)}, bf16[32,3,128]{2,1,0:T(4,128)(2,1)S(1)}, u32[]{:S(2)}, u32[]{:S(2)}) collective-permute-start(bf16[32,3,128]{2,1,0:T(4,128)(2,1)S(1)} %get-tuple-element.47), channel_id=1, source_target_pairs={{0,8},{16,24},{32,40},{48,56},{64,72},{80,88},{96,104},{112,120},{... | collective-permute-start | bytes 73736 | tf_op jit(solution)/shard_map/ppermute | solution.py:264
  63.0 0.1 reduce_sum.24
  63.1 0.6 broadcast_in_dim.7
  63.8 3.5 %all-to-all-start.1 = ((bf16[12,3,3,128]{3,2,1,0:T(4,128)(2,1)}), bf16[12,3,3,128]{3,2,1,0:T(4,128)(2,1)S(1)}, u32[]{:S(2)}, u32[]{:S(2)}) async-start(bf16[12,3,3,128]{3,2,1,0:T(4,128)(2,1)} %broadcast_in_dim.7), calls=%async_computation.1 | async-start | bytes 73728 | tf_op jit(solution)/shard_map/all_to_all | solution.py:296
  67.3 0.3 broadcast_in_dim.6.ocean
  67.6 1.5 %shard_map.121 = bf16[32,48,128]{2,1,0:T(8,128)(2,1)} custom-call(bf16[1024,256]{1,0:T(8,128)(2,1)S(1)} %get-tuple-element.26.hidden_in, bf16[512,256]{1,0:T(8,128)(2,1)S(1)} %get-tuple-element.27.hidden_st, bf16[32,48,128]{2,1,0:T(8,128)(2,1)S(1)} %get-tuple-element.66.masked, bf16[32,48,128]{2,1,0:T(8,128)(2,1)S(1)} %broadcast_in_dim.6.ocean, ...), custom_call_target="tpu_custom_call" | custom-call | flops 100000000 | bytes 2097152 | tf_op jit(solution)/shard_map/pallas_call | solution.py:232
  69.1 7.6 %all-to-all-done.1 = bf16[12,3,3,128]{3,2,1,0:T(4,128)(2,1)S(1)} async-done(((bf16[12,3,3,128]{3,2,1,0:T(4,128)(2,1)}), bf16[12,3,3,128]{3,2,1,0:T(4,128)(2,1)S(1)}, u32[]{:S(2)}, u32[]{:S(2)}) %all-to-all-start.1) | async-done | bytes 27680 | tf_op jit(solution)/shard_map/all_to_all | solution.py:296
  76.8 0.7 broadcast_in_dim.8
  77.5 5.8 %all-to-all-start.2 = ((bf16[64,3,3,128]{3,2,1,0:T(4,128)(2,1)}), bf16[64,3,3,128]{3,2,1,0:T(4,128)(2,1)S(1)}, u32[]{:S(2)}, u32[]{:S(2)}) async-start(bf16[64,3,3,128]{3,2,1,0:T(4,128)(2,1)} %broadcast_in_dim.8), calls=%async_computation.2 | async-start | bytes 393216 | tf_op jit(solution)/shard_map/all_to_all | solution.py:302
  83.4 0.4 concatenate.18
  83.8 0.4 concatenate.19
  84.2 3.5 %collective-permute-start.6 = (bf16[3,54,128]{2,1,0:T(8,128)(2,1)S(1)}, bf16[3,54,128]{2,1,0:T(8,128)(2,1)S(1)}, u32[]{:S(2)}, u32[]{:S(2)}) collective-permute-start(bf16[3,54,128]{2,1,0:T(8,128)(2,1)S(1)} %get-tuple-element.50), channel_id=1, source_target_pairs={{1,2},{3,4},{5,6},{2,1},{4,3},{6,5},{9,10},{11,12},{13,14},{10,9},... | collective-permute-start | bytes 124424 | tf_op jit(solution)/shard_map/ppermute | solution.py:264
  87.8 1.9 %collective-permute-start.7 = (bf16[3,54,128]{2,1,0:T(8,128)(2,1)S(1)}, bf16[3,54,128]{2,1,0:T(8,128)(2,1)S(1)}, u32[]{:S(2)}, u32[]{:S(2)}) collective-permute-start(bf16[3,54,128]{2,1,0:T(8,128)(2,1)S(1)} %get-tuple-element.49), channel_id=1, source_target_pairs={{0,1},{2,3},{4,5},{6,7},{1,0},{3,2},{5,4},{7,6},{8,9},{10,11},{12,... | collective-permute-start | bytes 124424 | tf_op jit(solution)/shard_map/ppermute | solution.py:264
  89.7 0.8 collective-permute-done.6.lat_b
  90.5 0.4 collective-permute-done.7.lat_a
  90.9 4.0 %shard_map.122 = bf16[32,48,128]{2,1,0:T(8,128)(2,1)} custom-call(s32[2]{0:T(128)S(1)} %pad_add_fusion.flags, bf16[32,32,128]{2,1,0:T(8,128)(2,1)S(1)} %get-tuple-element.30.dz_in, bf16[32,16,128]{2,1,0:T(8,128)(2,1)S(1)} %get-tuple-element.24.dz_st, bf16[32,3,128]{2,1,0:T(4,128)(2,1)S(1)} %collective-permute-done.4.lon_b, ...), custom_call_target="tpu_custom_call" | custom-call | flops 100000000 | bytes 2097152 | tf_op jit(solution)/shard_map/pallas_call | solution.py:232
  94.9 0.8 shard_map.123
  (31 shorter events, 0.3 us)
Async XLA Ops:
  0.6 0.7 copy-start.3
  2.3 15.3 %collective-permute-start = (bf16[3,48,128]{2,1,0:T(8,128)(2,1)S(1)}, bf16[3,48,128]{2,1,0:T(8,128)(2,1)S(1)}, u32[]{:S(2)}, u32[]{:S(2)}) collective-permute-start(bf16[3,48,128]{2,1,0:T(8,128)(2,1)S(1)} %get-tuple-element.38), channel_id=1, source_target_pairs={{1,2},{3,4},{5,6},{2,1},{4,3},{6,5},{9,10},{11,12},{13,14},{10,9},... | collective-permute-start | bytes 110600 | tf_op jit(solution)/shard_map/ppermute | solution.py:264
  6.9 10.7 %collective-permute-start.1 = (bf16[3,48,128]{2,1,0:T(8,128)(2,1)S(1)}, bf16[3,48,128]{2,1,0:T(8,128)(2,1)S(1)}, u32[]{:S(2)}, u32[]{:S(2)}) collective-permute-start(bf16[3,48,128]{2,1,0:T(8,128)(2,1)S(1)} %get-tuple-element.37), channel_id=1, source_target_pairs={{0,1},{2,3},{4,5},{6,7},{1,0},{3,2},{5,4},{7,6},{8,9},{10,11},{12,... | collective-permute-start | bytes 110600 | tf_op jit(solution)/shard_map/ppermute | solution.py:264
  16.8 0.7 copy-start.4
  16.8 0.7 copy-start.5
  17.6 16.3 %copy-start = (bf16[256,128]{1,0:T(8,128)(2,1)S(1)}, bf16[256,128]{1,0:T(8,128)(2,1)}, u32[]{:S(2)}) copy-start(bf16[256,128]{1,0:T(8,128)(2,1)} %w_out.5) | copy-start | bytes 196612
  17.6 16.3 %copy-start.1 = (f32[7,7,128]{2,1,0:T(8,128)S(1)}, f32[7,7,128]{2,1,0:T(8,128)}, u32[]{:S(2)}) copy-start(f32[7,7,128]{2,1,0:T(8,128)} %taps.5) | copy-start | bytes 75268
  17.7 16.3 %copy-start.2 = (bf16[128,256]{1,0:T(8,128)(2,1)S(1)}, bf16[128,256]{1,0:T(8,128)(2,1)}, u32[]{:S(2)}) copy-start(bf16[128,256]{1,0:T(8,128)(2,1)} %w_in.3) | copy-start | bytes 196612
  17.7 22.0 %collective-permute-start.2 = (bf16[38,3,128]{2,1,0:T(4,128)(2,1)S(1)}, bf16[38,3,128]{2,1,0:T(4,128)(2,1)S(1)}, u32[]{:S(2)}, u32[]{:S(2)}) collective-permute-start(bf16[38,3,128]{2,1,0:T(4,128)(2,1)S(1)} %get-tuple-element.52), channel_id=1, source_target_pairs={{8,16},{24,32},{40,48},{56,64},{72,80},{88,96},{104,112},{120,128}... | collective-permute-start | bytes 87560 | tf_op jit(solution)/shard_map/ppermute | solution.py:264
  32.0 7.7 %collective-permute-start.3 = (bf16[38,3,128]{2,1,0:T(4,128)(2,1)S(1)}, bf16[38,3,128]{2,1,0:T(4,128)(2,1)S(1)}, u32[]{:S(2)}, u32[]{:S(2)}) collective-permute-start(bf16[38,3,128]{2,1,0:T(4,128)(2,1)S(1)} %get-tuple-element.51), channel_id=1, source_target_pairs={{0,8},{16,24},{32,40},{48,56},{64,72},{80,88},{96,104},{112,120},{... | collective-permute-start | bytes 87560 | tf_op jit(solution)/shard_map/ppermute | solution.py:264
  44.5 18.5 %all-to-all-start = ((bf16[64,3,3,128]{3,2,1,0:T(4,128)(2,1)}), bf16[64,3,3,128]{3,2,1,0:T(4,128)(2,1)S(1)}, u32[]{:S(2)}, u32[]{:S(2)}) async-start(bf16[64,3,3,128]{3,2,1,0:T(4,128)(2,1)} %get-tuple-element.28), calls=%async_computation | async-start | bytes 393216 | tf_op jit(solution)/shard_map/all_to_all | solution.py:288
  49.4 27.3 %collective-permute-start.4 = (bf16[32,3,128]{2,1,0:T(4,128)(2,1)S(1)}, bf16[32,3,128]{2,1,0:T(4,128)(2,1)S(1)}, u32[]{:S(2)}, u32[]{:S(2)}) collective-permute-start(bf16[32,3,128]{2,1,0:T(4,128)(2,1)S(1)} %get-tuple-element.48), channel_id=1, source_target_pairs={{8,16},{24,32},{40,48},{56,64},{72,80},{88,96},{104,112},{120,128}... | collective-permute-start | bytes 73736 | tf_op jit(solution)/shard_map/ppermute | solution.py:264
  61.1 15.6 %collective-permute-start.5 = (bf16[32,3,128]{2,1,0:T(4,128)(2,1)S(1)}, bf16[32,3,128]{2,1,0:T(4,128)(2,1)S(1)}, u32[]{:S(2)}, u32[]{:S(2)}) collective-permute-start(bf16[32,3,128]{2,1,0:T(4,128)(2,1)S(1)} %get-tuple-element.47), channel_id=1, source_target_pairs={{0,8},{16,24},{32,40},{48,56},{64,72},{80,88},{96,104},{112,120},{... | collective-permute-start | bytes 73736 | tf_op jit(solution)/shard_map/ppermute | solution.py:264
  63.8 12.9 %all-to-all-start.1 = ((bf16[12,3,3,128]{3,2,1,0:T(4,128)(2,1)}), bf16[12,3,3,128]{3,2,1,0:T(4,128)(2,1)S(1)}, u32[]{:S(2)}, u32[]{:S(2)}) async-start(bf16[12,3,3,128]{3,2,1,0:T(4,128)(2,1)} %broadcast_in_dim.7), calls=%async_computation.1 | async-start | bytes 73728 | tf_op jit(solution)/shard_map/all_to_all | solution.py:296
  77.5 17.4 %all-to-all-start.2 = ((bf16[64,3,3,128]{3,2,1,0:T(4,128)(2,1)}), bf16[64,3,3,128]{3,2,1,0:T(4,128)(2,1)S(1)}, u32[]{:S(2)}, u32[]{:S(2)}) async-start(bf16[64,3,3,128]{3,2,1,0:T(4,128)(2,1)} %broadcast_in_dim.8), calls=%async_computation.2 | async-start | bytes 393216 | tf_op jit(solution)/shard_map/all_to_all | solution.py:302
  84.2 6.3 %collective-permute-start.6 = (bf16[3,54,128]{2,1,0:T(8,128)(2,1)S(1)}, bf16[3,54,128]{2,1,0:T(8,128)(2,1)S(1)}, u32[]{:S(2)}, u32[]{:S(2)}) collective-permute-start(bf16[3,54,128]{2,1,0:T(8,128)(2,1)S(1)} %get-tuple-element.50), channel_id=1, source_target_pairs={{1,2},{3,4},{5,6},{2,1},{4,3},{6,5},{9,10},{11,12},{13,14},{10,9},... | collective-permute-start | bytes 124424 | tf_op jit(solution)/shard_map/ppermute | solution.py:264
  87.8 3.1 %collective-permute-start.7 = (bf16[3,54,128]{2,1,0:T(8,128)(2,1)S(1)}, bf16[3,54,128]{2,1,0:T(8,128)(2,1)S(1)}, u32[]{:S(2)}, u32[]{:S(2)}) collective-permute-start(bf16[3,54,128]{2,1,0:T(8,128)(2,1)S(1)} %get-tuple-element.49), channel_id=1, source_target_pairs={{0,1},{2,3},{4,5},{6,7},{1,0},{3,2},{5,4},{7,6},{8,9},{10,11},{12,... | collective-permute-start | bytes 124424 | tf_op jit(solution)/shard_map/ppermute | solution.py:264

commit v10 on v9

--- a/solution.py
+++ b/solution.py
@@ -183,7 +183,23 @@
     lax.fori_loop(0, ROWS // 8, block, 0)
 
 
-def back_kernel(flags, dz_in, dz_st, lon_b, lon_a, lat_b, lat_a, gmask, ocean, taps, field_grad, pad):
+def back_inside_kernel(dz_in, dz_st, gmask, ocean, taps, part, pad):
+    f32 = jnp.float32
+    pad[:, 0:8, :] = dz_st[:, 0:8, :].astype(f32)
+    pad[:, 8:40, :] = dz_in[...].astype(f32)
+    pad[:, 40:48, :] = dz_st[:, 8:16, :].astype(f32)
+
+    def block(index, carry):
+        back = conv_rows(((pad, 5, 32),), taps, 4 * index + 1, 4, True)
+        own = read_cells(gmask, 4 * index + 4, 4, INSIDE)
+        keep = read_cells(ocean, 4 * index + 4, 4, INSIDE)
+        write_cells(part, 4 * index, 4, INSIDE_OUT, own + keep * back)
+        return carry
+
+    lax.fori_loop(0, 6, block, 0)
+
+
+def back_kernel(flags, dz_in, dz_st, lon_b, lon_a, lat_b, lat_a, gmask, ocean, taps, part, field_grad, pad):
     f32 = jnp.float32
     even = flags[1] == 0
     from_a, from_b = lon_a[...].astype(f32), lon_b[...].astype(f32)
@@ -197,15 +213,20 @@
     pad[0:3, 5 : 11 + COLS, :] = jnp.where(even, from_b, from_a)
     pad[3 + ROWS : 6 + ROWS, 5 : 11 + COLS, :] = jnp.where(even, from_a, from_b)
 
-    def block(index, carry):
-        back_rows(4, ((0, COLS),), ((pad, 5, COLS),), gmask, ocean, taps, field_grad, index)
+    def ends(index, carry):
+        back_rows(4, 28 * index, ((0, COLS),), ((pad, 5, COLS),), gmask, ocean, taps, field_grad)
         return carry
 
-    lax.fori_loop(0, ROWS // 4, block, 0)
-
-
-def back_rows(step, segs, pads, gmask, ocean, taps, field_grad, index):
-    first = index * step
+    def sides(index, carry):
+        back_rows(8, 8 * index + 4, STRIPS, ((pad, 5, 8), (pad, 45, 8)), gmask, ocean, taps, field_grad)
+        return carry
+
+    field_grad[4:28, 8:40, :] = part[...]
+    lax.fori_loop(0, 2, ends, 0)
+    lax.fori_loop(0, 3, sides, 0)
+
+
+def back_rows(step, first, segs, pads, gmask, ocean, taps, field_grad):
     back = conv_rows(pads, taps, first, step, True)
     own = read_cells(gmask, first, step, segs)
     keep = read_cells(ocean, first, step, segs)
@@ -349,8 +370,15 @@
     )
     near = jnp.where(even, high, low)
     lon_a = swap(near, LON, group_size(LON), 0, True)
-    lon_b, lon_a, dz_in, advanced, total = lax.optimization_barrier(
-        (lon_b, lon_a, dz_in, advanced, inner_sum(copies))
+    (part,) = call(
+        back_inside_kernel,
+        (dz_in, dz_st, gmask, ocean_b, kernel),
+        [kind(24, 32, C, dtype=jnp.bfloat16)],
+        [pltpu.VMEM((ROWS, COLS, C), jnp.float32)],
+        50_000_000,
+    )
+    lon_b, lon_a, dz_in, advanced, part, total = lax.optimization_barrier(
+        (lon_b, lon_a, dz_in, advanced, part, inner_sum(copies))
     )
     west, east = jnp.where(even, lon_b, lon_a), jnp.where(even, lon_a, lon_b)
 
@@ -360,7 +388,7 @@
     lat = exchange(full(slice(0, 3)), full(slice(ROWS - 3, ROWS)), LAT, group_size(LAT), False)
     sums = hand_out(total)
     (field_grad,) = call(
-        back_kernel, (flags, dz_in, dz_st, lon_b, lon_a, *lat, gmask, ocean_b, kernel), [CELLS], [PADDED], 100_000_000
+        back_kernel, (flags, dz_in, dz_st, lon_b, lon_a, *lat, gmask, ocean_b, kernel, part), [CELLS], [PADDED], 50_000_000
     )
     cells = ROWS * COLS * group_size(LAT) * group_size(LON)
     kernel_grad, w_in_grad, w_out_grad = call(

time: 96.5 us -> 95.9 us (level)
    all_to_all x1, waiting for transfers between devices: 7.56 us -> 6.16 us  [inner_sum(): parts = lax.all_to_all(copies, INNER, 0, 0, tiled=True).astype(jnp.float32)]
    pallas_call x5 -> x6, Pallas kernels: 16.9 us -> 17 us  [call(): pl.pallas_call(body, out_shape=outs, in_specs=[smem if a.dtype == jnp.int...]
  transfers between devices with their start and end apart: 11 -> 11, of which waited for: 3 -> 4; matrix products, arithmetic and copies ran while one was open for 4% -> 4% of each run, Pallas kernels for 12% -> 12%
where the time goes in v10:
time: 95.9 us; the launch traced here: 95.3 us
  starting transfers between devices  62.6 us (65%)
  Pallas kernels  17 us (18%)
  waiting for transfers between devices  8.12 us (8%)
  local copies, waits for them, and re-layouts  3.89 us (4%)
  other arithmetic  2.69 us (3%)
  between operations  0.98 us (1%)
    ppermute x8, starting transfers between devices, swap(): return lax.ppermute(values, axes, pairs)  48.4 us
    pallas_call x6, Pallas kernels, call(): pl.pallas_call(body, out_shape=outs, in_specs=[smem if a.dtype == jnp.int...  17 us
    all_to_all x1, waiting for transfers between devices, inner_sum(): parts = lax.all_to_all(copies, INNER, 0, 0, tiled=True).astype(jnp.float32)  6.16 us
    all_to_all x1, starting transfers between devices, hand_out(): return lax.all_to_all(spread, OUTER, 0, 0, tiled=True)  5.84 us
    all_to_all x1, starting transfers between devices, scatter_sum(): lax.all_to_all(parts, OUTER, 0, 0, tiled=True).astype(jnp.float32)  4.83 us
    all_to_all x1, starting transfers between devices, inner_sum(): parts = lax.all_to_all(copies, INNER, 0, 0, tiled=True).astype(jnp.float32)  3.5 us
  transfers between devices with their start and end apart: 11, of which 4 were waited for; matrix products, arithmetic and copies ran while one was open for 4% of the time, Pallas kernels for 12%

profile of v10, /device:TPU:1, one launch (start us, length us, event | category | flops | bytes accessed | tf_op | source)
XLA Modules:
  0.0 95.3 jit_solution(13075759407545700493)
XLA Ops:
  0.6 0.7 copy-done.3
  1.4 0.9 broadcast_select_fusion.6
  2.3 4.6 %collective-permute-start = (bf16[3,48,128]{2,1,0:T(8,128)(2,1)S(1)}, bf16[3,48,128]{2,1,0:T(8,128)(2,1)S(1)}, u32[]{:S(2)}, u32[]{:S(2)}) collective-permute-start(bf16[3,48,128]{2,1,0:T(8,128)(2,1)S(1)} %get-tuple-element.40), channel_id=1, source_target_pairs={{1,2},{3,4},{5,6},{2,1},{4,3},{6,5},{9,10},{11,12},{13,14},{10,9},... | collective-permute-start | bytes 110600 | tf_op jit(solution)/shard_map/ppermute | solution.py:285
  6.9 8.5 %collective-permute-start.1 = (bf16[3,48,128]{2,1,0:T(8,128)(2,1)S(1)}, bf16[3,48,128]{2,1,0:T(8,128)(2,1)S(1)}, u32[]{:S(2)}, u32[]{:S(2)}) collective-permute-start(bf16[3,48,128]{2,1,0:T(8,128)(2,1)S(1)} %get-tuple-element.39), channel_id=1, source_target_pairs={{0,1},{2,3},{4,5},{6,7},{1,0},{3,2},{5,4},{7,6},{8,9},{10,11},{12,... | collective-permute-start | bytes 110600 | tf_op jit(solution)/shard_map/ppermute | solution.py:285
  15.4 1.4 %broadcast_multiply_fusion = (bf16[32,48,128]{2,1,0:T(8,128)(2,1)S(1)}, bf16[32,48,128]{2,1,0:T(8,128)(2,1)S(1)}) fusion(bf16[32,48,128]{2,1,0:T(8,128)(2,1)} %param.10, bf16[32,48]{1,0:T(8,128)(2,1)S(1)} %convert_element_type.2, bf16[32,48,128]{2,1,0:T(8,128)(2,1)} %param.8), kind=kLoop, calls=%fused_computation | loop fusion | flops 393216 | bytes 1575936 | tf_op jit(solution)/shard_map/mul | solution.py:338
  16.8 0.7 copy-done.4
  17.5 0.1 pad_add_fusion.flags
  17.7 14.3 %collective-permute-start.2 = (bf16[38,3,128]{2,1,0:T(4,128)(2,1)S(1)}, bf16[38,3,128]{2,1,0:T(4,128)(2,1)S(1)}, u32[]{:S(2)}, u32[]{:S(2)}) collective-permute-start(bf16[38,3,128]{2,1,0:T(4,128)(2,1)S(1)} %get-tuple-element.54), channel_id=1, source_target_pairs={{8,16},{24,32},{40,48},{56,64},{72,80},{88,96},{104,112},{120,128}... | collective-permute-start | bytes 87560 | tf_op jit(solution)/shard_map/ppermute | solution.py:285
  32.0 1.9 %collective-permute-start.3 = (bf16[38,3,128]{2,1,0:T(4,128)(2,1)S(1)}, bf16[38,3,128]{2,1,0:T(4,128)(2,1)S(1)}, u32[]{:S(2)}, u32[]{:S(2)}) collective-permute-start(bf16[38,3,128]{2,1,0:T(4,128)(2,1)S(1)} %get-tuple-element.53), channel_id=1, source_target_pairs={{0,8},{16,24},{32,40},{48,56},{64,72},{80,88},{96,104},{112,120},{... | collective-permute-start | bytes 87560 | tf_op jit(solution)/shard_map/ppermute | solution.py:285
  34.0 5.7 %shard_map.119 = (bf16[1024,256]{1,0:T(8,128)(2,1)S(1)}, bf16[32,32,128]{2,1,0:T(8,128)(2,1)S(1)}, f32[128,256]{1,0:T(8,128)S(1)}, f32[128,256]{1,0:T(8,128)S(1)}, f32[49,8,128]{2,1,0:T(8,128)S(1)}) custom-call(s32[2]{0:T(128)S(1)} %pad_add_fusion.flags, bf16[32,48,128]{2,1,0:T(8,128)(2,1)S(1)} %get-tuple-element.68.masked, ...), custom_call_target="tpu_custom_call" | custom-call | flops 350000000 | bytes 2097152 | tf_op jit(solution)/shard_map/pallas_call | solution.py:253
  39.8 4.7 %shard_map.120 = (bf16[512,256]{1,0:T(8,128)(2,1)S(1)}, bf16[32,16,128]{2,1,0:T(8,128)(2,1)S(1)}, bf16[64,3,3,128]{3,2,1,0:T(4,128)(2,1)}) custom-call(s32[2]{0:T(128)S(1)} %pad_add_fusion.flags, bf16[32,48,128]{2,1,0:T(8,128)(2,1)S(1)} %get-tuple-element.68.masked, bf16[3,48,128]{2,1,0:T(8,128)(2,1)S(1)} %collective-permute-done.lat_b, ...), custom_call_target="tpu_custom_call" | custom-call | flops 170000000 | bytes 2097152 | tf_op jit(solution)/shard_map/pallas_call | solution.py:253
  44.5 4.8 %all-to-all-start = ((bf16[64,3,3,128]{3,2,1,0:T(4,128)(2,1)}), bf16[64,3,3,128]{3,2,1,0:T(4,128)(2,1)S(1)}, u32[]{:S(2)}, u32[]{:S(2)}) async-start(bf16[64,3,3,128]{3,2,1,0:T(4,128)(2,1)} %get-tuple-element.29), calls=%async_computation | async-start | bytes 393216 | tf_op jit(solution)/shard_map/all_to_all | solution.py:309
  49.4 11.7 %collective-permute-start.4 = (bf16[32,3,128]{2,1,0:T(4,128)(2,1)S(1)}, bf16[32,3,128]{2,1,0:T(4,128)(2,1)S(1)}, u32[]{:S(2)}, u32[]{:S(2)}) collective-permute-start(bf16[32,3,128]{2,1,0:T(4,128)(2,1)S(1)} %get-tuple-element.50), channel_id=1, source_target_pairs={{8,16},{24,32},{40,48},{56,64},{72,80},{88,96},{104,112},{120,128}... | collective-permute-start | bytes 73736 | tf_op jit(solution)/shard_map/ppermute | solution.py:285
  61.1 1.9 %collective-permute-start.5 = (bf16[32,3,128]{2,1,0:T(4,128)(2,1)S(1)}, bf16[32,3,128]{2,1,0:T(4,128)(2,1)S(1)}, u32[]{:S(2)}, u32[]{:S(2)}) collective-permute-start(bf16[32,3,128]{2,1,0:T(4,128)(2,1)S(1)} %get-tuple-element.49), channel_id=1, source_target_pairs={{0,8},{16,24},{32,40},{48,56},{64,72},{80,88},{96,104},{112,120},{... | collective-permute-start | bytes 73736 | tf_op jit(solution)/shard_map/ppermute | solution.py:285
  63.0 0.1 reduce_sum.24
  63.1 0.6 broadcast_in_dim.7
  63.8 3.5 %all-to-all-start.1 = ((bf16[12,3,3,128]{3,2,1,0:T(4,128)(2,1)}), bf16[12,3,3,128]{3,2,1,0:T(4,128)(2,1)S(1)}, u32[]{:S(2)}, u32[]{:S(2)}) async-start(bf16[12,3,3,128]{3,2,1,0:T(4,128)(2,1)} %broadcast_in_dim.7), calls=%async_computation.1 | async-start | bytes 73728 | tf_op jit(solution)/shard_map/all_to_all | solution.py:317
  67.3 0.3 broadcast_in_dim.6.ocean
  67.6 1.4 %shard_map.122.part = bf16[24,32,128]{2,1,0:T(8,128)(2,1)S(1)} custom-call(bf16[32,32,128]{2,1,0:T(8,128)(2,1)S(1)} %get-tuple-element.31.dz_in, bf16[32,16,128]{2,1,0:T(8,128)(2,1)S(1)} %get-tuple-element.25.dz_st, bf16[32,48,128]{2,1,0:T(8,128)(2,1)S(1)} %get-tuple-element.67.gmask, bf16[32,48,128]{2,1,0:T(8,128)(2,1)S(1)} %broadcast_in_dim.6.ocean, ...), custom_call_target="tpu_custom_call" | custom-call | flops 50000000 | bytes 2097152 | tf_op jit(solution)/shard_map/pallas_call | solution.py:253
  69.0 1.5 %shard_map.121 = bf16[32,48,128]{2,1,0:T(8,128)(2,1)} custom-call(bf16[1024,256]{1,0:T(8,128)(2,1)S(1)} %get-tuple-element.27.hidden_in, bf16[512,256]{1,0:T(8,128)(2,1)S(1)} %get-tuple-element.28.hidden_st, bf16[32,48,128]{2,1,0:T(8,128)(2,1)S(1)} %get-tuple-element.68.masked, bf16[32,48,128]{2,1,0:T(8,128)(2,1)S(1)} %broadcast_in_dim.6.ocean, ...), custom_call_target="tpu_custom_call" | custom-call | flops 100000000 | bytes 2097152 | tf_op jit(solution)/shard_map/pallas_call | solution.py:253
  70.5 6.2 %all-to-all-done.1 = bf16[12,3,3,128]{3,2,1,0:T(4,128)(2,1)S(1)} async-done(((bf16[12,3,3,128]{3,2,1,0:T(4,128)(2,1)}), bf16[12,3,3,128]{3,2,1,0:T(4,128)(2,1)S(1)}, u32[]{:S(2)}, u32[]{:S(2)}) %all-to-all-start.1) | async-done | bytes 27680 | tf_op jit(solution)/shard_map/all_to_all | solution.py:317
  76.8 0.7 broadcast_in_dim.8
  77.5 5.8 %all-to-all-start.2 = ((bf16[64,3,3,128]{3,2,1,0:T(4,128)(2,1)}), bf16[64,3,3,128]{3,2,1,0:T(4,128)(2,1)S(1)}, u32[]{:S(2)}, u32[]{:S(2)}) async-start(bf16[64,3,3,128]{3,2,1,0:T(4,128)(2,1)} %broadcast_in_dim.8), calls=%async_computation.2 | async-start | bytes 393216 | tf_op jit(solution)/shard_map/all_to_all | solution.py:323
  83.4 0.4 concatenate.19
  83.8 0.4 concatenate.18
  84.2 3.5 %collective-permute-start.6 = (bf16[3,54,128]{2,1,0:T(8,128)(2,1)S(1)}, bf16[3,54,128]{2,1,0:T(8,128)(2,1)S(1)}, u32[]{:S(2)}, u32[]{:S(2)}) collective-permute-start(bf16[3,54,128]{2,1,0:T(8,128)(2,1)S(1)} %get-tuple-element.52), channel_id=1, source_target_pairs={{1,2},{3,4},{5,6},{2,1},{4,3},{6,5},{9,10},{11,12},{13,14},{10,9},... | collective-permute-start | bytes 124424 | tf_op jit(solution)/shard_map/ppermute | solution.py:285
  87.8 1.9 %collective-permute-start.7 = (bf16[3,54,128]{2,1,0:T(8,128)(2,1)S(1)}, bf16[3,54,128]{2,1,0:T(8,128)(2,1)S(1)}, u32[]{:S(2)}, u32[]{:S(2)}) collective-permute-start(bf16[3,54,128]{2,1,0:T(8,128)(2,1)S(1)} %get-tuple-element.51), channel_id=1, source_target_pairs={{0,1},{2,3},{4,5},{6,7},{1,0},{3,2},{5,4},{7,6},{8,9},{10,11},{12,... | collective-permute-start | bytes 124424 | tf_op jit(solution)/shard_map/ppermute | solution.py:285
  89.7 0.8 collective-permute-done.6.lat_b
  90.5 0.4 collective-permute-done.7.lat_a
  90.9 2.8 %shard_map.123 = bf16[32,48,128]{2,1,0:T(8,128)(2,1)} custom-call(s32[2]{0:T(128)S(1)} %pad_add_fusion.flags, bf16[32,32,128]{2,1,0:T(8,128)(2,1)S(1)} %get-tuple-element.31.dz_in, bf16[32,16,128]{2,1,0:T(8,128)(2,1)S(1)} %get-tuple-element.25.dz_st, bf16[32,3,128]{2,1,0:T(4,128)(2,1)S(1)} %collective-permute-done.4.lon_b, ...), custom_call_target="tpu_custom_call" | custom-call | flops 50000000 | bytes 2097152 | tf_op jit(solution)/shard_map/pallas_call | solution.py:253
  93.7 0.7 all-to-all-done.2.parts
  94.4 0.8 shard_map.124
  (32 shorter events, 0.3 us)
Async XLA Ops:
  0.6 0.7 copy-start.3
  2.3 15.3 %collective-permute-start = (bf16[3,48,128]{2,1,0:T(8,128)(2,1)S(1)}, bf16[3,48,128]{2,1,0:T(8,128)(2,1)S(1)}, u32[]{:S(2)}, u32[]{:S(2)}) collective-permute-start(bf16[3,48,128]{2,1,0:T(8,128)(2,1)S(1)} %get-tuple-element.40), channel_id=1, source_target_pairs={{1,2},{3,4},{5,6},{2,1},{4,3},{6,5},{9,10},{11,12},{13,14},{10,9},... | collective-permute-start | bytes 110600 | tf_op jit(solution)/shard_map/ppermute | solution.py:285
  6.9 10.7 %collective-permute-start.1 = (bf16[3,48,128]{2,1,0:T(8,128)(2,1)S(1)}, bf16[3,48,128]{2,1,0:T(8,128)(2,1)S(1)}, u32[]{:S(2)}, u32[]{:S(2)}) collective-permute-start(bf16[3,48,128]{2,1,0:T(8,128)(2,1)S(1)} %get-tuple-element.39), channel_id=1, source_target_pairs={{0,1},{2,3},{4,5},{6,7},{1,0},{3,2},{5,4},{7,6},{8,9},{10,11},{12,... | collective-permute-start | bytes 110600 | tf_op jit(solution)/shard_map/ppermute | solution.py:285
  16.8 0.7 copy-start.4
  16.8 0.7 copy-start.5
  17.6 16.3 %copy-start = (bf16[256,128]{1,0:T(8,128)(2,1)S(1)}, bf16[256,128]{1,0:T(8,128)(2,1)}, u32[]{:S(2)}) copy-start(bf16[256,128]{1,0:T(8,128)(2,1)} %w_out.5) | copy-start | bytes 196612
  17.6 16.3 %copy-start.1 = (f32[7,7,128]{2,1,0:T(8,128)S(1)}, f32[7,7,128]{2,1,0:T(8,128)}, u32[]{:S(2)}) copy-start(f32[7,7,128]{2,1,0:T(8,128)} %taps.7) | copy-start | bytes 75268
  17.7 16.3 %copy-start.2 = (bf16[128,256]{1,0:T(8,128)(2,1)S(1)}, bf16[128,256]{1,0:T(8,128)(2,1)}, u32[]{:S(2)}) copy-start(bf16[128,256]{1,0:T(8,128)(2,1)} %w_in.3) | copy-start | bytes 196612
  17.7 22.0 %collective-permute-start.2 = (bf16[38,3,128]{2,1,0:T(4,128)(2,1)S(1)}, bf16[38,3,128]{2,1,0:T(4,128)(2,1)S(1)}, u32[]{:S(2)}, u32[]{:S(2)}) collective-permute-start(bf16[38,3,128]{2,1,0:T(4,128)(2,1)S(1)} %get-tuple-element.54), channel_id=1, source_target_pairs={{8,16},{24,32},{40,48},{56,64},{72,80},{88,96},{104,112},{120,128}... | collective-permute-start | bytes 87560 | tf_op jit(solution)/shard_map/ppermute | solution.py:285
  32.0 7.7 %collective-permute-start.3 = (bf16[38,3,128]{2,1,0:T(4,128)(2,1)S(1)}, bf16[38,3,128]{2,1,0:T(4,128)(2,1)S(1)}, u32[]{:S(2)}, u32[]{:S(2)}) collective-permute-start(bf16[38,3,128]{2,1,0:T(4,128)(2,1)S(1)} %get-tuple-element.53), channel_id=1, source_target_pairs={{0,8},{16,24},{32,40},{48,56},{64,72},{80,88},{96,104},{112,120},{... | collective-permute-start | bytes 87560 | tf_op jit(solution)/shard_map/ppermute | solution.py:285
  44.5 18.5 %all-to-all-start = ((bf16[64,3,3,128]{3,2,1,0:T(4,128)(2,1)}), bf16[64,3,3,128]{3,2,1,0:T(4,128)(2,1)S(1)}, u32[]{:S(2)}, u32[]{:S(2)}) async-start(bf16[64,3,3,128]{3,2,1,0:T(4,128)(2,1)} %get-tuple-element.29), calls=%async_computation | async-start | bytes 393216 | tf_op jit(solution)/shard_map/all_to_all | solution.py:309
  49.4 27.3 %collective-permute-start.4 = (bf16[32,3,128]{2,1,0:T(4,128)(2,1)S(1)}, bf16[32,3,128]{2,1,0:T(4,128)(2,1)S(1)}, u32[]{:S(2)}, u32[]{:S(2)}) collective-permute-start(bf16[32,3,128]{2,1,0:T(4,128)(2,1)S(1)} %get-tuple-element.50), channel_id=1, source_target_pairs={{8,16},{24,32},{40,48},{56,64},{72,80},{88,96},{104,112},{120,128}... | collective-permute-start | bytes 73736 | tf_op jit(solution)/shard_map/ppermute | solution.py:285
  61.1 15.6 %collective-permute-start.5 = (bf16[32,3,128]{2,1,0:T(4,128)(2,1)S(1)}, bf16[32,3,128]{2,1,0:T(4,128)(2,1)S(1)}, u32[]{:S(2)}, u32[]{:S(2)}) collective-permute-start(bf16[32,3,128]{2,1,0:T(4,128)(2,1)S(1)} %get-tuple-element.49), channel_id=1, source_target_pairs={{0,8},{16,24},{32,40},{48,56},{64,72},{80,88},{96,104},{112,120},{... | collective-permute-start | bytes 73736 | tf_op jit(solution)/shard_map/ppermute | solution.py:285
  63.8 12.9 %all-to-all-start.1 = ((bf16[12,3,3,128]{3,2,1,0:T(4,128)(2,1)}), bf16[12,3,3,128]{3,2,1,0:T(4,128)(2,1)S(1)}, u32[]{:S(2)}, u32[]{:S(2)}) async-start(bf16[12,3,3,128]{3,2,1,0:T(4,128)(2,1)} %broadcast_in_dim.7), calls=%async_computation.1 | async-start | bytes 73728 | tf_op jit(solution)/shard_map/all_to_all | solution.py:317
  77.5 16.9 %all-to-all-start.2 = ((bf16[64,3,3,128]{3,2,1,0:T(4,128)(2,1)}), bf16[64,3,3,128]{3,2,1,0:T(4,128)(2,1)S(1)}, u32[]{:S(2)}, u32[]{:S(2)}) async-start(bf16[64,3,3,128]{3,2,1,0:T(4,128)(2,1)} %broadcast_in_dim.8), calls=%async_computation.2 | async-start | bytes 393216 | tf_op jit(solution)/shard_map/all_to_all | solution.py:323
  84.2 6.3 %collective-permute-start.6 = (bf16[3,54,128]{2,1,0:T(8,128)(2,1)S(1)}, bf16[3,54,128]{2,1,0:T(8,128)(2,1)S(1)}, u32[]{:S(2)}, u32[]{:S(2)}) collective-permute-start(bf16[3,54,128]{2,1,0:T(8,128)(2,1)S(1)} %get-tuple-element.52), channel_id=1, source_target_pairs={{1,2},{3,4},{5,6},{2,1},{4,3},{6,5},{9,10},{11,12},{13,14},{10,9},... | collective-permute-start | bytes 124424 | tf_op jit(solution)/shard_map/ppermute | solution.py:285
  87.8 3.1 %collective-permute-start.7 = (bf16[3,54,128]{2,1,0:T(8,128)(2,1)S(1)}, bf16[3,54,128]{2,1,0:T(8,128)(2,1)S(1)}, u32[]{:S(2)}, u32[]{:S(2)}) collective-permute-start(bf16[3,54,128]{2,1,0:T(8,128)(2,1)S(1)} %get-tuple-element.51), channel_id=1, source_target_pairs={{0,1},{2,3},{4,5},{6,7},{1,0},{3,2},{5,4},{7,6},{8,9},{10,11},{12,... | collective-permute-start | bytes 124424 | tf_op jit(solution)/shard_map/ppermute | solution.py:285
